TPU v7x, 32 devices: a whole 2x2x4 slice. The times are simulated.
32 devices in a mesh: mem: 4 (over x, core), tile: 8 (over z, y).
Axes of the slice: x: 2, y: 2, z: 4, core: 2. Of those that a mesh axis runs over, the one named last changes fastest.
Arguments:
- perturbations: bfloat16 [8, 32, 2, 64, 3072], P('mem', None, None, 'tile'), may hold values from -6 to 6
- gradient: bfloat16 [32, 2, 64, 3072], P('mem', None, 'tile'), may hold values from -6 to 6
- static_variance: float32 [32, 2, 64, 3072], P('mem', None, 'tile'), may hold values from 0.05 to 0.5
- level_steps: int32 [32], replicated, may hold values from 1 to 10, as said below
- class_map: int32 [64, 3072], replicated, may hold values from 0 to 3
- class_diffusivity: float32 [4], replicated, may hold values from 0.05 to 0.35
Outputs:
- increment: float32 [32, 2, 64, 3072], P('mem', None, 'tile')
Inputs may be any that keep to these rules, and one draw needn't show every extreme that they name: `level_steps`: each level's number of diffusion steps; some level takes exactly 10.
All inputs are finite; a program needn't handle non-finite values.
Results may differ from a plain program's by a relative error of at most 0.0021.
Values may be sent and summed in bfloat16 or wider, within the bound.
No kernel may reach another device: no remote copies, remote signals or barrier semaphores. Data moves between devices by JAX's collectives and lax.ppermute only.
A program may use at most 128 MiB of HBM per device.

v0:
```python
import jax
import jax.numpy as jnp
from jax import lax
from jax.sharding import PartitionSpec as P


def diffusivity_field(class_map, class_diffusivity):
    classes = jnp.arange(class_diffusivity.shape[0], dtype=jnp.int32)
    match = (class_map[None, :, :] == classes[:, None, None]).astype(jnp.float32)
    return jnp.sum(match * class_diffusivity[:, None, None], axis=0)


def diffusion_step(field, diffusivity):
    zero_row = jnp.zeros_like(field[:1])
    northern = jnp.concatenate([zero_row, field[:-1]], axis=0)
    southern = jnp.concatenate([field[1:], zero_row], axis=0)
    eastern = jnp.roll(field, -1, axis=1)
    western = jnp.roll(field, 1, axis=1)
    corners = jnp.roll(northern, -1, axis=1) + jnp.roll(northern, 1, axis=1)
    corners = corners + jnp.roll(southern, -1, axis=1) + jnp.roll(southern, 1, axis=1)
    laplace = (4.0 * (northern + southern + eastern + western) + corners - 20.0 * field) / 6.0
    return field + diffusivity * laplace


def diffuse(field, steps, diffusivity):
    return lax.fori_loop(
        jnp.int32(0), steps, lambda step_index, state: diffusion_step(state, diffusivity), field
    )


def shards(perturbations, gradient, static_variance, level_steps, class_map, class_diffusivity):
    members, levels, variables, lat_rows, lon_cells = perturbations.shape
    tile_count = lax.axis_size("tile")
    full_grad = lax.all_gather(gradient, "mem", axis=0, tiled=True)
    product = jnp.sum(
        perturbations.astype(jnp.float32) * full_grad.astype(jnp.float32)[None], axis=2
    ).astype(jnp.bfloat16)
    plane_total = members * levels
    per_dev = plane_total // tile_count
    planes = product.reshape(plane_total, lat_rows, lon_cells)
    plane_ids = jnp.arange(plane_total, dtype=jnp.int32)
    level_of = plane_ids % levels
    level_ids = jnp.arange(levels, dtype=jnp.int32)
    plane_steps = jnp.sum(
        jnp.where(level_of[:, None] == level_ids[None, :], level_steps[None, :], 0), axis=1
    )
    ranked = jnp.argsort(-plane_steps, stable=True)
    owner_index = plane_ids // per_dev
    sweep_index = plane_ids % per_dev
    position = jnp.where(sweep_index % 2 == 0, owner_index, tile_count - 1 - owner_index)
    source = ranked[sweep_index * tile_count + position]
    planes = planes[source]
    arrived = lax.all_to_all(planes, "tile", split_axis=0, concat_axis=1, tiled=True)
    device_index = lax.axis_index("tile")
    local_ids = lax.dynamic_slice_in_dim(source, device_index * per_dev, per_dev)
    local_steps = jnp.sum(
        jnp.where(local_ids[:, None] == plane_ids[None, :], plane_steps[None, :], 0), axis=1
    )
    diffusivity = diffusivity_field(class_map, class_diffusivity)

    def smooth_one(packed):
        return diffuse(packed[0].astype(jnp.float32), packed[1], diffusivity).astype(jnp.bfloat16)

    smooth = lax.map(smooth_one, (arrived, local_steps))
    returned = lax.all_to_all(smooth, "tile", split_axis=1, concat_axis=0, tiled=True)
    returned = returned[jnp.argsort(source)]
    smooth_tiles = returned.reshape(members, levels, lat_rows, lon_cells)
    partial_value = jnp.sum(
        perturbations.astype(jnp.float32) * smooth_tiles.astype(jnp.float32)[:, :, None], axis=0
    )
    reduced = lax.psum_scatter(partial_value, "mem", scatter_dimension=0, tiled=True)
    return static_variance * gradient.astype(jnp.float32) + reduced


def solution(mesh):
    placed = (
        P("mem", None, None, "tile", None),
        P("mem", None, "tile", None),
        P("mem", None, "tile", None),
        P(),
        P(),
        P(),
    )
    return jax.shard_map(
        shards, mesh=mesh, in_specs=placed, out_specs=P("mem", None, "tile", None), check_vma=False
    )
```

profile of v0, /device:TPU:0, one launch (start us, length us, event | category | flops | bytes accessed | tf_op | source)
XLA Modules:
  0.0 385.2 jit_solution(16818328238675514954)
XLA Ops:
  8.0 2.0 sort.34
  10.9 29.3 %all-gather.2.cloned.1.call-done = bf16[32,2,8,3072]{3,2,1,0:T(8,128)(2,1)} async-done(((bf16[8,2,8,3072]{3,2,1,0:T(8,128)(2,1)}), bf16[32,2,8,3072]{3,2,1,0:T(8,128)(2,1)}) %all-gather.2.cloned.1.call-update) | async-done | bytes 3145744 | tf_op jit(solution)/shard_map/all_gather | solution.py:34
  40.2 5.4 %convert_element_type.39 = f32[32,2,8,3072]{3,2,1,0:T(8,128)} convert(bf16[32,2,8,3072]{3,2,1,0:T(8,128)(2,1)} %all-gather.2.cloned.1.call-done) | non-fusion elementwise | flops 1572864 | bytes 9437184 | tf_op jit(solution)/shard_map/convert_element_type | solution.py:36
  45.5 6.6 %fusion.9 = bf16[2,32,8,3072]{3,2,1,0:T(8,128)(2,1)S(1)} fusion(bf16[2,32,2,8,3072]{4,3,2,1,0:T(8,128)(2,1)} %param.10, f32[32,2,8,3072]{3,2,1,0:T(8,128)} %convert_element_type.39), kind=kLoop, calls=%fused_computation.26 | loop fusion | flops 7864320 | bytes 15728640 | tf_op jit(solution)/shard_map/reduce_sum | solution.py:35
  52.1 2.4 gather_fusion.1
  54.6 5.6 %all-to-all-start = ((bf16[64,8,3072]{2,1,0:T(8,128)(2,1)}), bf16[64,8,3072]{2,1,0:T(8,128)(2,1)}, u32[]{:S(2)}, u32[]{:S(2)}) async-start(bf16[64,8,3072]{2,1,0:T(8,128)(2,1)} %gather_fusion.1), calls=%async_computation | async-start | bytes 6291456 | tf_op jit(solution)/shard_map/all_to_all | solution.py:53
  60.9 70.5 %all-to-all-done = bf16[64,8,3072]{2,1,0:T(8,128)(2,1)} async-done(((bf16[64,8,3072]{2,1,0:T(8,128)(2,1)}), bf16[64,8,3072]{2,1,0:T(8,128)(2,1)}, u32[]{:S(2)}, u32[]{:S(2)}) %all-to-all-start) | async-done | bytes 3145760 | tf_op jit(solution)/shard_map/all_to_all | solution.py:53
  131.4 3.8 copy.19
  135.2 84.3 %while.21 = (s32[]{:T(128)}, bf16[8,64,3072]{2,1,0:T(8,128)(2,1)}, bf16[8,64,3072]{2,1,0:T(8,128)(2,1)}, s32[8]{0:T(128)S(1)}, f32[64,3072]{1,0:T(8,128)S(1)}, /*index=5*/s32[]{:T(128)}, s32[]{:T(128)}, s32[]{:T(128)}) while((s32[]{:T(128)}, bf16[8,64,3072]{2,1,0:T(8,128)(2,1)}, bf16[8,64,3072]{2,1,0:T(8,128)(2,1)}, s32[8]{0:T(128)S(1)}, ...), condition=%wide.region_8.9_spmd, body=%wide.region_5.8_spmd.sunk | while | flops 4128772 | bytes 23470800 | solution.py:64
  135.2 1.0 bitcast_convert_fusion.3
  136.9 26.7 %while.22 = (s32[]{:T(128)}, f32[64,3072]{1,0:T(8,128)S(1)}, s32[]{:T(128)}, f32[64,3072]{1,0:T(8,128)S(1)}, s32[]{:T(128)}) while((s32[]{:T(128)}, f32[64,3072]{1,0:T(8,128)S(1)}, s32[]{:T(128)}, f32[64,3072]{1,0:T(8,128)S(1)}, s32[]{:T(128)}) %tuple.55), condition=%wide.region_7.7_spmd, body=%wide.region_6.6_spmd.sunk | while | flops 3735554 | bytes 21110844 | solution.py:26
  164.4 1.0 bitcast_convert_fusion.3
  166.0 8.4 %while.22 = (s32[]{:T(128)}, f32[64,3072]{1,0:T(8,128)S(1)}, s32[]{:T(128)}, f32[64,3072]{1,0:T(8,128)S(1)}, s32[]{:T(128)}) while((s32[]{:T(128)}, f32[64,3072]{1,0:T(8,128)S(1)}, s32[]{:T(128)}, f32[64,3072]{1,0:T(8,128)S(1)}, s32[]{:T(128)}) %tuple.55), condition=%wide.region_7.7_spmd, body=%wide.region_6.6_spmd.sunk | while | flops 3735554 | bytes 21110844 | solution.py:26
  175.2 1.0 bitcast_convert_fusion.3
  176.9 8.4 %while.22 = (s32[]{:T(128)}, f32[64,3072]{1,0:T(8,128)S(1)}, s32[]{:T(128)}, f32[64,3072]{1,0:T(8,128)S(1)}, s32[]{:T(128)}) while((s32[]{:T(128)}, f32[64,3072]{1,0:T(8,128)S(1)}, s32[]{:T(128)}, f32[64,3072]{1,0:T(8,128)S(1)}, s32[]{:T(128)}) %tuple.55), condition=%wide.region_7.7_spmd, body=%wide.region_6.6_spmd.sunk | while | flops 3735554 | bytes 21110844 | solution.py:26
  186.1 1.0 bitcast_convert_fusion.3
  187.7 5.8 %while.22 = (s32[]{:T(128)}, f32[64,3072]{1,0:T(8,128)S(1)}, s32[]{:T(128)}, f32[64,3072]{1,0:T(8,128)S(1)}, s32[]{:T(128)}) while((s32[]{:T(128)}, f32[64,3072]{1,0:T(8,128)S(1)}, s32[]{:T(128)}, f32[64,3072]{1,0:T(8,128)S(1)}, s32[]{:T(128)}) %tuple.55), condition=%wide.region_7.7_spmd, body=%wide.region_6.6_spmd.sunk | while | flops 3735554 | bytes 21110844 | solution.py:26
  194.4 1.0 bitcast_convert_fusion.3
  196.0 5.8 %while.22 = (s32[]{:T(128)}, f32[64,3072]{1,0:T(8,128)S(1)}, s32[]{:T(128)}, f32[64,3072]{1,0:T(8,128)S(1)}, s32[]{:T(128)}) while((s32[]{:T(128)}, f32[64,3072]{1,0:T(8,128)S(1)}, s32[]{:T(128)}, f32[64,3072]{1,0:T(8,128)S(1)}, s32[]{:T(128)}) %tuple.55), condition=%wide.region_7.7_spmd, body=%wide.region_6.6_spmd.sunk | while | flops 3735554 | bytes 21110844 | solution.py:26
  204.3 3.2 while.22
  209.9 3.2 while.22
  215.6 3.2 while.22
  219.6 5.3 %copy.14 = bf16[8,64,3072]{2,0,1:T(8,128)(2,1)} copy(bf16[8,64,3072]{2,1,0:T(8,128)(2,1)} %get-tuple-element.58) | data formatting | bytes 6291456 | tf_op jit(solution)/shard_map/while | solution.py:64
  224.8 3.8 all-to-all-start.1
  228.9 2.0 sort.35
  230.9 67.9 %all-to-all-done.1 = bf16[8,64,3072]{2,0,1:T(8,128)(2,1)S(1)} async-done(((bf16[8,64,3072]{2,0,1:T(8,128)(2,1)}), bf16[8,64,3072]{2,0,1:T(8,128)(2,1)S(1)}, u32[]{:S(2)}, u32[]{:S(2)}) %all-to-all-start.1) | async-done | bytes 3145760 | tf_op jit(solution)/shard_map/all_to_all | solution.py:65
  298.8 3.4 copy.16
  302.3 2.6 gather_fusion.2
  304.9 3.5 bitcast_convert_fusion.1
  308.4 10.1 %fusion.10 = f32[32,2,8,3072]{3,2,1,0:T(8,128)} fusion(bf16[2,32,2,8,3072]{4,3,2,1,0:T(8,128)(2,1)} %param.10, f32[2,32,8,3072]{3,2,1,0:T(8,128)} %bitcast_convert_fusion.1), kind=kLoop, calls=%fused_computation.27 | loop fusion | flops 7864320 | bytes 18874368 | tf_op jit(solution)/shard_map/reduce_sum | solution.py:68
  318.5 57.1 %reduce-scatter.2.cloned.1.call-done = f32[8,2,8,3072]{3,2,1,0:T(8,128)} async-done(((f32[32,2,8,3072]{3,2,1,0:T(8,128)}), f32[8,2,8,3072]{3,2,1,0:T(8,128)}) %reduce-scatter.2.cloned.1.call-update) | async-done | bytes 1572880 | tf_op jit(solution)/shard_map/reduce_scatter | solution.py:71
  375.6 2.8 multiply_add_fusion
  (189 shorter events, 63.5 us)
Async XLA Ops:
  6.5 33.6 %all-gather.2.cloned.1.call-start = ((), (), s32[]{:S(2)}) async-start(), calls=%async_computation.3 | async-start | bytes 3932160 | tf_op jit(solution)/shard_map/all_gather | solution.py:34
  10.9 49.3 %copy-start.4 = (s32[64]{0:T(128)}, s32[64]{0:T(128)S(1)}, u32[]{:S(2)}) copy-start(s32[64]{0:T(128)S(1)} %gather_fusion) | copy-start | bytes 772
  54.5 5.9 %copy-start.2 = (s32[64,3072]{1,0:T(8,128)S(1)}, s32[64,3072]{1,0:T(8,128)}, u32[]{:S(2)}) copy-start(s32[64,3072]{1,0:T(8,128)} %param.14) | copy-start | bytes 2359300
  54.5 5.9 %copy-start.3 = (f32[4]{0:T(128)S(1)}, f32[4]{0:T(128)}, u32[]{:S(2)}) copy-start(f32[4]{0:T(128)} %param.15) | copy-start | bytes 52
  54.6 76.9 %all-to-all-start = ((bf16[64,8,3072]{2,1,0:T(8,128)(2,1)}), bf16[64,8,3072]{2,1,0:T(8,128)(2,1)}, u32[]{:S(2)}, u32[]{:S(2)}) async-start(bf16[64,8,3072]{2,1,0:T(8,128)(2,1)} %gather_fusion.1), calls=%async_computation | async-start | bytes 6291456 | tf_op jit(solution)/shard_map/all_to_all | solution.py:53
  224.8 4.0 %copy-start.5 = (s32[64]{0:T(128)S(1)}, s32[64]{0:T(128)}, u32[]{:S(2)}) copy-start(s32[64]{0:T(128)} %copy-done.4) | copy-start | bytes 772
  224.8 74.0 %all-to-all-start.1 = ((bf16[8,64,3072]{2,0,1:T(8,128)(2,1)}), bf16[8,64,3072]{2,0,1:T(8,128)(2,1)S(1)}, u32[]{:S(2)}, u32[]{:S(2)}) async-start(bf16[8,64,3072]{2,0,1:T(8,128)(2,1)} %copy.14), calls=%async_computation.1 | async-start | bytes 6291456 | tf_op jit(solution)/shard_map/all_to_all | solution.py:65
  228.6 146.9 %reduce-scatter.2.cloned.1.call-start = ((), (), s32[]{:S(2)}) async-start(), calls=%async_computation.4 | async-start | bytes 7864320 | tf_op jit(solution)/shard_map/reduce_scatter | solution.py:71
  318.4 57.1 %copy-start = (bf16[8,2,8,3072]{3,2,1,0:T(8,128)(2,1)S(1)}, bf16[8,2,8,3072]{3,2,1,0:T(8,128)(2,1)}, u32[]{:S(2)}) copy-start(bf16[8,2,8,3072]{3,2,1,0:T(8,128)(2,1)} %param.11) | copy-start | bytes 2359300
  318.4 57.1 %copy-start.1 = (f32[8,2,8,3072]{3,2,1,0:T(8,128)S(1)}, f32[8,2,8,3072]{3,2,1,0:T(8,128)}, u32[]{:S(2)}) copy-start(f32[8,2,8,3072]{3,2,1,0:T(8,128)} %param.12) | copy-start | bytes 4718596
Sparse Core Ops, SparseCore 0:
  8.9 31.2 all-gather.1
  318.6 56.9 reduce-scatter.1
where the time goes:
time: 386 us; the launch traced here: 385 us
  waiting for transfers between devices  226 us (59%)
  other arithmetic  69 us (18%)
  local copies, waits for them, and re-layouts  48.7 us (13%)
  loops' own time  18.8 us (5%)
  between operations  13.5 us (3%)
  starting transfers between devices  9.65 us (2%)
    all_to_all x1, waiting for transfers between devices, shards(): lax.all_to_all(planes, 'tile', split_axis=0, concat_axis=1, tiled=True)  70.5 us
    all_to_all x1, waiting for transfers between devices, shards(): lax.all_to_all(smooth, 'tile', split_axis=1, concat_axis=0, tiled=True)  67.9 us
    reduce_scatter x1, waiting for transfers between devices, shards(): lax.psum_scatter(partial_value, 'mem', scatter_dimension=0, tiled=True)  57.1 us
    all_gather x1, waiting for transfers between devices, shards(): full_grad = lax.all_gather(gradient, 'mem', axis=0, tiled=True)  29.3 us
    add x23, other arithmetic, diffusion_step(): return field + diffusivity * laplace  20.5 us
    another operation x8, loops' own time, diffuse(): lax.fori_loop(jnp.int32(0), steps, lambda step_index, state: diffusion_st...  18.7 us
    slice x46, local copies, waits for them, and re-layouts, diffusion_step(): jnp.roll(southern, 1, axis=1)  14.5 us
    reduce_sum x1, other arithmetic, shards(): jnp.sum(perturbations.astype(jnp.float32) * smooth_tiles.astype(jnp.float...  10.1 us
  transfers between devices with their start and end apart: 4, of which 4 were waited for; matrix products, arithmetic and copies ran while one was open for 2% of the time, Pallas kernels for 0%

commit v1 on v0

v1 whole, which is shorter than its diff:
```python
import functools
import jax
import jax.numpy as jnp
from jax import lax
from jax.experimental import pallas as pl
from jax.experimental.pallas import tpu as pltpu
from jax.sharding import PartitionSpec as P

F32 = jnp.float32
BF16 = jnp.bfloat16
I32 = jnp.int32
LANES = 128
ROWS = 8
EDGE = 4
VMEM_BYTES = 60 * 1024 * 1024
SMEM_SPEC = pl.BlockSpec(memory_space=pltpu.SMEM)
VMEM_SPEC = pl.BlockSpec(memory_space=pltpu.VMEM)
ANY_SPEC = pl.BlockSpec(memory_space=pl.ANY)


def cost(flops, size):
    return pl.CostEstimate(flops=int(flops), transcendentals=0, bytes_accessed=int(size))


def span(c):
    return slice(c * LANES, (c + 1) * LANES)


def diffuse_columns(field, keep, mix, index, first, rows, weight_first, emit):
    tiles = field.shape[1]
    lane = lax.broadcasted_iota(I32, (rows, LANES), 1)
    first_lane = lane == 0
    last_lane = lane == LANES - 1

    def load(c):
        here = field[index, c, first:first + rows, :]
        beside = field[index, c, first - 1:first - 1 + rows, :] + field[index, c, first + 1:first + 1 + rows, :]
        line = 4.0 * here + beside
        return here, line, pltpu.roll(line, 1, axis=1), pltpu.roll(line, LANES - 1, axis=1)

    here, line, to_east, to_west = load(0)
    start_west = to_west
    before = load(tiles - 1)[2]
    for c in range(tiles):
        if c + 1 < tiles:
            there = load(c + 1)
            after = there[3]
        else:
            there, after = None, start_west
        west = jnp.where(first_lane, before, to_east)
        east = jnp.where(last_lane, after, to_west)
        across = 4.0 * line + (west + east)
        place = slice(weight_first, weight_first + rows)
        emit(c, keep[c, place, :] * here + mix[c, place, :] * across)
        if there is not None:
            before = to_east
            here, line, to_east, to_west = there


def sweep(field, keep, mix, index, first, rows):
    def store(c, value):
        field[index, c, first:first + rows, :] = value

    diffuse_columns(field, keep, mix, index, first, rows, 0, store)


def diffusivity_of(classes, values, valid=None):
    total = jnp.zeros(classes.shape, F32)
    for k in range(values.shape[0]):
        total = jnp.where(classes == k, values[k], total)
    return total if valid is None else jnp.where(valid, total, 0.0)


def store_weights(keep, mix, c, place, diffusivity):
    keep[c, place, :] = 1.0 - 6.0 * diffusivity
    mix[c, place, :] = diffusivity * (1.0 / 6.0)


def product_of(pert, grad, member, level, c):
    total = None
    for v in range(grad.shape[1]):
        term = pert[member, level, v, :, span(c)].astype(F32) * grad[level, v, :, span(c)].astype(F32)
        total = term if total is None else total + term
    return total.astype(BF16)


def pack_kernel(first, steps, pert, near, far, tops, bottoms, top_rows, bottom_rows, offset):
    members, block = pert.shape[:2]
    capacity = tops.shape[0]
    at = pl.program_id(0)
    half = pl.num_programs(0) // 2

    @pl.when(at == 0)
    def _():
        offset[0] = 0

    def pack(grad):
        for j in range(block):
            count = steps[first[at] + j]
            for m in range(members):
                off = jnp.minimum(offset[0], capacity)
                for c in range(top_rows.shape[0]):
                    part = product_of(pert, grad, m, j, c).astype(F32)
                    top_rows[c, pl.ds(off, ROWS), :] = part
                    bottom_rows[c, pl.ds(capacity - off, ROWS), :] = part
                offset[0] = off + count

    @pl.when(at < half)
    def _():
        pack(near)

    @pl.when(at >= half)
    def _():
        pack(far)

    @pl.when(at == 2 * half - 1)
    def _():
        for c in range(top_rows.shape[0]):
            tops[:, span(c)] = top_rows[c, :capacity, :].astype(BF16)
            bottoms[:, span(c)] = bottom_rows[c, ROWS:, :].astype(BF16)


def pack_halos(pert, near, far, owners, steps, block, capacity):
    members, _, variables, rows, cells = pert.shape
    owned = near.shape[0]
    blocks = owned // block
    first = (owners[:, None] * owned + block * jnp.arange(blocks, dtype=I32)[None, :]).reshape(-1)
    out = jax.ShapeDtypeStruct((capacity, cells), BF16)
    whole = pl.BlockSpec((capacity, cells), lambda i, lv, st: (0, 0))
    grad_block = (block, variables, rows, cells)
    return pl.pallas_call(
        pack_kernel,
        out_shape=(out, out),
        grid_spec=pltpu.PrefetchScalarGridSpec(
            num_scalar_prefetch=2,
            grid=(2 * blocks,),
            in_specs=[
                pl.BlockSpec((members,) + grad_block, lambda i, lv, st: (0, lv[i] // block, 0, 0, 0)),
                pl.BlockSpec(grad_block, lambda i, lv, st: (jnp.minimum(i, blocks - 1), 0, 0, 0)),
                pl.BlockSpec(grad_block, lambda i, lv, st: (jnp.maximum(i - blocks, 0), 0, 0, 0)),
            ],
            out_specs=[whole, whole],
            scratch_shapes=[
                pltpu.VMEM((cells // LANES, capacity + ROWS, LANES), F32),
                pltpu.VMEM((cells // LANES, capacity + ROWS, LANES), F32),
                pltpu.SMEM((1,), I32),
            ],
        ),
        compiler_params=pltpu.CompilerParams(vmem_limit_bytes=VMEM_BYTES),
        cost_estimate=cost(8 * near.size, 2 * near.size * 2 * (members + 1)),
    )(first, steps, pert, near, far)


def deep_product_kernel(levels, me, pert, *rest):
    grads, (out, pert_rows, grad_rows, pert_sem, grad_sem) = rest[:-5], rest[-5:]
    count, members = pert_rows.shape[:2]
    owned = grads[0].shape[0]
    planes = count * members
    chips = len(grads) // 2

    def pert_copy(k):
        return pltpu.make_async_copy(pert.at[:, levels[k]], pert_rows.at[k], pert_sem.at[k])

    def grad_copy(g, k):
        return pltpu.make_async_copy(grads[g].at[levels[k] % owned], grad_rows.at[k], grad_sem.at[k])

    def begin(k, carry):
        owner = levels[k] // owned
        shift = lax.rem(me[0] // 2 - owner // 2 + chips, chips)
        place = 2 * shift + lax.rem(me[0] + owner, 2)
        pert_copy(k).start()
        for g in range(len(grads)):
            @pl.when(place == g)
            def _():
                grad_copy(g, k).start()
        return carry

    lax.fori_loop(0, count, begin, 0)
    per_device = me[1]

    def form(k, carry):
        pert_copy(k).wait()
        grad_copy(0, k).wait()
        for m in range(members):
            q = k * members + m
            place = deep_place(q, planes, per_device)
            for c in range(pert.shape[-1] // LANES):
                total = None
                for v in range(pert.shape[2]):
                    term = pert_rows[k, m, v, :, span(c)].astype(F32) * grad_rows[k, v, :, span(c)].astype(F32)
                    total = term if total is None else total + term
                out[place, :, span(c)] = total.astype(BF16)
        return carry

    lax.fori_loop(0, count, form, 0)


def deep_products(pert, grads, levels, me, per_device):
    members, _, variables, rows, cells = pert.shape
    count = levels.shape[0]
    info = jnp.stack([me, jnp.int32(per_device)])
    return pl.pallas_call(
        deep_product_kernel,
        out_shape=jax.ShapeDtypeStruct((count * members, rows, cells), BF16),
        in_specs=[SMEM_SPEC, SMEM_SPEC] + [ANY_SPEC] * (1 + len(grads)),
        out_specs=VMEM_SPEC,
        scratch_shapes=[
            pltpu.VMEM((count, members, variables, rows, cells), BF16),
            pltpu.VMEM((count, variables, rows, cells), BF16),
            pltpu.SemaphoreType.DMA((count,)),
            pltpu.SemaphoreType.DMA((count,)),
        ],
        compiler_params=pltpu.CompilerParams(vmem_limit_bytes=VMEM_BYTES),
        cost_estimate=cost(count * members * rows * cells * 4, count * members * rows * cells * 8),
        name="deep_product",
    )(levels, info, pert, *grads)


def deep_kernel(counts, values, planes, class_map, out, field, keep, mix):
    at = pl.program_id(0)
    parts, _, rows, _ = planes.shape
    height = parts * rows
    tiles = field.shape[1]

    @pl.when(at == 0)
    def _():
        for c in range(tiles):
            field[0, c, :ROWS, :] = jnp.zeros((ROWS, LANES), F32)
            field[0, c, ROWS + height:, :] = jnp.zeros((ROWS, LANES), F32)
            store_weights(keep, mix, c, slice(0, height), diffusivity_of(class_map[:, span(c)], values))

    for p in range(parts):
        for c in range(tiles):
            field[0, c, ROWS + p * rows:ROWS + (p + 1) * rows, :] = planes[p, 0, :, span(c)].astype(F32)

    def step(i, carry):
        sweep(field, keep, mix, 0, ROWS, height)
        return carry

    lax.fori_loop(0, counts[at], step, 0)
    for p in range(parts):
        for c in range(tiles):
            out[p, 0, :, span(c)] = field[0, c, ROWS + p * rows:ROWS + (p + 1) * rows, :].astype(BF16)


def deep_smooth(planes, class_map, values, counts):
    parts, per_device, rows, cells = planes.shape
    tiles = cells // LANES
    plane = pl.BlockSpec((parts, 1, rows, cells), lambda i: (0, i, 0, 0))
    return pl.pallas_call(
        deep_kernel,
        out_shape=jax.ShapeDtypeStruct(planes.shape, BF16),
        grid=(per_device,),
        in_specs=[SMEM_SPEC, SMEM_SPEC, plane, VMEM_SPEC],
        out_specs=plane,
        scratch_shapes=[
            pltpu.VMEM((1, tiles, parts * rows + 2 * ROWS, LANES), F32),
            pltpu.VMEM((tiles, parts * rows, LANES), F32),
            pltpu.VMEM((tiles, parts * rows, LANES), F32),
        ],
        compiler_params=pltpu.CompilerParams(vmem_limit_bytes=VMEM_BYTES),
        cost_estimate=cost(150 * planes.size, planes.size * 4 + parts * rows * cells * 4),
        name="deep_smooth",
    )(counts, values, planes, class_map)


def deep_place(q, planes, per_device):
    devices = planes // per_device
    return lax.rem(q, devices) * per_device + q // devices


def smooth_kernel(with_deep, with_part, with_variance, info, steps, ranks, values, pert, grad, below, above, before, here, after, *rest):
    extra, (out, below_rows, above_rows, field, keep, mix, offset) = rest[:-7], rest[-7:]
    deep = extra[0] if with_deep else None
    extra = extra[1:] if with_deep else extra
    members, block = pert.shape[:2]
    capacity = below.shape[0]
    tiles = field.shape[1]
    owned = pl.num_programs(0) * block
    planes = deep.shape[0] if with_deep else 0
    at = pl.program_id(0)
    row = lax.broadcasted_iota(I32, (ROWS, LANES), 0)

    @pl.when(at == 0)
    def _():
        start = jnp.int32(0)
        for j in range(owned):
            start = start + steps[jnp.maximum(info[1], 0) + j]
        offset[0] = jnp.where(info[1] >= 0, members * start, 0)
        inside_before = jnp.broadcast_to(info[2] > 0, (ROWS, LANES))
        inside_after = jnp.broadcast_to(info[2] < info[3] - 1, (ROWS, LANES))
        for c in range(tiles):
            below_rows[c, :capacity, :] = below[:, span(c)].astype(F32)
            below_rows[c, capacity:, :] = jnp.zeros((ROWS, LANES), F32)
            above_rows[c, ROWS:, :] = above[:, span(c)].astype(F32)
            above_rows[c, :ROWS, :] = jnp.zeros((ROWS, LANES), F32)
            upper = diffusivity_of(before[:, span(c)], values, inside_before)
            lower = diffusivity_of(after[:, span(c)], values, inside_after)
            store_weights(keep, mix, c, slice(0, EDGE), upper[ROWS - EDGE:])
            store_weights(keep, mix, c, slice(EDGE, EDGE + ROWS), diffusivity_of(here[:, span(c)], values))
            store_weights(keep, mix, c, slice(EDGE + ROWS, 2 * EDGE + ROWS), lower[:EDGE])

    def one_level(j, carry):
        level = info[0] + at * block + j
        count = steps[level]
        rank = ranks[level]

        @pl.when(rank >= info[4])
        def _():
            for m in range(members):
                off = jnp.minimum(offset[0], capacity)
                for c in range(tiles):
                    field[m, c, :ROWS, :] = above_rows[c, pl.ds(capacity - off, ROWS), :]
                    field[m, c, ROWS:2 * ROWS, :] = product_of(pert, grad, m, j, c).astype(F32)
                    field[m, c, 2 * ROWS:, :] = below_rows[c, pl.ds(off, ROWS), :]
                offset[0] = off + count

            def step(i, carry):
                for m in range(members):
                    sweep(field, keep, mix, m, ROWS - EDGE, ROWS + 2 * EDGE)
                return carry

            lax.fori_loop(1, count, step, 0)

            for m in range(members):
                def store(c, value):
                    field[m, c, ROWS:2 * ROWS, :] = value

                diffuse_columns(field, keep, mix, m, ROWS, ROWS, EDGE, store)

        if deep is None:
            @pl.when(rank < info[4])
            def _():
                for m in range(members):
                    for c in range(tiles):
                        field[m, c, ROWS:2 * ROWS, :] = jnp.zeros((ROWS, LANES), F32)
        else:
            @pl.when(rank < info[4])
            def _():
                for m in range(members):
                    place = deep_place(rank * members + m, planes, info[5])
                    for c in range(tiles):
                        field[m, c, ROWS:2 * ROWS, :] = deep[place, :, span(c)].astype(F32)

        for c in range(tiles):
            smooth = [field[m, c, ROWS:2 * ROWS, :].astype(BF16).astype(F32) for m in range(members)]
            for v in range(out.shape[1]):
                total = None
                for m in range(members):
                    term = pert[m, j, v, :, span(c)].astype(F32) * smooth[m]
                    total = term if total is None else total + term
                if with_part:
                    total = total + extra[0][j, v, :, span(c)].astype(F32)
                if with_variance:
                    total = total + extra[0][j, v, :, span(c)] * grad[j, v, :, span(c)].astype(F32)
                out[j, v, :, span(c)] = total.astype(out.dtype)
        return carry

    lax.fori_loop(0, block, one_level, 0)


def smooth_owner(pert, grad, halos, class_map, deep, part, variance, info, steps, ranks, values, block, dtype):
    members, _, variables, rows, cells = pert.shape
    tiles = cells // LANES
    capacity = halos[0].shape[0]
    extra = [x for x in (part, variance) if x is not None]
    whole_deep = [] if deep is None else [deep]
    kernel = functools.partial(smooth_kernel, deep is not None, part is not None, variance is not None)
    row_tiles = class_map.shape[0] // rows

    def whole(shape):
        return pl.BlockSpec(shape, lambda i, *refs: (0,) * len(shape))

    def rows_at(shift):
        return pl.BlockSpec((rows, cells), lambda i, info, *refs: (jnp.clip(info[2] + shift, 0, row_tiles - 1), 0))

    grad_block = pl.BlockSpec((block, variables, rows, cells), lambda i, *refs: (i, 0, 0, 0))
    return pl.pallas_call(
        kernel,
        out_shape=jax.ShapeDtypeStruct(grad.shape, dtype),
        grid_spec=pltpu.PrefetchScalarGridSpec(
            num_scalar_prefetch=4,
            grid=(grad.shape[0] // block,),
            in_specs=[
                pl.BlockSpec((members, block, variables, rows, cells), lambda i, info, *refs: (0, info[0] // block + i, 0, 0, 0)),
                grad_block,
                whole(halos[0].shape), whole(halos[1].shape), rows_at(-1), rows_at(0), rows_at(1),
            ] + [whole(x.shape) for x in whole_deep] + [grad_block] * len(extra),
            out_specs=grad_block,
            scratch_shapes=[
                pltpu.VMEM((tiles, capacity + ROWS, LANES), F32),
                pltpu.VMEM((tiles, capacity + ROWS, LANES), F32),
                pltpu.VMEM((members, tiles, 3 * ROWS, LANES), F32),
                pltpu.VMEM((tiles, 2 * EDGE + ROWS, LANES), F32),
                pltpu.VMEM((tiles, 2 * EDGE + ROWS, LANES), F32),
                pltpu.SMEM((1,), I32),
            ],
        ),
        compiler_params=pltpu.CompilerParams(vmem_limit_bytes=VMEM_BYTES),
        cost_estimate=cost(100 * grad.size, grad.size * 2 * (members + 3)),
    )(info, steps, ranks, values, pert, grad, halos[0], halos[1], class_map, class_map, class_map, *whole_deep, *extra)


def final_kernel(info, ranks, pert, near, part, deep, *rest):
    arrived, out = rest[:-1], rest[-1]
    members = pert.shape[0]
    at = pl.program_id(0)
    rank = ranks[info[0] + at]
    planes = deep.shape[0]

    def terms(v, c):
        total = near[0, v, :, span(c)] + part[0, v, :, span(c)].astype(F32)
        for value in arrived:
            total = total + value[0, v, :, span(c)].astype(F32)
        return total

    @pl.when(rank >= info[4])
    def _():
        for v in range(out.shape[1]):
            for c in range(out.shape[3] // LANES):
                out[0, v, :, span(c)] = terms(v, c)

    @pl.when(rank < info[4])
    def _():
        for v in range(out.shape[1]):
            for c in range(out.shape[3] // LANES):
                total = terms(v, c)
                for m in range(members):
                    smooth = deep[deep_place(rank * members + m, planes, info[5]), :, span(c)].astype(F32)
                    total = total + pert[m, 0, v, :, span(c)].astype(F32) * smooth
                out[0, v, :, span(c)] = total


def final_sum(pert, near, part, deep, arrived, info, ranks):
    members, _, variables, rows, cells = pert.shape
    block = pl.BlockSpec((1, variables, rows, cells), lambda i, *refs: (i, 0, 0, 0))

    def deep_level(i, info, ranks):
        return (0, info[0] + jnp.where(ranks[info[0] + i] < info[4], i, 0), 0, 0, 0)

    return pl.pallas_call(
        final_kernel,
        out_shape=jax.ShapeDtypeStruct(near.shape, F32),
        grid_spec=pltpu.PrefetchScalarGridSpec(
            num_scalar_prefetch=2,
            grid=(near.shape[0],),
            in_specs=[
                pl.BlockSpec((members, 1, variables, rows, cells), deep_level),
                block, block, pl.BlockSpec(deep.shape, lambda i, *refs: (0, 0, 0)),
            ] + [block] * len(arrived),
            out_specs=block,
        ),
        compiler_params=pltpu.CompilerParams(vmem_limit_bytes=VMEM_BYTES),
        cost_estimate=cost(4 * near.size, near.size * 12),
        name="final_sum",
    )(info, ranks, pert, near, part, deep, *arrived)


def program(pert, gradient, variance, class_map, values, level_steps, ranks, top, capacity):
    members, levels, _, rows, cells = pert.shape
    mem_count = lax.axis_size("mem")
    tile_count = lax.axis_size("tile")
    me = lax.axis_index("mem")
    tile = lax.axis_index("tile")
    owned = gradient.shape[0]
    block = 4
    chips = mem_count // 2
    per_device = top * members // tile_count
    level_ids = jnp.arange(levels, dtype=I32)

    def hop(value, d):
        return lax.ppermute(value, "mem", [(i, ((i // 2 + d) % chips) * 2 + i % 2) for i in range(mem_count)])

    def swap(value):
        return lax.ppermute(value, "mem", [(i, i ^ 1) for i in range(mem_count)])

    south = [(i + 1, i) for i in range(tile_count - 1)]
    north = [(i, i + 1) for i in range(tile_count - 1)]

    steps = jnp.where(ranks < top, 0, level_steps)
    here = ranks[None, :] == level_ids[:top, None]
    deep_levels = jnp.sum(jnp.where(here, level_ids[None, :], 0), axis=1)
    deep_steps = jnp.sum(jnp.where(here, level_steps[None, :], 0), axis=1)
    my_ranks = (jnp.arange(per_device, dtype=I32) * tile_count + tile) // members
    my_steps = jnp.sum(jnp.where(my_ranks[:, None] == level_ids[None, :top], deep_steps[None, :], 0), axis=1)

    def owner(d, other):
        return ((me // 2 - d) % chips) * 2 + ((me % 2) ^ other)

    grads, halos = [], []
    far = []
    for d in range(1, chips):
        far.append(hop(gradient, d))
    for d in range(chips):
        near = gradient if d == 0 else far[d - 1]
        other = swap(near)
        grads += [near, other]
        if top < levels:
            owners = jnp.stack([owner(d, 0), owner(d, 1)])
            tops, bottoms = pack_halos(pert, near, other, owners, steps, block, capacity)
            below = lax.ppermute(tops, "tile", south)
            above = lax.ppermute(bottoms, "tile", north)
            halos.append((below, above))
        else:
            halos.append((jnp.zeros((16, cells), BF16),) * 2)

    deep = deep_products(pert, grads, deep_levels, me, per_device)
    deep = deep.reshape(tile_count, per_device, rows, cells)
    field = lax.all_to_all(deep, "tile", split_axis=0, concat_axis=0, tiled=True)
    field = deep_smooth(field, class_map, values, my_steps)
    deep = lax.all_to_all(field, "tile", split_axis=0, concat_axis=0, tiled=True).reshape(-1, rows, cells)

    def info_of(d, other):
        first = owner(d, other) * owned
        ahead = owner(d, 0) * owned if other else jnp.int32(-1)
        return jnp.stack([first, ahead, tile, jnp.int32(tile_count), jnp.int32(top), jnp.int32(per_device)])

    def smooth(d, other, whole, part, var, dtype):
        return smooth_owner(
            pert, grads[2 * d + other], halos[d], class_map, whole, part, var, info_of(d, other), steps, ranks, values, block, dtype
        )

    near_sum = smooth(0, 0, None, None, variance, F32)
    arrived = []
    for d in range(1, chips):
        part = smooth(d, 1, deep, None, None, BF16)
        part = swap(part)
        both = smooth(d, 0, deep, part, None, BF16)
        arrived.append(hop(both, chips - d))
    part = smooth(0, 1, deep, None, None, BF16)
    part = swap(part)
    return final_sum(pert, near_sum, part, deep, arrived, info_of(0, 0), ranks)


def shards(perturbations, gradient, static_variance, level_steps, class_map, class_diffusivity):
    members, levels = perturbations.shape[:2]
    owned = gradient.shape[0]
    top = lax.axis_size("tile") // members
    capacity = (5 * members * owned + 15) // 16 * 16
    level_ids = jnp.arange(levels, dtype=I32)
    ahead = (level_steps[None, :] > level_steps[:, None]) | (
        (level_steps[None, :] == level_steps[:, None]) & (level_ids[None, :] < level_ids[:, None])
    )
    ranks = jnp.sum(ahead.astype(I32), axis=1)
    steps = jnp.where(ranks < top, 0, level_steps)
    group_rows = members * jnp.sum(steps.reshape(-1, 2 * owned), axis=1)
    fits = (jnp.max(steps) <= EDGE) & (jnp.max(group_rows) <= capacity)
    operands = (perturbations, gradient, static_variance, class_map, class_diffusivity, level_steps, ranks)

    result = program(*operands, top, capacity)

    def general(result, *operands):
        return program(*operands, levels, 16)

    return lax.cond(fits, lambda result, *operands: result, general, result, *operands)


def solution(mesh):
    placed = (
        P("mem", None, None, "tile", None),
        P("mem", None, "tile", None),
        P("mem", None, "tile", None),
        P(),
        P(),
        P(),
    )
    return jax.shard_map(
        shards, mesh=mesh, in_specs=placed, out_specs=P("mem", None, "tile", None), check_vma=False
    )
```

time: 386 us -> 178 us (0.46)
  waiting for transfers between devices: 226 us -> 78.4 us
  other arithmetic: 69 us -> 5.78 us
  Pallas kernels: 0 us -> 58.6 us
  local copies, waits for them, and re-layouts: 48.7 us -> 7.49 us
  loops' own time: 18.8 us -> 0.01 us
  starting transfers between devices: 9.65 us -> 25.3 us
  between operations: 13.5 us -> 1.42 us
    all_to_all x2, waiting for transfers between devices: 138 us -> 10.8 us  [the longest x1 10.8 us: program(): lax.all_to_all(deep, 'tile', split_axis=0, concat_axis=0, tiled=True)]
    ppermute x0 -> x10, waiting for transfers between devices: none -> 67.6 us  [the longest x2 29.8 us: hop(): lax.ppermute(value, 'mem', [(i, (i // 2 + d) % chips * 2 + i % 2) for i i...]
    pallas_call x0 -> x9, Pallas kernels: none -> 58.6 us  [the longest x4 30 us: smooth_owner(): pl.pallas_call(kernel, out_shape=jax.ShapeDtypeStruct(grad.shape, dtype),...]
    reduce_scatter x1 -> x0, waiting for transfers between devices: 57.1 us -> none  [shards(): lax.psum_scatter(partial_value, 'mem', scatter_dimension=0, tiled=True)]
    all_gather x1 -> x0, waiting for transfers between devices: 29.3 us -> none  [shards(): full_grad = lax.all_gather(gradient, 'mem', axis=0, tiled=True)]
    slice x115 -> x0, local copies, waits for them, and re-layouts: 25.5 us -> none  [the longest x46 14.5 us: diffusion_step(): jnp.roll(southern, 1, axis=1)]
    add x24 -> x1, other arithmetic: 23.3 us -> 0.07 us  [pack_halos(): owners[:, None] * owned + block * jnp.arange(blocks, dtype=I32)[None, :]]
    another operation x9 -> x1, loops' own time: 18.8 us -> 0.01 us  [shards(): lax.cond(fits, lambda result, *operands: result, general, result, *operands)]
  transfers between devices with their start and end apart: 4 -> 12, of which waited for: 4 -> 7; matrix products, arithmetic and copies ran while one was open for 2% -> 5% of each run, Pallas kernels for 0% -> 19%
where the time goes in v1:
time: 178 us; the launch traced here: 177 us
  waiting for transfers between devices  78.4 us (44%)
  Pallas kernels  58.6 us (33%)
  starting transfers between devices  25.3 us (14%)
  local copies, waits for them, and re-layouts  7.49 us (4%)
  other arithmetic  5.78 us (3%)
    pallas_call x4, Pallas kernels, smooth_owner(): pl.pallas_call(kernel, out_shape=jax.ShapeDtypeStruct(grad.shape, dtype),...  30 us
    ppermute x2, waiting for transfers between devices, hop(): lax.ppermute(value, 'mem', [(i, (i // 2 + d) % chips * 2 + i % 2) for i i...  29.8 us
    ppermute x2, waiting for transfers between devices, program(): above = lax.ppermute(bottoms, 'tile', north)  21.4 us
    ppermute x2, waiting for transfers between devices, program(): below = lax.ppermute(tops, 'tile', south)  16.4 us
    all_to_all x1, waiting for transfers between devices, program(): lax.all_to_all(deep, 'tile', split_axis=0, concat_axis=0, tiled=True)  10.8 us
    pallas_call x2, Pallas kernels, pack_halos(): pl.pallas_call(pack_kernel, out_shape=(out, out), grid_spec=pltpu.Prefetc...  10.6 us
    ppermute x2, starting transfers between devices, program(): above = lax.ppermute(bottoms, 'tile', north)  9.51 us
    pallas_call x1, Pallas kernels, deep_smooth(): pl.pallas_call(deep_kernel, out_shape=jax.ShapeDtypeStruct(planes.shape,...  7.71 us
  transfers between devices with their start and end apart: 12, of which 7 were waited for; matrix products, arithmetic and copies ran while one was open for 5% of the time, Pallas kernels for 19%

profile of v1, /device:TPU:0, one launch (start us, length us, event | category | flops | bytes accessed | tf_op | source)
XLA Modules:
  0.0 176.9 jit_solution(15915032135982396575)
XLA Ops:
  0.0 3.0 %collective-permute-start.9 = (bf16[8,2,8,3072]{3,2,1,0:T(8,128)(2,1)}, bf16[8,2,8,3072]{3,2,1,0:T(8,128)(2,1)S(1)}, u32[]{:S(2)}, u32[]{:S(2)}) collective-permute-start(bf16[8,2,8,3072]{3,2,1,0:T(8,128)(2,1)} %rest_0_.3), channel_id=1, source_target_pairs={{0,16},{8,24},{16,0},{24,8},{1,17},{9,25},{17,1},{25,9},{2,18},{10... | collective-permute-start | bytes 2359304 | tf_op jit(solution)/shard_map/ppermute | solution.py:472
  3.0 17.7 %collective-permute-done.9.rest_2_.near.grad = bf16[8,2,8,3072]{3,2,1,0:T(8,128)(2,1)S(1)} collective-permute-done((bf16[8,2,8,3072]{3,2,1,0:T(8,128)(2,1)}, bf16[8,2,8,3072]{3,2,1,0:T(8,128)(2,1)S(1)}, u32[]{:S(2)}, u32[]{:S(2)}) %collective-permute-start.9) | collective-permute-done | bytes 786464 | tf_op jit(solution)/shard_map/ppermute | solution.py:472
  20.7 0.7 pad_add_fusion.1.me
  21.4 0.9 convert_reduce_fusion.ranks
  22.3 1.4 fusion.3
  23.8 0.9 copy-done.4
  24.9 3.1 %deep_product.3 = bf16[8,8,3072]{2,1,0:T(8,128)(2,1)} custom-call(s32[4]{0:T(128)} %get-tuple-element.41.levels, s32[2]{0:T(128)} %pad_add_fusion.1.me, bf16[2,32,2,8,3072]{4,3,2,1,0:T(8,128)(2,1)} %pert.15, bf16[8,2,8,3072]{3,2,1,0:T(8,128)(2,1)} %rest_0_.3, bf16[8,2,8,3072]{3,2,1,0:T(8,128)(2,1)} %copy-done.4, bf16[8,2,8,3072]{3,2,1,0:T(8,128)(2,1)} %copy-done.3, ...), custom_call_target="tpu_custom_call" | custom-call | flops 786432 | bytes 1572864 | tf_op jit(solution)/shard_map/deep_product/pallas_call | solution.py:202
  28.0 6.1 %all-to-all-start.2 = ((bf16[8,1,8,3072]{3,2,1,0:T(8,128)(2,1)}), bf16[8,1,8,3072]{3,2,1,0:T(8,128)(2,1)S(1)}, u32[]{:S(2)}, u32[]{:S(2)}) async-start(bf16[8,1,8,3072]{3,2,1,0:T(8,128)(2,1)} %bitcast.28), calls=%async_computation.2 | async-start | bytes 786432 | tf_op jit(solution)/shard_map/all_to_all | solution.py:509
  35.5 10.8 %all-to-all-done.2.planes = bf16[8,1,8,3072]{3,2,1,0:T(8,128)(2,1)S(1)} async-done(((bf16[8,1,8,3072]{3,2,1,0:T(8,128)(2,1)}), bf16[8,1,8,3072]{3,2,1,0:T(8,128)(2,1)S(1)}, u32[]{:S(2)}, u32[]{:S(2)}) %all-to-all-start.2) | async-done | bytes 393248 | tf_op jit(solution)/shard_map/all_to_all | solution.py:509
  46.3 0.8 copy-done.11
  47.1 7.7 %deep_smooth.3 = bf16[8,1,8,3072]{3,2,1,0:T(8,128)(2,1)} custom-call(s32[1]{0:T(128)} %bitcast.14.counts, f32[4]{0:T(128)S(1)} %copy-done.12, bf16[8,1,8,3072]{3,2,1,0:T(8,128)(2,1)} %copy-done.11, s32[64,3072]{1,0:T(8,128)S(1)} %copy-done), custom_call_target="tpu_custom_call" | custom-call | flops 29491200 | bytes 1572864 | tf_op jit(solution)/shard_map/deep_smooth/pallas_call | solution.py:250
  54.8 3.5 %all-to-all-start.3 = ((bf16[8,1,8,3072]{3,2,1,0:T(8,128)(2,1)}), bf16[8,1,8,3072]{3,2,1,0:T(8,128)(2,1)S(1)}, u32[]{:S(2)}, u32[]{:S(2)}) async-start(bf16[8,1,8,3072]{3,2,1,0:T(8,128)(2,1)} %deep_smooth.3), calls=%async_computation.3 | async-start | bytes 786432 | tf_op jit(solution)/shard_map/all_to_all | solution.py:511
  58.3 1.2 fusion.5
  59.5 5.4 %shard_map.69 = (bf16[80,3072]{1,0:T(8,128)(2,1)}, bf16[80,3072]{1,0:T(8,128)(2,1)}) custom-call(s32[4]{0:T(128)} %add.151.first, s32[32]{0:T(128)} %get-tuple-element.44.steps, bf16[2,32,2,8,3072]{4,3,2,1,0:T(8,128)(2,1)} %pert.15, bf16[8,2,8,3072]{3,2,1,0:T(8,128)(2,1)} %copy-done.3, bf16[8,2,8,3072]{3,2,1,0:T(8,128)(2,1)} %copy-done.5), custom_call_target="tpu_custom_call" | custom-call | flops 3145728 | bytes 4718592 | tf_op jit(solution)/shard_map/pallas_call | solution.py:131
  64.9 1.3 collective-permute-start.12
  66.1 4.6 %collective-permute-start.13 = (bf16[80,3072]{1,0:T(8,128)(2,1)}, bf16[80,3072]{1,0:T(8,128)(2,1)S(1)}, u32[]{:S(2)}, u32[]{:S(2)}) collective-permute-start(bf16[80,3072]{1,0:T(8,128)(2,1)} %get-tuple-element.37), channel_id=1, source_target_pairs={{0,1},{1,2},{2,3},{3,4},{4,5},{5,6},{6,7},{8,9},{9,10},{10,11},{11... | collective-permute-start | bytes 1474568 | tf_op jit(solution)/shard_map/ppermute | solution.py:502
  71.3 8.0 %collective-permute-done.12.below = bf16[80,3072]{1,0:T(8,128)(2,1)S(1)} collective-permute-done((bf16[80,3072]{1,0:T(8,128)(2,1)}, bf16[80,3072]{1,0:T(8,128)(2,1)S(1)}, u32[]{:S(2)}, u32[]{:S(2)}) %collective-permute-start.12) | collective-permute-done | bytes 491552 | tf_op jit(solution)/shard_map/ppermute | solution.py:501
  79.4 10.6 %collective-permute-done.13.above = bf16[80,3072]{1,0:T(8,128)(2,1)S(1)} collective-permute-done((bf16[80,3072]{1,0:T(8,128)(2,1)}, bf16[80,3072]{1,0:T(8,128)(2,1)S(1)}, u32[]{:S(2)}, u32[]{:S(2)}) %collective-permute-start.13) | collective-permute-done | bytes 491552 | tf_op jit(solution)/shard_map/ppermute | solution.py:502
  90.0 0.8 copy-done.8
  90.9 7.5 %shard_map.70 = bf16[8,2,8,3072]{3,2,1,0:T(8,128)(2,1)} custom-call(s32[6]{0:T(128)} %stack.116.info, s32[32]{0:T(128)} %get-tuple-element.44.steps, s32[32]{0:T(128)S(1)} %convert_reduce_fusion.ranks, f32[4]{0:T(128)S(1)} %copy-done.12, bf16[2,32,2,8,3072]{4,3,2,1,0:T(8,128)(2,1)} %pert.15, bf16[8,2,8,3072]{3,2,1,0:T(8,128)(2,1)} %copy-done.5, ...), custom_call_target="tpu_custom_call" | custom-call | flops 39321600 | bytes 3932160 | tf_op jit(solution)/shard_map/pallas_call | solution.py:378
  99.7 5.2 %shard_map.66 = (bf16[80,3072]{1,0:T(8,128)(2,1)}, bf16[80,3072]{1,0:T(8,128)(2,1)}) custom-call(s32[4]{0:T(128)} %add.145.first, s32[32]{0:T(128)} %get-tuple-element.44.steps, bf16[2,32,2,8,3072]{4,3,2,1,0:T(8,128)(2,1)} %pert.15, bf16[8,2,8,3072]{3,2,1,0:T(8,128)(2,1)S(1)} %copy-done.1, bf16[8,2,8,3072]{3,2,1,0:T(8,128)(2,1)} %copy-done.4), custom_call_target="tpu_custom_call" | custom-call | flops 3145728 | bytes 4718592 | tf_op jit(solution)/shard_map/pallas_call | solution.py:131
  104.9 1.3 collective-permute-start.7
  106.2 4.9 %collective-permute-start.8 = (bf16[80,3072]{1,0:T(8,128)(2,1)}, bf16[80,3072]{1,0:T(8,128)(2,1)S(1)}, u32[]{:S(2)}, u32[]{:S(2)}) collective-permute-start(bf16[80,3072]{1,0:T(8,128)(2,1)} %get-tuple-element.35), channel_id=1, source_target_pairs={{0,1},{1,2},{2,3},{3,4},{4,5},{5,6},{6,7},{8,9},{9,10},{10,11},{11... | collective-permute-start | bytes 1474568 | tf_op jit(solution)/shard_map/ppermute | solution.py:502
  111.1 0.7 stack.111.info
  112.4 8.4 %collective-permute-done.7.below = bf16[80,3072]{1,0:T(8,128)(2,1)S(1)} collective-permute-done((bf16[80,3072]{1,0:T(8,128)(2,1)}, bf16[80,3072]{1,0:T(8,128)(2,1)S(1)}, u32[]{:S(2)}, u32[]{:S(2)}) %collective-permute-start.7) | collective-permute-done | bytes 491552 | tf_op jit(solution)/shard_map/ppermute | solution.py:501
  120.7 10.8 %collective-permute-done.8.above = bf16[80,3072]{1,0:T(8,128)(2,1)S(1)} collective-permute-done((bf16[80,3072]{1,0:T(8,128)(2,1)}, bf16[80,3072]{1,0:T(8,128)(2,1)S(1)}, u32[]{:S(2)}, u32[]{:S(2)}) %collective-permute-start.8) | collective-permute-done | bytes 491552 | tf_op jit(solution)/shard_map/ppermute | solution.py:502
  131.5 0.8 copy-done.10
  132.3 8.5 %shard_map.68 = bf16[8,2,8,3072]{3,2,1,0:T(8,128)(2,1)} custom-call(s32[6]{0:T(128)} %stack.107.info, s32[32]{0:T(128)} %get-tuple-element.44.steps, s32[32]{0:T(128)S(1)} %convert_reduce_fusion.ranks, f32[4]{0:T(128)S(1)} %copy-done.12, bf16[2,32,2,8,3072]{4,3,2,1,0:T(8,128)(2,1)} %pert.15, bf16[8,2,8,3072]{3,2,1,0:T(8,128)(2,1)} %copy-done.4, ...), custom_call_target="tpu_custom_call" | custom-call | flops 39321600 | bytes 3932160 | tf_op jit(solution)/shard_map/pallas_call | solution.py:378
  140.9 8.3 %shard_map.71 = bf16[8,2,8,3072]{3,2,1,0:T(8,128)(2,1)} custom-call(s32[6]{0:T(128)} %stack.111.info, s32[32]{0:T(128)} %get-tuple-element.44.steps, s32[32]{0:T(128)S(1)} %convert_reduce_fusion.ranks, f32[4]{0:T(128)S(1)} %copy-done.12, bf16[2,32,2,8,3072]{4,3,2,1,0:T(8,128)(2,1)} %pert.15, bf16[8,2,8,3072]{3,2,1,0:T(8,128)(2,1)} %copy-done.3, ...), custom_call_target="tpu_custom_call" | custom-call | flops 39321600 | bytes 3932160 | tf_op jit(solution)/shard_map/pallas_call | solution.py:378
  151.9 5.9 %shard_map.67.near = f32[8,2,8,3072]{3,2,1,0:T(8,128)} custom-call(s32[6]{0:T(128)} %stack.102.info, s32[32]{0:T(128)} %get-tuple-element.44.steps, s32[32]{0:T(128)S(1)} %convert_reduce_fusion.ranks, f32[4]{0:T(128)S(1)} %copy-done.12, bf16[2,32,2,8,3072]{4,3,2,1,0:T(8,128)(2,1)} %pert.15, bf16[8,2,8,3072]{3,2,1,0:T(8,128)(2,1)S(1)} %copy-done.1, ...), custom_call_target="tpu_custom_call" | custom-call | flops 39321600 | bytes 3932160 | tf_op jit(solution)/shard_map/pallas_call | solution.py:378
  157.7 12.0 %collective-permute-done.15.rest_0_ = bf16[8,2,8,3072]{3,2,1,0:T(8,128)(2,1)} collective-permute-done((bf16[8,2,8,3072]{3,2,1,0:T(8,128)(2,1)}, bf16[8,2,8,3072]{3,2,1,0:T(8,128)(2,1)}, u32[]{:S(2)}, u32[]{:S(2)}) %collective-permute-start.15) | collective-permute-done | bytes 786464 | tf_op jit(solution)/shard_map/ppermute | solution.py:472
  169.8 7.2 %final_sum.3 = f32[8,2,8,3072]{3,2,1,0:T(8,128)} custom-call(s32[6]{0:T(128)} %stack.102.info, s32[32]{0:T(128)S(1)} %convert_reduce_fusion.ranks, bf16[2,32,2,8,3072]{4,3,2,1,0:T(8,128)(2,1)} %pert.15, f32[8,2,8,3072]{3,2,1,0:T(8,128)} %shard_map.67.near, bf16[8,2,8,3072]{3,2,1,0:T(8,128)(2,1)} %collective-permute-done.11.part, ...), custom_call_target="tpu_custom_call" | custom-call | flops 1572864 | bytes 4718592 | tf_op jit(solution)/shard_map/final_sum/pallas_call | solution.py:441
  (50 shorter events, 5.9 us)
Async XLA Ops:
  0.0 20.7 %collective-permute-start.9 = (bf16[8,2,8,3072]{3,2,1,0:T(8,128)(2,1)}, bf16[8,2,8,3072]{3,2,1,0:T(8,128)(2,1)S(1)}, u32[]{:S(2)}, u32[]{:S(2)}) collective-permute-start(bf16[8,2,8,3072]{3,2,1,0:T(8,128)(2,1)} %rest_0_.3), channel_id=1, source_target_pairs={{0,16},{8,24},{16,0},{24,8},{1,17},{9,25},{17,1},{25,9},{2,18},{10... | collective-permute-start | bytes 2359304 | tf_op jit(solution)/shard_map/ppermute | solution.py:472
  3.0 20.8 %collective-permute-start.6 = (bf16[8,2,8,3072]{3,2,1,0:T(8,128)(2,1)}, bf16[8,2,8,3072]{3,2,1,0:T(8,128)(2,1)S(1)}, u32[]{:S(2)}, u32[]{:S(2)}) collective-permute-start(bf16[8,2,8,3072]{3,2,1,0:T(8,128)(2,1)} %rest_0_.3), channel_id=1, source_target_pairs={{0,8},{8,0},{16,24},{24,16},{1,9},{9,1},{17,25},{25,17},{2,10},{10... | collective-permute-start | bytes 2359304 | tf_op jit(solution)/shard_map/ppermute | solution.py:475
  20.7 3.0 %copy-start.3 = (bf16[8,2,8,3072]{3,2,1,0:T(8,128)(2,1)}, bf16[8,2,8,3072]{3,2,1,0:T(8,128)(2,1)S(1)}, u32[]{:S(2)}) copy-start(bf16[8,2,8,3072]{3,2,1,0:T(8,128)(2,1)S(1)} %collective-permute-done.9.rest_2_.near.grad) | copy-start | bytes 2359300
  20.7 3.0 %collective-permute-start.10 = (bf16[8,2,8,3072]{3,2,1,0:T(8,128)(2,1)S(1)}, bf16[8,2,8,3072]{3,2,1,0:T(8,128)(2,1)S(1)}, u32[]{:S(2)}, u32[]{:S(2)}) collective-permute-start(bf16[8,2,8,3072]{3,2,1,0:T(8,128)(2,1)S(1)} %collective-permute-done.9.rest_2_.near.grad), channel_id=1, source_target_pairs={{0,8},{8,0},{16,24},{24,16},{1,9},{9,1},{17,25},{25,17},{2,10},{10... | collective-permute-start | bytes 2359304 | tf_op jit(solution)/shard_map/ppermute | solution.py:475
  23.7 0.9 copy-start.4
  23.7 1.2 copy-start.5
  24.9 22.2 %copy-start = (s32[64,3072]{1,0:T(8,128)S(1)}, s32[64,3072]{1,0:T(8,128)}, u32[]{:S(2)}) copy-start(s32[64,3072]{1,0:T(8,128)} %after.7) | copy-start | bytes 2359300
  24.9 22.2 %copy-start.12 = (f32[4]{0:T(128)S(1)}, f32[4]{0:T(128)}, u32[]{:S(2)}) copy-start(f32[4]{0:T(128)} %values.9) | copy-start | bytes 52
  28.0 30.3 %copy-start.14 = (s32[32]{0:T(128)S(1)}, s32[32]{0:T(128)}, u32[]{:S(2)}) copy-start(s32[32]{0:T(128)} %param.11) | copy-start | bytes 388
  28.0 18.3 %all-to-all-start.2 = ((bf16[8,1,8,3072]{3,2,1,0:T(8,128)(2,1)}), bf16[8,1,8,3072]{3,2,1,0:T(8,128)(2,1)S(1)}, u32[]{:S(2)}, u32[]{:S(2)}) async-start(bf16[8,1,8,3072]{3,2,1,0:T(8,128)(2,1)} %bitcast.28), calls=%async_computation.2 | async-start | bytes 786432 | tf_op jit(solution)/shard_map/all_to_all | solution.py:509
  46.3 0.8 copy-start.11
  54.8 35.2 %all-to-all-start.3 = ((bf16[8,1,8,3072]{3,2,1,0:T(8,128)(2,1)}), bf16[8,1,8,3072]{3,2,1,0:T(8,128)(2,1)S(1)}, u32[]{:S(2)}, u32[]{:S(2)}) async-start(bf16[8,1,8,3072]{3,2,1,0:T(8,128)(2,1)} %deep_smooth.3), calls=%async_computation.3 | async-start | bytes 786432 | tf_op jit(solution)/shard_map/all_to_all | solution.py:511
  64.9 14.5 %collective-permute-start.12 = (bf16[80,3072]{1,0:T(8,128)(2,1)}, bf16[80,3072]{1,0:T(8,128)(2,1)S(1)}, u32[]{:S(2)}, u32[]{:S(2)}) collective-permute-start(bf16[80,3072]{1,0:T(8,128)(2,1)} %get-tuple-element.36), channel_id=1, source_target_pairs={{1,0},{2,1},{3,2},{4,3},{5,4},{6,5},{7,6},{9,8},{10,9},{11,10},{12... | collective-permute-start | bytes 1474568 | tf_op jit(solution)/shard_map/ppermute | solution.py:501
  66.1 23.9 %collective-permute-start.13 = (bf16[80,3072]{1,0:T(8,128)(2,1)}, bf16[80,3072]{1,0:T(8,128)(2,1)S(1)}, u32[]{:S(2)}, u32[]{:S(2)}) collective-permute-start(bf16[80,3072]{1,0:T(8,128)(2,1)} %get-tuple-element.37), channel_id=1, source_target_pairs={{0,1},{1,2},{2,3},{3,4},{4,5},{5,6},{6,7},{8,9},{9,10},{10,11},{11... | collective-permute-start | bytes 1474568 | tf_op jit(solution)/shard_map/ppermute | solution.py:502
  79.4 10.7 %copy-start.7 = (bf16[80,3072]{1,0:T(8,128)(2,1)}, bf16[80,3072]{1,0:T(8,128)(2,1)S(1)}, u32[]{:S(2)}) copy-start(bf16[80,3072]{1,0:T(8,128)(2,1)S(1)} %collective-permute-done.12.below) | copy-start | bytes 1474564
  90.0 0.8 copy-start.8
  90.0 0.9 copy-start.2
  90.9 8.7 %copy-start.1 = (bf16[8,2,8,3072]{3,2,1,0:T(8,128)(2,1)S(1)}, bf16[8,2,8,3072]{3,2,1,0:T(8,128)(2,1)}, u32[]{:S(2)}) copy-start(bf16[8,2,8,3072]{3,2,1,0:T(8,128)(2,1)} %rest_0_.3) | copy-start | bytes 2359300
  98.4 42.5 %collective-permute-start.14 = (bf16[8,2,8,3072]{3,2,1,0:T(8,128)(2,1)}, bf16[8,2,8,3072]{3,2,1,0:T(8,128)(2,1)}, u32[]{:S(2)}, u32[]{:S(2)}) collective-permute-start(bf16[8,2,8,3072]{3,2,1,0:T(8,128)(2,1)} %shard_map.70), channel_id=1, source_target_pairs={{0,8},{8,0},{16,24},{24,16},{1,9},{9,1},{17,25},{25,17},{2,10},{10... | collective-permute-start | bytes 2359304 | tf_op jit(solution)/shard_map/ppermute | solution.py:475
  104.9 15.9 %collective-permute-start.7 = (bf16[80,3072]{1,0:T(8,128)(2,1)}, bf16[80,3072]{1,0:T(8,128)(2,1)S(1)}, u32[]{:S(2)}, u32[]{:S(2)}) collective-permute-start(bf16[80,3072]{1,0:T(8,128)(2,1)} %get-tuple-element.34), channel_id=1, source_target_pairs={{1,0},{2,1},{3,2},{4,3},{5,4},{6,5},{7,6},{9,8},{10,9},{11,10},{12... | collective-permute-start | bytes 1474568 | tf_op jit(solution)/shard_map/ppermute | solution.py:501
  106.2 25.4 %collective-permute-start.8 = (bf16[80,3072]{1,0:T(8,128)(2,1)}, bf16[80,3072]{1,0:T(8,128)(2,1)S(1)}, u32[]{:S(2)}, u32[]{:S(2)}) collective-permute-start(bf16[80,3072]{1,0:T(8,128)(2,1)} %get-tuple-element.35), channel_id=1, source_target_pairs={{0,1},{1,2},{2,3},{3,4},{4,5},{5,6},{6,7},{8,9},{9,10},{10,11},{11... | collective-permute-start | bytes 1474568 | tf_op jit(solution)/shard_map/ppermute | solution.py:502
  120.7 10.8 %copy-start.9 = (bf16[80,3072]{1,0:T(8,128)(2,1)}, bf16[80,3072]{1,0:T(8,128)(2,1)S(1)}, u32[]{:S(2)}) copy-start(bf16[80,3072]{1,0:T(8,128)(2,1)S(1)} %collective-permute-done.7.below) | copy-start | bytes 1474564
  131.5 0.8 copy-start.10
  140.8 8.9 %copy-start.13 = (s32[32]{0:T(128)S(1)}, s32[32]{0:T(128)}, u32[]{:S(2)}) copy-start(s32[32]{0:T(128)} %get-tuple-element.44.steps) | copy-start | bytes 388
  140.8 11.1 %copy-start.6 = (f32[8,2,8,3072]{3,2,1,0:T(8,128)S(1)}, f32[8,2,8,3072]{3,2,1,0:T(8,128)}, u32[]{:S(2)}) copy-start(f32[8,2,8,3072]{3,2,1,0:T(8,128)} %rest_0_.2) | copy-start | bytes 4718596
  140.8 16.9 %collective-permute-start.11 = (bf16[8,2,8,3072]{3,2,1,0:T(8,128)(2,1)}, bf16[8,2,8,3072]{3,2,1,0:T(8,128)(2,1)}, u32[]{:S(2)}, u32[]{:S(2)}) collective-permute-start(bf16[8,2,8,3072]{3,2,1,0:T(8,128)(2,1)} %shard_map.68), channel_id=1, source_target_pairs={{0,8},{8,0},{16,24},{24,16},{1,9},{9,1},{17,25},{25,17},{2,10},{10... | collective-permute-start | bytes 2359304 | tf_op jit(solution)/shard_map/ppermute | solution.py:475
  149.1 20.6 %collective-permute-start.15 = (bf16[8,2,8,3072]{3,2,1,0:T(8,128)(2,1)}, bf16[8,2,8,3072]{3,2,1,0:T(8,128)(2,1)}, u32[]{:S(2)}, u32[]{:S(2)}) collective-permute-start(bf16[8,2,8,3072]{3,2,1,0:T(8,128)(2,1)} %shard_map.71), channel_id=1, source_target_pairs={{0,16},{8,24},{16,0},{24,8},{1,17},{9,25},{17,1},{25,9},{2,18},{10... | collective-permute-start | bytes 2359304 | tf_op jit(solution)/shard_map/ppermute | solution.py:472

commit v2 on v1

v2 whole, which is shorter than its diff:
```python
import functools
import jax
import jax.numpy as jnp
from jax import lax
from jax.experimental import pallas as pl
from jax.experimental.pallas import tpu as pltpu
from jax.sharding import PartitionSpec as P

F32 = jnp.float32
BF16 = jnp.bfloat16
I32 = jnp.int32
LANES = 128
ROWS = 8
EDGE = 4
PARTS = 2
VMEM_BYTES = 67043328
SMEM_SPEC = pl.BlockSpec(memory_space=pltpu.SMEM)
VMEM_SPEC = pl.BlockSpec(memory_space=pltpu.VMEM)
ANY_SPEC = pl.BlockSpec(memory_space=pl.ANY)


def cost(flops, size):
    return pl.CostEstimate(flops=int(flops), transcendentals=0, bytes_accessed=int(size))


def span(c):
    return slice(c * LANES, (c + 1) * LANES)


def diffuse_columns(field, keep, mix, index, first, rows, weight_first):
    tiles = field.shape[1]
    lane = lax.broadcasted_iota(I32, (rows, LANES), 1)
    first_lane = lane == 0
    last_lane = lane == LANES - 1

    def load(c):
        here = field[index, c, first:first + rows, :]
        beside = field[index, c, first - 1:first - 1 + rows, :] + field[index, c, first + 1:first + 1 + rows, :]
        line = 4.0 * here + beside
        return here, line, pltpu.roll(line, 1, axis=1), pltpu.roll(line, LANES - 1, axis=1)

    here, line, to_east, to_west = load(0)
    start_west = to_west
    before = load(tiles - 1)[2]
    for c in range(tiles):
        if c + 1 < tiles:
            there = load(c + 1)
            after = there[3]
        else:
            there, after = None, start_west
        west = jnp.where(first_lane, before, to_east)
        east = jnp.where(last_lane, after, to_west)
        across = 4.0 * line + (west + east)
        place = slice(weight_first, weight_first + rows)
        yield keep[c, place, :] * here + mix[c, place, :] * across
        if there is not None:
            before = to_east
            here, line, to_east, to_west = there


def sweep(field, keep, mix, index, first, rows):
    for c, value in enumerate(diffuse_columns(field, keep, mix, index, first, rows, 0)):
        field[index, c, first:first + rows, :] = value


def diffusivity_of(classes, values, valid=None):
    total = jnp.zeros(classes.shape, F32)
    for k in range(values.shape[0]):
        total = jnp.where(classes == k, values[k], total)
    return total if valid is None else jnp.where(valid, total, 0.0)


def store_weights(keep, mix, c, place, diffusivity):
    keep[c, place, :] = 1.0 - 6.0 * diffusivity
    mix[c, place, :] = diffusivity * (1.0 / 6.0)


class Plan:
    ME, TILE, FITS = 0, 1, 2

    def __init__(self, levels, top, per_device):
        self.steps = 8
        self.ranks = self.steps + levels
        self.deep = self.ranks + levels
        self.mine = self.deep + top + 1
        self.size = self.mine + per_device


BINS = 16


def plan_kernel(places, top, per_device, owned, members, capacity, position, level_steps, values, before, here, after, plan, keep, mix, bins, deep_steps):
    levels = level_steps.shape[0]
    me, tile, tile_count = position[0], position[1], position[2]
    plan[places.ME] = me
    plan[places.TILE] = tile
    for i in range(3, 8):
        plan[i] = 0

    def bin_of(level):
        return jnp.clip(level_steps[level], 0, BINS - 1)

    for i in range(BINS):
        bins[i] = 0

    def count(level, carry):
        bins[bin_of(level)] += 1
        return carry

    lax.fori_loop(0, levels, count, 0)
    total = jnp.int32(0)
    for i in reversed(range(BINS)):
        here_count = bins[i]
        bins[i] = total
        total = total + here_count

    def assign(level, carry):
        rows, most_rows, most_steps = carry
        b = bin_of(level)
        rank = bins[b]
        bins[b] = rank + 1
        whole = rank < top
        steps = jnp.where(whole, 0, level_steps[level])
        plan[places.ranks + level] = rank
        plan[places.steps + level] = steps
        slot = jnp.minimum(rank, top)
        plan[places.deep + slot] = level
        deep_steps[slot] = level_steps[level]
        rows = jnp.where(lax.rem(level, 2 * owned) == 0, 0, rows) + members * steps
        return rows, jnp.maximum(most_rows, rows), jnp.maximum(most_steps, steps)

    _, most_rows, most_steps = lax.fori_loop(0, levels, assign, (jnp.int32(0), jnp.int32(0), jnp.int32(0)))
    plan[places.FITS] = ((most_rows <= capacity) & (most_steps <= EDGE)).astype(I32)
    plan[places.deep + top] = 0
    for j in range(per_device):
        plan[places.mine + j] = deep_steps[(j * tile_count + tile) // members]

    inside_before = jnp.broadcast_to(tile > 0, (ROWS, LANES))
    inside_after = jnp.broadcast_to(tile < tile_count - 1, (ROWS, LANES))
    for c in range(keep.shape[0]):
        upper = diffusivity_of(before[:, span(c)], values, inside_before)
        lower = diffusivity_of(after[:, span(c)], values, inside_after)
        store_weights(keep, mix, c, slice(0, EDGE), upper[ROWS - EDGE:])
        store_weights(keep, mix, c, slice(EDGE, EDGE + ROWS), diffusivity_of(here[:, span(c)], values))
        store_weights(keep, mix, c, slice(EDGE + ROWS, 2 * EDGE + ROWS), lower[:EDGE])


def make_plan(places, top, per_device, owned, members, capacity, position, level_steps, values, class_map, rows):
    cells = class_map.shape[1]
    tiles = cells // LANES
    row_tiles = class_map.shape[0] // rows
    weights = jax.ShapeDtypeStruct((tiles, 2 * EDGE + rows, LANES), F32)
    weight_spec = pl.BlockSpec(weights.shape, lambda i, *refs: (0, 0, 0))

    def rows_at(shift):
        return pl.BlockSpec((rows, cells), lambda i, position, *refs: (jnp.clip(position[1] + shift, 0, row_tiles - 1), 0))

    return pl.pallas_call(
        functools.partial(plan_kernel, places, top, per_device, owned, members, capacity),
        out_shape=(jax.ShapeDtypeStruct((places.size,), I32), weights, weights),
        grid_spec=pltpu.PrefetchScalarGridSpec(
            num_scalar_prefetch=3,
            grid=(1,),
            in_specs=[rows_at(-1), rows_at(0), rows_at(1)],
            out_specs=[SMEM_SPEC, weight_spec, weight_spec],
            scratch_shapes=[pltpu.SMEM((BINS,), I32), pltpu.SMEM((top + 1,), I32)],
        ),
        compiler_params=pltpu.CompilerParams(vmem_limit_bytes=VMEM_BYTES),
        cost_estimate=cost(0, 4 * weights.size * 2),
        name="plan",
    )(position, level_steps, values, class_map, class_map, class_map)


def owner_of(me, chips, d, other):
    return lax.rem(me // 2 - d + chips, chips) * 2 + lax.rem(me + other, 2)


def product_of(pert, grad, member, level, c):
    total = None
    for v in range(grad.shape[1]):
        term = pert[member, level, v, :, span(c)].astype(F32) * grad[level, v, :, span(c)].astype(F32)
        total = term if total is None else total + term
    return total.astype(BF16)


def pack_kernel(places, chips, d, plan, pert, near, far, tops, bottoms, top_rows, bottom_rows, offset):
    members, block = pert.shape[:2]
    capacity = tops.shape[0]
    at = pl.program_id(0)
    half = pl.num_programs(0) // 2
    owned = half * block

    @pl.when(at == 0)
    def _():
        offset[0] = 0

    def pack(grad, other, i):
        first = owner_of(plan[places.ME], chips, d, other) * owned + i * block
        for j in range(block):
            count = plan[places.steps + first + j]
            for m in range(members):
                off = jnp.minimum(offset[0], capacity)
                for c in range(top_rows.shape[0]):
                    part = product_of(pert, grad, m, j, c).astype(F32)
                    top_rows[c, pl.ds(off, ROWS), :] = part
                    bottom_rows[c, pl.ds(capacity - off, ROWS), :] = part
                offset[0] = off + count

    @pl.when(at < half)
    def _():
        pack(near, 0, at)

    @pl.when(at >= half)
    def _():
        pack(far, 1, at - half)

    @pl.when(at == 2 * half - 1)
    def _():
        for c in range(top_rows.shape[0]):
            tops[:, span(c)] = top_rows[c, :capacity, :].astype(BF16)
            bottoms[:, span(c)] = bottom_rows[c, ROWS:, :].astype(BF16)


def pack_halos(places, chips, d, plan, pert, near, far, block, capacity):
    members, _, variables, rows, cells = pert.shape
    blocks = near.shape[0] // block
    out = jax.ShapeDtypeStruct((capacity, cells), BF16)
    whole = pl.BlockSpec((capacity, cells), lambda i, plan: (0, 0))
    grad_block = (block, variables, rows, cells)

    def pert_place(i, plan):
        other = i // blocks
        return (0, owner_of(plan[places.ME], chips, d, other) * blocks + lax.rem(i, blocks), 0, 0, 0)

    return pl.pallas_call(
        functools.partial(pack_kernel, places, chips, d),
        out_shape=(out, out),
        grid_spec=pltpu.PrefetchScalarGridSpec(
            num_scalar_prefetch=1,
            grid=(2 * blocks,),
            in_specs=[
                pl.BlockSpec((members,) + grad_block, pert_place),
                pl.BlockSpec(grad_block, lambda i, plan: (jnp.minimum(i, blocks - 1), 0, 0, 0)),
                pl.BlockSpec(grad_block, lambda i, plan: (jnp.maximum(i - blocks, 0), 0, 0, 0)),
            ],
            out_specs=[whole, whole],
            scratch_shapes=[
                pltpu.VMEM((cells // LANES, capacity + ROWS, LANES), F32),
                pltpu.VMEM((cells // LANES, capacity + ROWS, LANES), F32),
                pltpu.SMEM((1,), I32),
            ],
        ),
        compiler_params=pltpu.CompilerParams(vmem_limit_bytes=VMEM_BYTES),
        cost_estimate=cost(8 * near.size, 2 * near.size * 2 * (members + 1)),
    )(plan, pert, near, far)


def deep_product_kernel(places, chips, per_device, group, plan, *refs):
    perts, grads, out = refs[:group], refs[group:-1], refs[-1]
    members = perts[0].shape[0]
    count = len(grads) // group

    for u in range(group):
        k = pl.program_id(0) * group + u
        pert = perts[u]
        place = grad_place(places, chips, count, plan, k)[0]

        def form(grad):
            for m in range(members):
                spot = deep_place(k * members + m, out.shape[0], per_device)
                for c in range(pert.shape[-1] // LANES):
                    out[spot, :, span(c)] = product_of(pert, grad, m, 0, c)

        for g in range(count):
            pl.when(place == g)(functools.partial(form, grads[u * count + g]))


def grad_place(places, chips, count, plan, k):
    levels = places.ranks - places.steps
    owned = levels // count
    level = plan[places.deep + k]
    owner = level // owned
    shift = lax.rem(plan[places.ME] // 2 - owner // 2 + chips, chips)
    return 2 * shift + lax.rem(plan[places.ME] + owner, 2), lax.rem(level, owned)


def deep_products(places, chips, plan, pert, grads, top, per_device):
    members, _, variables, rows, cells = pert.shape
    group = 4 if top % 4 == 0 else 1

    def pert_spec(u):
        return pl.BlockSpec((members, 1, variables, rows, cells), lambda i, plan: (0, plan[places.deep + i * group + u], 0, 0, 0))

    def grad_spec(u, g):
        def where(i, plan):
            place, level = grad_place(places, chips, len(grads), plan, i * group + u)
            return (jnp.where(place == g, level, 0), 0, 0, 0)

        return pl.BlockSpec((1, variables, rows, cells), where)

    return pl.pallas_call(
        functools.partial(deep_product_kernel, places, chips, per_device, group),
        out_shape=jax.ShapeDtypeStruct((top * members, rows, cells), BF16),
        grid_spec=pltpu.PrefetchScalarGridSpec(
            num_scalar_prefetch=1,
            grid=(top // group,),
            in_specs=[pert_spec(u) for u in range(group)] + [grad_spec(u, g) for u in range(group) for g in range(len(grads))],
            out_specs=pl.BlockSpec((top * members, rows, cells), lambda i, plan: (0, 0, 0)),
        ),
        compiler_params=pltpu.CompilerParams(vmem_limit_bytes=VMEM_BYTES),
        cost_estimate=cost(top * members * rows * cells * 4, top * members * rows * cells * 8),
        name="deep_product",
    )(plan, *([pert] * group), *(list(grads) * group))


def deep_kernel(mine, plan, values, planes, class_map, out, field, keep, mix):
    at = pl.program_id(0)
    parts, _, rows, _ = planes.shape
    height = parts * rows
    tiles = field.shape[1]

    @pl.when(at == 0)
    def _():
        for c in range(tiles):
            field[0, c, :ROWS, :] = jnp.zeros((ROWS, LANES), F32)
            field[0, c, ROWS + height:, :] = jnp.zeros((ROWS, LANES), F32)
            store_weights(keep, mix, c, slice(0, height), diffusivity_of(class_map[:, span(c)], values))

    for p in range(parts):
        for c in range(tiles):
            field[0, c, ROWS + p * rows:ROWS + (p + 1) * rows, :] = planes[p, 0, :, span(c)].astype(F32)

    def step(i, carry):
        sweep(field, keep, mix, 0, ROWS, height)
        return carry

    lax.fori_loop(0, plan[mine + at], step, 0)
    for p in range(parts):
        for c in range(tiles):
            out[p, 0, :, span(c)] = field[0, c, ROWS + p * rows:ROWS + (p + 1) * rows, :].astype(BF16)


def deep_smooth(places, plan, planes, class_map, values):
    parts, per_device, rows, cells = planes.shape
    tiles = cells // LANES
    plane = pl.BlockSpec((parts, 1, rows, cells), lambda i: (0, i, 0, 0))
    return pl.pallas_call(
        functools.partial(deep_kernel, places.mine),
        out_shape=jax.ShapeDtypeStruct(planes.shape, BF16),
        grid=(per_device,),
        in_specs=[SMEM_SPEC, SMEM_SPEC, plane, VMEM_SPEC],
        out_specs=plane,
        scratch_shapes=[
            pltpu.VMEM((1, tiles, parts * rows + 2 * ROWS, LANES), F32),
            pltpu.VMEM((tiles, parts * rows, LANES), F32),
            pltpu.VMEM((tiles, parts * rows, LANES), F32),
        ],
        compiler_params=pltpu.CompilerParams(vmem_limit_bytes=VMEM_BYTES),
        cost_estimate=cost(150 * planes.size, planes.size * 4 + parts * rows * cells * 4),
        name="deep_smooth",
    )(plan, values, planes, class_map)


def deep_place(q, planes, per_device):
    devices = planes // per_device
    return lax.rem(q, devices) * per_device + q // devices


def smooth_kernel(places, chips, d, other, low, owned, top, per_device, with_deep, with_part, with_variance, plan, pert, grad, below, above, keep, mix, *rest):
    extra, (out, below_rows, above_rows, field, offset) = rest[:-5], rest[-5:]
    if with_deep:
        deep, extra = extra[0], extra[1:]
    members, block = pert.shape[:2]
    capacity = below.shape[0]
    tiles = field.shape[1]
    at = pl.program_id(0)
    first = owner_of(plan[places.ME], chips, d, other) * owned + low + at * block

    @pl.when(at == 0)
    def _():
        start = jnp.int32(0)
        for owner, count in ([(0, owned)] if other else []) + [(other, low)]:
            ahead = owner_of(plan[places.ME], chips, d, owner) * owned

            def add(j, total):
                return total + plan[places.steps + ahead + j]

            start = lax.fori_loop(0, count, add, start)
        offset[0] = members * start
        for c in range(tiles):
            below_rows[c, :capacity, :] = below[:, span(c)].astype(F32)
            below_rows[c, capacity:, :] = jnp.zeros((ROWS, LANES), F32)
            above_rows[c, ROWS:, :] = above[:, span(c)].astype(F32)
            above_rows[c, :ROWS, :] = jnp.zeros((ROWS, LANES), F32)

    def emit(j, c, values):
        smooth = [value.astype(BF16).astype(F32) for value in values]
        for v in range(out.shape[1]):
            total = None
            for m in range(members):
                term = pert[m, j, v, :, span(c)].astype(F32) * smooth[m]
                total = term if total is None else total + term
            if with_part:
                total = total + extra[0][j, v, :, span(c)].astype(F32)
            if with_variance:
                total = total + extra[0][j, v, :, span(c)] * grad[j, v, :, span(c)].astype(F32)
            out[j, v, :, span(c)] = total.astype(out.dtype)

    def one_level(j, carry):
        level = first + j
        count = plan[places.steps + level]
        rank = plan[places.ranks + level]

        @pl.when(rank >= top)
        def _():
            for m in range(members):
                off = jnp.minimum(offset[0], capacity)
                for c in range(tiles):
                    field[m, c, :ROWS, :] = above_rows[c, pl.ds(capacity - off, ROWS), :]
                    field[m, c, ROWS:2 * ROWS, :] = product_of(pert, grad, m, j, c).astype(F32)
                    field[m, c, 2 * ROWS:, :] = below_rows[c, pl.ds(off, ROWS), :]
                offset[0] = off + count

            def step(i, carry):
                for m in range(members):
                    sweep(field, keep, mix, m, ROWS - EDGE, ROWS + 2 * EDGE)
                return carry

            lax.fori_loop(1, count, step, 0)
            last = [diffuse_columns(field, keep, mix, m, ROWS, ROWS, EDGE) for m in range(members)]
            for c, values in enumerate(zip(*last)):
                emit(j, c, values)

        @pl.when(rank < top)
        def _():
            for c in range(tiles):
                if with_deep:
                    spots = [deep_place(rank * members + m, deep.shape[0], per_device) for m in range(members)]
                    emit(j, c, [deep[spot, :, span(c)] for spot in spots])
                else:
                    emit(j, c, [jnp.zeros((ROWS, LANES), F32)] * members)

        return carry

    lax.fori_loop(0, block, one_level, 0)


def smooth_owner(places, chips, d, other, low, count, top, per_device, plan, pert, grad, halos, keep, mix, deep, part, variance, block, dtype):
    members, _, variables, rows, cells = pert.shape
    tiles = cells // LANES
    capacity = halos[0].shape[0]
    owned = grad.shape[0]
    wholes = [halos[0], halos[1], keep, mix] + ([] if deep is None else [deep])
    extra = [x for x in (part, variance) if x is not None]
    kernel = functools.partial(
        smooth_kernel, places, chips, d, other, low, owned, top, per_device, deep is not None, part is not None, variance is not None
    )

    def whole(x):
        return pl.BlockSpec(x.shape, lambda i, *refs: (0,) * x.ndim)

    def pert_place(i, plan):
        return (0, owner_of(plan[places.ME], chips, d, other) * (owned // block) + low // block + i, 0, 0, 0)

    def levels_from(start):
        return pl.BlockSpec((block, variables, rows, cells), lambda i, *refs: (start // block + i, 0, 0, 0))

    return pl.pallas_call(
        kernel,
        out_shape=jax.ShapeDtypeStruct((count,) + grad.shape[1:], dtype),
        grid_spec=pltpu.PrefetchScalarGridSpec(
            num_scalar_prefetch=1,
            grid=(count // block,),
            in_specs=[pl.BlockSpec((members, block, variables, rows, cells), pert_place), levels_from(low)]
            + [whole(x) for x in wholes]
            + [levels_from(0) for x in extra],
            out_specs=levels_from(0),
            scratch_shapes=[
                pltpu.VMEM((tiles, capacity + ROWS, LANES), F32),
                pltpu.VMEM((tiles, capacity + ROWS, LANES), F32),
                pltpu.VMEM((members, tiles, 3 * ROWS, LANES), F32),
                pltpu.SMEM((1,), I32),
            ],
        ),
        compiler_params=pltpu.CompilerParams(vmem_limit_bytes=VMEM_BYTES),
        cost_estimate=cost(100 * grad.size, grad.size * 2 * (members + 3)),
    )(plan, pert, grad, *wholes, *extra)


def final_kernel(places, top, per_device, owned, parts, plan, pert, near, part, deep, *rest):
    arrived, out = rest[:-1], rest[-1]
    members, block = pert.shape[:2]
    at = pl.program_id(0)
    steps = pl.num_programs(0)
    first = plan[places.ME] * owned + at * block

    def total_of(j, v, c):
        total = near[j, v, :, span(c)] + part[j, v, :, span(c)].astype(F32)
        for d in range(0, len(arrived), parts):
            value = arrived[d][j, v, :, span(c)]
            for p in range(1, parts):
                value = jnp.where(at >= p * steps // parts, arrived[d + p][j, v, :, span(c)], value)
            total = total + value.astype(F32)
        return total

    for j in range(block):
        rank = plan[places.ranks + first + j]
        for v in range(out.shape[1]):
            for c in range(out.shape[3] // LANES):
                out[j, v, :, span(c)] = total_of(j, v, c)

        @pl.when(rank < top)
        def _():
            for c in range(out.shape[3] // LANES):
                smooth = [deep[deep_place(rank * members + m, deep.shape[0], per_device), :, span(c)].astype(F32) for m in range(members)]
                for v in range(out.shape[1]):
                    total = out[j, v, :, span(c)]
                    for m in range(members):
                        total = total + pert[m, j, v, :, span(c)].astype(F32) * smooth[m]
                    out[j, v, :, span(c)] = total


def final_sum(places, top, per_device, parts, plan, pert, near, part, deep, arrived, block):
    members, _, variables, rows, cells = pert.shape
    owned = near.shape[0]
    steps = owned // block

    def levels_at(p):
        def where(i, plan):
            return (jnp.clip(i - p * steps // parts, 0, steps // parts - 1), 0, 0, 0)

        return pl.BlockSpec((block, variables, rows, cells), where)

    here = pl.BlockSpec((block, variables, rows, cells), lambda i, plan: (i, 0, 0, 0))
    return pl.pallas_call(
        functools.partial(final_kernel, places, top, per_device, owned, parts),
        out_shape=jax.ShapeDtypeStruct(near.shape, F32),
        grid_spec=pltpu.PrefetchScalarGridSpec(
            num_scalar_prefetch=1,
            grid=(steps,),
            in_specs=[
                pl.BlockSpec((members, block, variables, rows, cells), lambda i, plan: (0, plan[places.ME] * steps + i, 0, 0, 0)),
                here, here, pl.BlockSpec(deep.shape, lambda i, plan: (0, 0, 0)),
            ] + [levels_at(i % parts) for i in range(len(arrived))],
            out_specs=here,
        ),
        compiler_params=pltpu.CompilerParams(vmem_limit_bytes=VMEM_BYTES),
        cost_estimate=cost(4 * near.size, near.size * 12),
        name="final_sum",
    )(plan, pert, near, part, deep, *arrived)


def program(pert, gradient, variance, class_map, values, level_steps, top, capacity):
    members, levels, _, rows, cells = pert.shape
    mem_count = lax.axis_size("mem")
    tile_count = lax.axis_size("tile")
    owned = gradient.shape[0]
    block, smooth_block, parts = 4, 2, PARTS
    chips = mem_count // 2
    per_device = top * members // tile_count
    places = Plan(levels, top, per_device)

    def hop(value, d):
        return lax.ppermute(value, "mem", [(i, ((i // 2 + d) % chips) * 2 + i % 2) for i in range(mem_count)])

    def swap(value):
        return lax.ppermute(value, "mem", [(i, i ^ 1) for i in range(mem_count)])

    south = [(i + 1, i) for i in range(tile_count - 1)]
    north = [(i, i + 1) for i in range(tile_count - 1)]

    far = []
    for d in range(1, chips):
        far.append(hop(gradient, d))
    position = jnp.stack([lax.axis_index("mem"), lax.axis_index("tile"), jnp.int32(tile_count)])
    plan, keep, mix = make_plan(places, top, per_device, owned, members, capacity, position, level_steps, values, class_map, rows)
    grads, halos = [], []
    for d in range(chips):
        near = gradient if d == 0 else far[d - 1]
        other = swap(near)
        grads += [near, other]
        if top < levels:
            tops, bottoms = pack_halos(places, chips, d, plan, pert, near, other, block, capacity)
            below = lax.ppermute(tops, "tile", south)
            above = lax.ppermute(bottoms, "tile", north)
            halos.append((below, above))
        else:
            halos.append((jnp.zeros((16, cells), BF16),) * 2)

    deep = deep_products(places, chips, plan, pert, grads, top, per_device)
    deep = deep.reshape(tile_count, per_device, rows, cells)
    field = lax.all_to_all(deep, "tile", split_axis=0, concat_axis=0, tiled=True)
    field = deep_smooth(places, plan, field, class_map, values)
    deep = lax.all_to_all(field, "tile", split_axis=0, concat_axis=0, tiled=True).reshape(-1, rows, cells)

    def smooth(d, other, low, count, whole, part, var, dtype):
        return smooth_owner(
            places, chips, d, other, low, count, top, per_device, plan, pert, grads[2 * d + other], halos[d], keep, mix,
            whole, part, var, smooth_block, dtype
        )

    near_sum = smooth(0, 0, 0, owned, None, None, variance, F32)
    arrived = []
    size = owned // parts
    for d in range(1, chips):
        crossed = []
        for p in range(parts):
            other = smooth(d, 1, p * size, size, deep, None, None, BF16)
            crossed.append(swap(other))
        for p in range(parts):
            both = smooth(d, 0, p * size, size, deep, crossed[p], None, BF16)
            arrived.append(hop(both, chips - d))
    part = smooth(0, 1, 0, owned, deep, None, None, BF16)
    part = swap(part)

    return plan, near_sum, part, deep, arrived


def finish(places, top, per_device, pert, sums):
    plan, near, part, deep, arrived = sums
    return final_sum(places, top, per_device, PARTS, plan, pert, near, part, deep, arrived, 2)


def shards(perturbations, gradient, static_variance, level_steps, class_map, class_diffusivity):
    members, levels = perturbations.shape[:2]
    owned = gradient.shape[0]
    top = lax.axis_size("tile") // members
    capacity = (5 * members * owned + 15) // 16 * 16
    operands = (perturbations, gradient, static_variance, class_map, class_diffusivity, level_steps)
    tiles = lax.axis_size("tile")
    sums = program(*operands, top, capacity)

    def halo(sums, *operands):
        return finish(Plan(levels, top, top * members // tiles), top, top * members // tiles, operands[0], sums)

    def general(sums, *operands):
        per_device = levels * members // tiles
        return finish(Plan(levels, levels, per_device), levels, per_device, operands[0], program(*operands, levels, 16))

    return lax.cond(sums[0][Plan.FITS] > 0, halo, general, sums, *operands)


def solution(mesh):
    placed = (
        P("mem", None, None, "tile", None),
        P("mem", None, "tile", None),
        P("mem", None, "tile", None),
        P(),
        P(),
        P(),
    )
    return jax.shard_map(
        shards, mesh=mesh, in_specs=placed, out_specs=P("mem", None, "tile", None), check_vma=False
    )
```

time: 178 us -> 151 us (0.85)
  waiting for transfers between devices: 78.4 us -> 41.1 us
  blocking collectives: 0 us -> 18.9 us
  Pallas kernels: 58.6 us -> 65.4 us
  local copies, waits for them, and re-layouts: 7.49 us -> 1.25 us
  other arithmetic: 5.78 us -> 0.61 us
  starting transfers between devices: 25.3 us -> 22 us
    all_to_all x0 -> x1, blocking collectives: none -> 18.9 us  [program(): lax.all_to_all(deep, 'tile', split_axis=0, concat_axis=0, tiled=True)]
    ppermute x2, waiting for transfers between devices: 16.4 us -> 0.01 us  [program(): below = lax.ppermute(tops, 'tile', south)]
    all_to_all x1 -> x0, waiting for transfers between devices: 10.8 us -> none  [program(): lax.all_to_all(deep, 'tile', split_axis=0, concat_axis=0, tiled=True)]
    ppermute x2 -> x3, waiting for transfers between devices: 29.8 us -> 22.8 us  [hop(): lax.ppermute(value, 'mem', [(i, (i // 2 + d) % chips * 2 + i % 2) for i i...]
    pallas_call x9 -> x12, Pallas kernels: 58.6 us -> 65.4 us  [the longest x6 36.1 us: smooth_owner(): pl.pallas_call(kernel, out_shape=jax.ShapeDtypeStruct((count,) + grad.sha...]
    all_to_all x1 -> x0, starting transfers between devices: 6.1 us -> none  [program(): lax.all_to_all(deep, 'tile', split_axis=0, concat_axis=0, tiled=True)]
    unnamed x30 -> x0, local copies, waits for them, and re-layouts: 3.66 us -> none
    ppermute x2, waiting for transfers between devices: 21.4 us -> 18.3 us  [program(): above = lax.ppermute(bottoms, 'tile', north)]
  transfers between devices with their start and end apart: 12 -> 13, of which waited for: 7 -> 3; matrix products, arithmetic and copies ran while one was open for 5% -> 1% of each run, Pallas kernels for 19% -> 33%
where the time goes in v2:
time: 151 us; the launch traced here: 150 us
  Pallas kernels  65.4 us (43%)
  waiting for transfers between devices  41.1 us (27%)
  starting transfers between devices  22 us (15%)
  blocking collectives  18.9 us (13%)
    pallas_call x6, Pallas kernels, smooth_owner(): pl.pallas_call(kernel, out_shape=jax.ShapeDtypeStruct((count,) + grad.sha...  36.1 us
    ppermute x3, waiting for transfers between devices, hop(): lax.ppermute(value, 'mem', [(i, (i // 2 + d) % chips * 2 + i % 2) for i i...  22.8 us
    all_to_all x1, blocking collectives, program(): lax.all_to_all(deep, 'tile', split_axis=0, concat_axis=0, tiled=True)  18.9 us
    ppermute x2, waiting for transfers between devices, program(): above = lax.ppermute(bottoms, 'tile', north)  18.3 us
    pallas_call x2, Pallas kernels, pack_halos(): pl.pallas_call(functools.partial(pack_kernel, places, chips, d), out_shap...  10.9 us
    ppermute x2, starting transfers between devices, program(): above = lax.ppermute(bottoms, 'tile', north)  10 us
    pallas_call x1, Pallas kernels, deep_smooth(): pl.pallas_call(functools.partial(deep_kernel, places.mine), out_shape=jax...  7.33 us
    pallas_call x1, Pallas kernels, final_sum(): pl.pallas_call(functools.partial(final_kernel, places, top, per_device, o...  5.12 us
  transfers between devices with their start and end apart: 13, of which 3 were waited for; matrix products, arithmetic and copies ran while one was open for 1% of the time, Pallas kernels for 33%

profile of v2, /device:TPU:0, one launch (start us, length us, event | category | flops | bytes accessed | tf_op | source)
XLA Modules:
  0.0 150.0 jit_solution(2847078973429896182)
XLA Ops:
  0.0 3.0 %collective-permute-start.11 = (bf16[8,2,8,3072]{3,2,1,0:T(8,128)(2,1)}, bf16[8,2,8,3072]{3,2,1,0:T(8,128)(2,1)}, u32[]{:S(2)}, u32[]{:S(2)}) collective-permute-start(bf16[8,2,8,3072]{3,2,1,0:T(8,128)(2,1)} %refs_16_.1), channel_id=1, source_target_pairs={{0,16},{8,24},{16,0},{24,8},{1,17},{9,25},{17,1},{25,9},{2,18},{10... | collective-permute-start | bytes 2359304 | tf_op jit(solution)/shard_map/ppermute | solution.py:564
  3.0 17.9 %collective-permute-done.11.refs_6_.refs_10_.refs_14_.refs_18_.near.grad = bf16[8,2,8,3072]{3,2,1,0:T(8,128)(2,1)} collective-permute-done((bf16[8,2,8,3072]{3,2,1,0:T(8,128)(2,1)}, bf16[8,2,8,3072]{3,2,1,0:T(8,128)(2,1)}, u32[]{:S(2)}, u32[]{:S(2)}) %collective-permute-start.11) | collective-permute-done | bytes 786464 | tf_op jit(solution)/shard_map/ppermute | solution.py:564
  20.8 0.0 collective-permute-start.12
  20.8 0.6 pad_add_fusion.1.position
  21.4 2.6 %plan.3 = (s32[78]{0:T(128)}, f32[24,16,128]{2,1,0:T(8,128)}, f32[24,16,128]{2,1,0:T(8,128)}) custom-call(s32[3]{0:T(128)} %pad_add_fusion.1.position, s32[32]{0:T(128)} %level_steps.1, f32[4]{0:T(128)} %values.3, s32[64,3072]{1,0:T(8,128)} %class_map.1, s32[64,3072]{1,0:T(8,128)} %class_map.1, s32[64,3072]{1,0:T(8,128)} %class_map.1), custom_call_target="tpu_custom_call" | custom-call | bytes 393216 | tf_op jit(solution)/shard_map/plan/pallas_call | solution.py:158
  24.0 0.0 collective-permute-done.12.refs_7_.refs_11_.refs_15_.refs_19_.far.grad
  24.0 3.5 %deep_product.3 = bf16[8,8,3072]{2,1,0:T(8,128)(2,1)} custom-call(s32[78]{0:T(128)} %get-tuple-element.57.plan, bf16[2,32,2,8,3072]{4,3,2,1,0:T(8,128)(2,1)} %pert.15, bf16[2,32,2,8,3072]{4,3,2,1,0:T(8,128)(2,1)} %pert.15, bf16[2,32,2,8,3072]{4,3,2,1,0:T(8,128)(2,1)} %pert.15, bf16[2,32,2,8,3072]{4,3,2,1,0:T(8,128)(2,1)} %pert.15, ...), custom_call_target="tpu_custom_call" | custom-call | flops 786432 | bytes 1572864 | tf_op jit(solution)/shard_map/deep_product/pallas_call | solution.py:301
  27.5 18.9 %all_to_all.20.planes = bf16[8,1,8,3072]{3,2,1,0:T(8,128)(2,1)} all-to-all(bf16[8,1,8,3072]{3,2,1,0:T(8,128)(2,1)} %bitcast.16), channel_id=1, replica_groups=mesh['mem'=4,'tile'=8] {'tile'}, dimensions={0} | all-to-all | bytes 786432 | tf_op jit(solution)/shard_map/all_to_all | solution.py:592
  46.4 7.3 %deep_smooth.3 = bf16[8,1,8,3072]{3,2,1,0:T(8,128)(2,1)} custom-call(s32[78]{0:T(128)} %get-tuple-element.57.plan, f32[4]{0:T(128)} %values.3, bf16[8,1,8,3072]{3,2,1,0:T(8,128)(2,1)} %all_to_all.20.planes, s32[64,3072]{1,0:T(8,128)} %class_map.1), custom_call_target="tpu_custom_call" | custom-call | flops 29491200 | bytes 1572864 | tf_op jit(solution)/shard_map/deep_smooth/pallas_call | solution.py:347
  53.8 4.1 %all-to-all-start.3 = ((bf16[8,1,8,3072]{3,2,1,0:T(8,128)(2,1)}), bf16[8,1,8,3072]{3,2,1,0:T(8,128)(2,1)}, u32[]{:S(2)}, u32[]{:S(2)}) async-start(bf16[8,1,8,3072]{3,2,1,0:T(8,128)(2,1)} %deep_smooth.3), calls=%async_computation.3 | async-start | bytes 786432 | tf_op jit(solution)/shard_map/all_to_all | solution.py:594
  57.8 5.4 %shard_map.69 = (bf16[80,3072]{1,0:T(8,128)(2,1)}, bf16[80,3072]{1,0:T(8,128)(2,1)}) custom-call(s32[78]{0:T(128)} %get-tuple-element.57.plan, bf16[2,32,2,8,3072]{4,3,2,1,0:T(8,128)(2,1)} %pert.15, bf16[8,2,8,3072]{3,2,1,0:T(8,128)(2,1)} %collective-permute-done.11.refs_6_.refs_10_.refs_14_.refs_18_.near.grad, ...), custom_call_target="tpu_custom_call" | custom-call | flops 3145728 | bytes 4718592 | tf_op jit(solution)/shard_map/pallas_call | solution.py:235
  63.3 1.3 collective-permute-start.14
  64.6 5.4 %collective-permute-start.15 = (bf16[80,3072]{1,0:T(8,128)(2,1)}, bf16[80,3072]{1,0:T(8,128)(2,1)}, u32[]{:S(2)}, u32[]{:S(2)}) collective-permute-start(bf16[80,3072]{1,0:T(8,128)(2,1)} %get-tuple-element.63), channel_id=1, source_target_pairs={{0,1},{1,2},{2,3},{3,4},{4,5},{5,6},{6,7},{8,9},{9,10},{10,11},{11... | collective-permute-start | bytes 1474568 | tf_op jit(solution)/shard_map/ppermute | solution.py:585
  69.9 5.4 %shard_map.66 = (bf16[80,3072]{1,0:T(8,128)(2,1)}, bf16[80,3072]{1,0:T(8,128)(2,1)}) custom-call(s32[78]{0:T(128)} %get-tuple-element.57.plan, bf16[2,32,2,8,3072]{4,3,2,1,0:T(8,128)(2,1)} %pert.15, bf16[8,2,8,3072]{3,2,1,0:T(8,128)(2,1)} %refs_16_.1, bf16[8,2,8,3072]{3,2,1,0:T(8,128)(2,1)} %collective-permute-done.8.far.refs_5_.refs_9_.refs_13_.refs_17_.grad), custom_call_target="tpu_custom_call" | custom-call | flops 3145728 | bytes 4718592 | tf_op jit(solution)/shard_map/pallas_call | solution.py:235
  75.4 4.7 %collective-permute-start.10 = (bf16[80,3072]{1,0:T(8,128)(2,1)}, bf16[80,3072]{1,0:T(8,128)(2,1)}, u32[]{:S(2)}, u32[]{:S(2)}) collective-permute-start(bf16[80,3072]{1,0:T(8,128)(2,1)} %get-tuple-element.59), channel_id=1, source_target_pairs={{0,1},{1,2},{2,3},{3,4},{4,5},{5,6},{6,7},{8,9},{9,10},{10,11},{11... | collective-permute-start | bytes 1474568 | tf_op jit(solution)/shard_map/ppermute | solution.py:585
  80.1 1.3 collective-permute-start.9
  81.4 0.0 collective-permute-done.14.below
  81.4 18.3 %collective-permute-done.15.above = bf16[80,3072]{1,0:T(8,128)(2,1)} collective-permute-done((bf16[80,3072]{1,0:T(8,128)(2,1)}, bf16[80,3072]{1,0:T(8,128)(2,1)}, u32[]{:S(2)}, u32[]{:S(2)}) %collective-permute-start.15) | collective-permute-done | bytes 491552 | tf_op jit(solution)/shard_map/ppermute | solution.py:585
  99.6 5.5 %shard_map.72 = bf16[4,2,8,3072]{3,2,1,0:T(8,128)(2,1)} custom-call(s32[78]{0:T(128)} %get-tuple-element.57.plan, bf16[2,32,2,8,3072]{4,3,2,1,0:T(8,128)(2,1)} %pert.15, bf16[8,2,8,3072]{3,2,1,0:T(8,128)(2,1)} %collective-permute-done.12.refs_7_.refs_11_.refs_15_.refs_19_.far.grad, bf16[80,3072]{1,0:T(8,128)(2,1)} %collective-permute-done.14.below, ...), custom_call_target="tpu_custom_call" | custom-call | flops 39321600 | bytes 3932160 | tf_op jit(solution)/shard_map/pallas_call | solution.py:468
  105.1 0.0 collective-permute-start.18
  105.1 4.6 %shard_map.70 = bf16[4,2,8,3072]{3,2,1,0:T(8,128)(2,1)} custom-call(s32[78]{0:T(128)} %get-tuple-element.57.plan, bf16[2,32,2,8,3072]{4,3,2,1,0:T(8,128)(2,1)} %pert.15, bf16[8,2,8,3072]{3,2,1,0:T(8,128)(2,1)} %collective-permute-done.12.refs_7_.refs_11_.refs_15_.refs_19_.far.grad, bf16[80,3072]{1,0:T(8,128)(2,1)} %collective-permute-done.14.below, ...), custom_call_target="tpu_custom_call" | custom-call | flops 39321600 | bytes 3932160 | tf_op jit(solution)/shard_map/pallas_call | solution.py:468
  109.8 1.1 collective-permute-start.16
  110.8 8.2 %shard_map.68 = bf16[8,2,8,3072]{3,2,1,0:T(8,128)(2,1)} custom-call(s32[78]{0:T(128)} %get-tuple-element.57.plan, bf16[2,32,2,8,3072]{4,3,2,1,0:T(8,128)(2,1)} %pert.15, bf16[8,2,8,3072]{3,2,1,0:T(8,128)(2,1)} %collective-permute-done.8.far.refs_5_.refs_9_.refs_13_.refs_17_.grad, bf16[80,3072]{1,0:T(8,128)(2,1)} %collective-permute-done.9.below, ...), custom_call_target="tpu_custom_call" | custom-call | flops 39321600 | bytes 3932160 | tf_op jit(solution)/shard_map/pallas_call | solution.py:468
  119.1 5.6 %shard_map.73 = bf16[4,2,8,3072]{3,2,1,0:T(8,128)(2,1)} custom-call(s32[78]{0:T(128)} %get-tuple-element.57.plan, bf16[2,32,2,8,3072]{4,3,2,1,0:T(8,128)(2,1)} %pert.15, bf16[8,2,8,3072]{3,2,1,0:T(8,128)(2,1)} %collective-permute-done.11.refs_6_.refs_10_.refs_14_.refs_18_.near.grad, bf16[80,3072]{1,0:T(8,128)(2,1)} %collective-permute-done.14.below, ...), custom_call_target="tpu_custom_call" | custom-call | flops 39321600 | bytes 3932160 | tf_op jit(solution)/shard_map/pallas_call | solution.py:468
  124.6 0.8 collective-permute-start.19
  125.4 5.3 %shard_map.71 = bf16[4,2,8,3072]{3,2,1,0:T(8,128)(2,1)} custom-call(s32[78]{0:T(128)} %get-tuple-element.57.plan, bf16[2,32,2,8,3072]{4,3,2,1,0:T(8,128)(2,1)} %pert.15, bf16[8,2,8,3072]{3,2,1,0:T(8,128)(2,1)} %collective-permute-done.11.refs_6_.refs_10_.refs_14_.refs_18_.near.grad, bf16[80,3072]{1,0:T(8,128)(2,1)} %collective-permute-done.14.below, ...), custom_call_target="tpu_custom_call" | custom-call | flops 39321600 | bytes 3932160 | tf_op jit(solution)/shard_map/pallas_call | solution.py:468
  130.7 0.5 collective-permute-start.17
  131.2 1.3 slice.3
  133.1 6.9 %shard_map.67 = f32[8,2,8,3072]{3,2,1,0:T(8,128)} custom-call(s32[78]{0:T(128)} %get-tuple-element.57.plan, bf16[2,32,2,8,3072]{4,3,2,1,0:T(8,128)(2,1)} %pert.15, bf16[8,2,8,3072]{3,2,1,0:T(8,128)(2,1)} %refs_16_.1, bf16[80,3072]{1,0:T(8,128)(2,1)} %collective-permute-done.9.below, bf16[80,3072]{1,0:T(8,128)(2,1)} %collective-permute-done.10.above, ...), custom_call_target="tpu_custom_call" | custom-call | flops 39321600 | bytes 3932160 | tf_op jit(solution)/shard_map/pallas_call | solution.py:468
  140.0 5.0 %collective-permute-done.17 = bf16[4,2,8,3072]{3,2,1,0:T(8,128)(2,1)} collective-permute-done((bf16[4,2,8,3072]{3,2,1,0:T(8,128)(2,1)}, bf16[4,2,8,3072]{3,2,1,0:T(8,128)(2,1)}, u32[]{:S(2)}, u32[]{:S(2)}) %collective-permute-start.17) | collective-permute-done | bytes 393248 | tf_op jit(solution)/shard_map/ppermute | solution.py:564
  144.9 5.1 %conditional.1 = (f32[8,2,8,3072]{3,2,1,0:T(8,128)}) conditional(s32[]{:T(128)} %bitcast.6, (s32[32]{0:T(128)}, f32[4]{0:T(128)}, s32[64,3072]{1,0:T(8,128)}, bf16[2,32,2,8,3072]{4,3,2,1,0:T(8,128)(2,1)}, bf16[8,2,8,3072]{3,2,1,0:T(8,128)(2,1)}, /*index=5*/f32[8,2,8,3072]{3,2,1,0:T(8,128)}) %tuple.11, (s32[78]{0:T(128)}, ...), branch_computations={%region_0.0_spmd, %region_1.0_spmd} | conditional | flops 479723520 | bytes 79921560 | solution.py:640
  144.9 5.1 %final_sum.3 = f32[8,2,8,3072]{3,2,1,0:T(8,128)} custom-call(s32[78]{0:T(128)} %get-tuple-element.43.plan, bf16[2,32,2,8,3072]{4,3,2,1,0:T(8,128)(2,1)} %get-tuple-element.44.pert, f32[8,2,8,3072]{3,2,1,0:T(8,128)} %get-tuple-element.45.near, bf16[8,2,8,3072]{3,2,1,0:T(8,128)(2,1)} %get-tuple-element.46.part, bf16[8,8,3072]{2,1,0:T(8,128)(2,1)} %get-tuple-element.47.deep, ...), custom_call_target="tpu_custom_call" | custom-call | flops 1572864 | bytes 4718592 | tf_op jit(solution)/shard_map/cond/branch_1_fun/final_sum/pallas_call | solution.py:535
  (10 shorter events, 0.0 us)
Async XLA Ops:
  0.0 20.8 %collective-permute-start.11 = (bf16[8,2,8,3072]{3,2,1,0:T(8,128)(2,1)}, bf16[8,2,8,3072]{3,2,1,0:T(8,128)(2,1)}, u32[]{:S(2)}, u32[]{:S(2)}) collective-permute-start(bf16[8,2,8,3072]{3,2,1,0:T(8,128)(2,1)} %refs_16_.1), channel_id=1, source_target_pairs={{0,16},{8,24},{16,0},{24,8},{1,17},{9,25},{17,1},{25,9},{2,18},{10... | collective-permute-start | bytes 2359304 | tf_op jit(solution)/shard_map/ppermute | solution.py:564
  3.0 21.0 %collective-permute-start.8 = (bf16[8,2,8,3072]{3,2,1,0:T(8,128)(2,1)}, bf16[8,2,8,3072]{3,2,1,0:T(8,128)(2,1)}, u32[]{:S(2)}, u32[]{:S(2)}) collective-permute-start(bf16[8,2,8,3072]{3,2,1,0:T(8,128)(2,1)} %refs_16_.1), channel_id=1, source_target_pairs={{0,8},{8,0},{16,24},{24,16},{1,9},{9,1},{17,25},{25,17},{2,10},{10... | collective-permute-start | bytes 2359304 | tf_op jit(solution)/shard_map/ppermute | solution.py:567
  20.8 3.2 %collective-permute-start.12 = (bf16[8,2,8,3072]{3,2,1,0:T(8,128)(2,1)}, bf16[8,2,8,3072]{3,2,1,0:T(8,128)(2,1)}, u32[]{:S(2)}, u32[]{:S(2)}) collective-permute-start(bf16[8,2,8,3072]{3,2,1,0:T(8,128)(2,1)} %collective-permute-done.11.refs_6_.refs_10_.refs_14_.refs_18_.near.grad), channel_id=1, source_target_pairs={{0,8},{8,0},{16,24},{24,16},{1,9},{9,1},{17,25},{25,17},{2,10},{10... | collective-permute-start | bytes 2359304 | tf_op jit(solution)/shard_map/ppermute | solution.py:567
  53.8 45.9 %all-to-all-start.3 = ((bf16[8,1,8,3072]{3,2,1,0:T(8,128)(2,1)}), bf16[8,1,8,3072]{3,2,1,0:T(8,128)(2,1)}, u32[]{:S(2)}, u32[]{:S(2)}) async-start(bf16[8,1,8,3072]{3,2,1,0:T(8,128)(2,1)} %deep_smooth.3), calls=%async_computation.3 | async-start | bytes 786432 | tf_op jit(solution)/shard_map/all_to_all | solution.py:594
  63.3 18.1 %collective-permute-start.14 = (bf16[80,3072]{1,0:T(8,128)(2,1)}, bf16[80,3072]{1,0:T(8,128)(2,1)}, u32[]{:S(2)}, u32[]{:S(2)}) collective-permute-start(bf16[80,3072]{1,0:T(8,128)(2,1)} %get-tuple-element.62), channel_id=1, source_target_pairs={{1,0},{2,1},{3,2},{4,3},{5,4},{6,5},{7,6},{9,8},{10,9},{11,10},{12... | collective-permute-start | bytes 1474568 | tf_op jit(solution)/shard_map/ppermute | solution.py:584
  64.6 35.0 %collective-permute-start.15 = (bf16[80,3072]{1,0:T(8,128)(2,1)}, bf16[80,3072]{1,0:T(8,128)(2,1)}, u32[]{:S(2)}, u32[]{:S(2)}) collective-permute-start(bf16[80,3072]{1,0:T(8,128)(2,1)} %get-tuple-element.63), channel_id=1, source_target_pairs={{0,1},{1,2},{2,3},{3,4},{4,5},{5,6},{6,7},{8,9},{9,10},{10,11},{11... | collective-permute-start | bytes 1474568 | tf_op jit(solution)/shard_map/ppermute | solution.py:585
  75.4 35.5 %collective-permute-start.10 = (bf16[80,3072]{1,0:T(8,128)(2,1)}, bf16[80,3072]{1,0:T(8,128)(2,1)}, u32[]{:S(2)}, u32[]{:S(2)}) collective-permute-start(bf16[80,3072]{1,0:T(8,128)(2,1)} %get-tuple-element.59), channel_id=1, source_target_pairs={{0,1},{1,2},{2,3},{3,4},{4,5},{5,6},{6,7},{8,9},{9,10},{10,11},{11... | collective-permute-start | bytes 1474568 | tf_op jit(solution)/shard_map/ppermute | solution.py:585
  80.1 30.8 %collective-permute-start.9 = (bf16[80,3072]{1,0:T(8,128)(2,1)}, bf16[80,3072]{1,0:T(8,128)(2,1)}, u32[]{:S(2)}, u32[]{:S(2)}) collective-permute-start(bf16[80,3072]{1,0:T(8,128)(2,1)} %get-tuple-element.58), channel_id=1, source_target_pairs={{1,0},{2,1},{3,2},{4,3},{5,4},{6,5},{7,6},{9,8},{10,9},{11,10},{12... | collective-permute-start | bytes 1474568 | tf_op jit(solution)/shard_map/ppermute | solution.py:584
  105.1 13.9 %collective-permute-start.18 = (bf16[4,2,8,3072]{3,2,1,0:T(8,128)(2,1)}, bf16[4,2,8,3072]{3,2,1,0:T(8,128)(2,1)}, u32[]{:S(2)}, u32[]{:S(2)}) collective-permute-start(bf16[4,2,8,3072]{3,2,1,0:T(8,128)(2,1)} %shard_map.72), channel_id=1, source_target_pairs={{0,8},{8,0},{16,24},{24,16},{1,9},{9,1},{17,25},{25,17},{2,10},{10... | collective-permute-start | bytes 1179656 | tf_op jit(solution)/shard_map/ppermute | solution.py:567
  109.8 15.7 %collective-permute-start.16 = (bf16[4,2,8,3072]{3,2,1,0:T(8,128)(2,1)}, bf16[4,2,8,3072]{3,2,1,0:T(8,128)(2,1)}, u32[]{:S(2)}, u32[]{:S(2)}) collective-permute-start(bf16[4,2,8,3072]{3,2,1,0:T(8,128)(2,1)} %shard_map.70), channel_id=1, source_target_pairs={{0,8},{8,0},{16,24},{24,16},{1,9},{9,1},{17,25},{25,17},{2,10},{10... | collective-permute-start | bytes 1179656 | tf_op jit(solution)/shard_map/ppermute | solution.py:567
  119.0 20.9 %collective-permute-start.13 = (bf16[8,2,8,3072]{3,2,1,0:T(8,128)(2,1)}, bf16[8,2,8,3072]{3,2,1,0:T(8,128)(2,1)}, u32[]{:S(2)}, u32[]{:S(2)}) collective-permute-start(bf16[8,2,8,3072]{3,2,1,0:T(8,128)(2,1)} %shard_map.68), channel_id=1, source_target_pairs={{0,8},{8,0},{16,24},{24,16},{1,9},{9,1},{17,25},{25,17},{2,10},{10... | collective-permute-start | bytes 2359304 | tf_op jit(solution)/shard_map/ppermute | solution.py:567
  124.6 15.3 %collective-permute-start.19 = (bf16[4,2,8,3072]{3,2,1,0:T(8,128)(2,1)}, bf16[4,2,8,3072]{3,2,1,0:T(8,128)(2,1)}, u32[]{:S(2)}, u32[]{:S(2)}) collective-permute-start(bf16[4,2,8,3072]{3,2,1,0:T(8,128)(2,1)} %shard_map.73), channel_id=1, source_target_pairs={{0,16},{8,24},{16,0},{24,8},{1,17},{9,25},{17,1},{25,9},{2,18},{10... | collective-permute-start | bytes 1179656 | tf_op jit(solution)/shard_map/ppermute | solution.py:564
  130.7 14.2 %collective-permute-start.17 = (bf16[4,2,8,3072]{3,2,1,0:T(8,128)(2,1)}, bf16[4,2,8,3072]{3,2,1,0:T(8,128)(2,1)}, u32[]{:S(2)}, u32[]{:S(2)}) collective-permute-start(bf16[4,2,8,3072]{3,2,1,0:T(8,128)(2,1)} %shard_map.71), channel_id=1, source_target_pairs={{0,16},{8,24},{16,0},{24,8},{1,17},{9,25},{17,1},{25,9},{2,18},{10... | collective-permute-start | bytes 1179656 | tf_op jit(solution)/shard_map/ppermute | solution.py:564

commit v3 on v2

--- a/solution.py
+++ b/solution.py
@@ -76,7 +76,7 @@
 
 
 class Plan:
-    ME, TILE, FITS = 0, 1, 2
+    ME, TILE = 0, 1
 
     def __init__(self, levels, top, per_device):
         self.steps = 8
@@ -89,12 +89,12 @@
 BINS = 16
 
 
-def plan_kernel(places, top, per_device, owned, members, capacity, position, level_steps, values, before, here, after, plan, keep, mix, bins, deep_steps):
+def plan_kernel(places, top, per_device, owned, members, capacities, level_steps, plan, fits, bins, deep_steps):
     levels = level_steps.shape[0]
-    me, tile, tile_count = position[0], position[1], position[2]
+    me, tile, tile_count = lax.axis_index("mem"), lax.axis_index("tile"), lax.axis_size("tile")
     plan[places.ME] = me
     plan[places.TILE] = tile
-    for i in range(3, 8):
+    for i in range(2, places.steps):
         plan[i] = 0
 
     def bin_of(level):
@@ -115,7 +115,7 @@
         total = total + here_count
 
     def assign(level, carry):
-        rows, most_rows, most_steps = carry
+        chip_rows, owner_rows, fits = carry
         b = bin_of(level)
         rank = bins[b]
         bins[b] = rank + 1
@@ -126,15 +126,32 @@
         slot = jnp.minimum(rank, top)
         plan[places.deep + slot] = level
         deep_steps[slot] = level_steps[level]
-        rows = jnp.where(lax.rem(level, 2 * owned) == 0, 0, rows) + members * steps
-        return rows, jnp.maximum(most_rows, rows), jnp.maximum(most_steps, steps)
-
-    _, most_rows, most_steps = lax.fori_loop(0, levels, assign, (jnp.int32(0), jnp.int32(0), jnp.int32(0)))
-    plan[places.FITS] = ((most_rows <= capacity) & (most_steps <= EDGE)).astype(I32)
+        chip_rows = jnp.where(lax.rem(level, 2 * owned) == 0, 0, chip_rows) + members * steps
+        owner_rows = jnp.where(lax.rem(level, owned) == 0, 0, owner_rows) + 2 * members * steps
+        inside = (chip_rows <= capacities[0]) & (owner_rows <= capacities[1]) & (steps <= EDGE)
+        return chip_rows, owner_rows, jnp.where(inside, fits, 0)
+
+    fits[0] = lax.fori_loop(0, levels, assign, (jnp.int32(0), jnp.int32(0), jnp.int32(1)))[2]
     plan[places.deep + top] = 0
     for j in range(per_device):
         plan[places.mine + j] = deep_steps[(j * tile_count + tile) // members]
 
+
+def make_plan(places, top, per_device, owned, members, capacities, level_steps):
+    return pl.pallas_call(
+        functools.partial(plan_kernel, places, top, per_device, owned, members, capacities),
+        out_shape=(jax.ShapeDtypeStruct((places.size,), I32), jax.ShapeDtypeStruct((1,), I32)),
+        in_specs=[SMEM_SPEC],
+        out_specs=[SMEM_SPEC, SMEM_SPEC],
+        scratch_shapes=[pltpu.SMEM((BINS,), I32), pltpu.SMEM((top + 1,), I32)],
+        compiler_params=pltpu.CompilerParams(vmem_limit_bytes=VMEM_BYTES),
+        cost_estimate=cost(0, 4 * places.size),
+        name="plan",
+    )(level_steps)
+
+
+def weights_kernel(places, tile_count, plan, values, before, here, after, keep, mix):
+    tile = plan[places.TILE]
     inside_before = jnp.broadcast_to(tile > 0, (ROWS, LANES))
     inside_after = jnp.broadcast_to(tile < tile_count - 1, (ROWS, LANES))
     for c in range(keep.shape[0]):
@@ -145,7 +162,7 @@
         store_weights(keep, mix, c, slice(EDGE + ROWS, 2 * EDGE + ROWS), lower[:EDGE])
 
 
-def make_plan(places, top, per_device, owned, members, capacity, position, level_steps, values, class_map, rows):
+def make_weights(places, plan, values, class_map, rows):
     cells = class_map.shape[1]
     tiles = cells // LANES
     row_tiles = class_map.shape[0] // rows
@@ -153,22 +170,21 @@
     weight_spec = pl.BlockSpec(weights.shape, lambda i, *refs: (0, 0, 0))
 
     def rows_at(shift):
-        return pl.BlockSpec((rows, cells), lambda i, position, *refs: (jnp.clip(position[1] + shift, 0, row_tiles - 1), 0))
+        return pl.BlockSpec((rows, cells), lambda i, plan, *refs: (jnp.clip(plan[places.TILE] + shift, 0, row_tiles - 1), 0))
 
     return pl.pallas_call(
-        functools.partial(plan_kernel, places, top, per_device, owned, members, capacity),
-        out_shape=(jax.ShapeDtypeStruct((places.size,), I32), weights, weights),
+        functools.partial(weights_kernel, places, row_tiles),
+        out_shape=(weights, weights),
         grid_spec=pltpu.PrefetchScalarGridSpec(
-            num_scalar_prefetch=3,
+            num_scalar_prefetch=2,
             grid=(1,),
             in_specs=[rows_at(-1), rows_at(0), rows_at(1)],
-            out_specs=[SMEM_SPEC, weight_spec, weight_spec],
-            scratch_shapes=[pltpu.SMEM((BINS,), I32), pltpu.SMEM((top + 1,), I32)],
+            out_specs=[weight_spec, weight_spec],
         ),
         compiler_params=pltpu.CompilerParams(vmem_limit_bytes=VMEM_BYTES),
         cost_estimate=cost(0, 4 * weights.size * 2),
-        name="plan",
-    )(position, level_steps, values, class_map, class_map, class_map)
+        name="weights",
+    )(plan, values, class_map, class_map, class_map)
 
 
 def owner_of(me, chips, d, other):
@@ -183,7 +199,7 @@
     return total.astype(BF16)
 
 
-def pack_kernel(places, chips, d, plan, pert, near, far, tops, bottoms, top_rows, bottom_rows, offset):
+def pack_owners_kernel(places, chips, d, plan, pert, near, far, tops, bottoms, top_rows, bottom_rows, offset):
     members, block = pert.shape[:2]
     capacity = tops.shape[0]
     at = pl.program_id(0)
@@ -221,7 +237,7 @@
             bottoms[:, span(c)] = bottom_rows[c, ROWS:, :].astype(BF16)
 
 
-def pack_halos(places, chips, d, plan, pert, near, far, block, capacity):
+def pack_owners(places, chips, d, plan, pert, near, far, block, capacity):
     members, _, variables, rows, cells = pert.shape
     blocks = near.shape[0] // block
     out = jax.ShapeDtypeStruct((capacity, cells), BF16)
@@ -233,7 +249,7 @@
         return (0, owner_of(plan[places.ME], chips, d, other) * blocks + lax.rem(i, blocks), 0, 0, 0)
 
     return pl.pallas_call(
-        functools.partial(pack_kernel, places, chips, d),
+        functools.partial(pack_owners_kernel, places, chips, d),
         out_shape=(out, out),
         grid_spec=pltpu.PrefetchScalarGridSpec(
             num_scalar_prefetch=1,
@@ -255,6 +271,68 @@
     )(plan, pert, near, far)
 
 
+def pack_members_kernel(places, chips, d, plan, pert, mate, grad, tops, bottoms, top_rows, bottom_rows, offset):
+    members, block = pert.shape[:2]
+    capacity = tops.shape[0]
+    at = pl.program_id(0)
+    owned = pl.num_programs(0) * block
+    first = owner_of(plan[places.ME], chips, d, 0) * owned + at * block
+
+    @pl.when(at == 0)
+    def _():
+        offset[0] = 0
+
+    for j in range(block):
+        count = plan[places.steps + first + j]
+        for source in (pert, mate):
+            for m in range(members):
+                off = jnp.minimum(offset[0], capacity)
+                for c in range(top_rows.shape[0]):
+                    part = product_of(source, grad, m, j, c).astype(F32)
+                    top_rows[c, pl.ds(off, ROWS), :] = part
+                    bottom_rows[c, pl.ds(capacity - off, ROWS), :] = part
+                offset[0] = off + count
+
+    @pl.when(at == pl.num_programs(0) - 1)
+    def _():
+        for c in range(top_rows.shape[0]):
+            tops[:, span(c)] = top_rows[c, :capacity, :].astype(BF16)
+            bottoms[:, span(c)] = bottom_rows[c, ROWS:, :].astype(BF16)
+
+
+def pack_members(places, chips, d, plan, pert, mate, grad, block, capacity):
+    members, _, variables, rows, cells = pert.shape
+    blocks = grad.shape[0] // block
+    out = jax.ShapeDtypeStruct((capacity, cells), BF16)
+    whole = pl.BlockSpec((capacity, cells), lambda i, plan: (0, 0))
+    pert_block = (members, block, variables, rows, cells)
+
+    def pert_place(i, plan):
+        return (0, owner_of(plan[places.ME], chips, d, 0) * blocks + i, 0, 0, 0)
+
+    return pl.pallas_call(
+        functools.partial(pack_members_kernel, places, chips, d),
+        out_shape=(out, out),
+        grid_spec=pltpu.PrefetchScalarGridSpec(
+            num_scalar_prefetch=1,
+            grid=(blocks,),
+            in_specs=[
+                pl.BlockSpec(pert_block, pert_place),
+                pl.BlockSpec(pert_block, lambda i, plan: (0, i, 0, 0, 0)),
+                pl.BlockSpec(pert_block[1:], lambda i, plan: (i, 0, 0, 0)),
+            ],
+            out_specs=[whole, whole],
+            scratch_shapes=[
+                pltpu.VMEM((cells // LANES, capacity + ROWS, LANES), F32),
+                pltpu.VMEM((cells // LANES, capacity + ROWS, LANES), F32),
+                pltpu.SMEM((1,), I32),
+            ],
+        ),
+        compiler_params=pltpu.CompilerParams(vmem_limit_bytes=VMEM_BYTES),
+        cost_estimate=cost(16 * grad.size, grad.size * 2 * (2 * members + 1)),
+    )(plan, pert, mate, grad)
+
+
 def deep_product_kernel(places, chips, per_device, group, plan, *refs):
     perts, grads, out = refs[:group], refs[group:-1], refs[-1]
     members = perts[0].shape[0]
@@ -286,7 +364,7 @@
 
 def deep_products(places, chips, plan, pert, grads, top, per_device):
     members, _, variables, rows, cells = pert.shape
-    group = 4 if top % 4 == 0 else 1
+    group = 4 if top == 4 else 1
 
     def pert_spec(u):
         return pl.BlockSpec((members, 1, variables, rows, cells), lambda i, plan: (0, plan[places.deep + i * group + u], 0, 0, 0))
@@ -366,27 +444,30 @@
     return lax.rem(q, devices) * per_device + q // devices
 
 
-def smooth_kernel(places, chips, d, other, low, owned, top, per_device, with_deep, with_part, with_variance, plan, pert, grad, below, above, keep, mix, *rest):
+def smooth_kernel(places, chips, d, other, low, owned, top, per_device, with_mate, deep_count, with_variance, plan, pert, grad, below, above, keep, mix, *rest):
     extra, (out, below_rows, above_rows, field, offset) = rest[:-5], rest[-5:]
-    if with_deep:
-        deep, extra = extra[0], extra[1:]
+    perts = (pert,)
+    if with_mate:
+        perts, extra = (pert, extra[0]), extra[1:]
+    deeps, extra = extra[:deep_count], extra[deep_count:]
     members, block = pert.shape[:2]
+    sources = [(source, m) for source in perts for m in range(members)]
     capacity = below.shape[0]
     tiles = field.shape[1]
     at = pl.program_id(0)
-    first = owner_of(plan[places.ME], chips, d, other) * owned + low + at * block
+    ahead = owner_of(plan[places.ME], chips, d, other) * owned
 
     @pl.when(at == 0)
     def _():
         start = jnp.int32(0)
         for owner, count in ([(0, owned)] if other else []) + [(other, low)]:
-            ahead = owner_of(plan[places.ME], chips, d, owner) * owned
+            base = places.steps + owner_of(plan[places.ME], chips, d, owner) * owned
 
             def add(j, total):
-                return total + plan[places.steps + ahead + j]
+                return total + plan[base + j]
 
             start = lax.fori_loop(0, count, add, start)
-        offset[0] = members * start
+        offset[0] = len(sources) * start
         for c in range(tiles):
             below_rows[c, :capacity, :] = below[:, span(c)].astype(F32)
             below_rows[c, capacity:, :] = jnp.zeros((ROWS, LANES), F32)
@@ -397,63 +478,61 @@
         smooth = [value.astype(BF16).astype(F32) for value in values]
         for v in range(out.shape[1]):
             total = None
-            for m in range(members):
-                term = pert[m, j, v, :, span(c)].astype(F32) * smooth[m]
+            for (source, m), value in zip(sources, smooth):
+                term = source[m, j, v, :, span(c)].astype(F32) * value
                 total = term if total is None else total + term
-            if with_part:
-                total = total + extra[0][j, v, :, span(c)].astype(F32)
             if with_variance:
                 total = total + extra[0][j, v, :, span(c)] * grad[j, v, :, span(c)].astype(F32)
             out[j, v, :, span(c)] = total.astype(out.dtype)
 
     def one_level(j, carry):
-        level = first + j
+        level = ahead + low + at * block + j
         count = plan[places.steps + level]
         rank = plan[places.ranks + level]
 
         @pl.when(rank >= top)
         def _():
-            for m in range(members):
+            for i, (source, m) in enumerate(sources):
                 off = jnp.minimum(offset[0], capacity)
                 for c in range(tiles):
-                    field[m, c, :ROWS, :] = above_rows[c, pl.ds(capacity - off, ROWS), :]
-                    field[m, c, ROWS:2 * ROWS, :] = product_of(pert, grad, m, j, c).astype(F32)
-                    field[m, c, 2 * ROWS:, :] = below_rows[c, pl.ds(off, ROWS), :]
+                    field[i, c, :ROWS, :] = above_rows[c, pl.ds(capacity - off, ROWS), :]
+                    field[i, c, ROWS:2 * ROWS, :] = product_of(source, grad, m, j, c).astype(F32)
+                    field[i, c, 2 * ROWS:, :] = below_rows[c, pl.ds(off, ROWS), :]
                 offset[0] = off + count
 
             def step(i, carry):
-                for m in range(members):
-                    sweep(field, keep, mix, m, ROWS - EDGE, ROWS + 2 * EDGE)
+                for i in range(len(sources)):
+                    sweep(field, keep, mix, i, ROWS - EDGE, ROWS + 2 * EDGE)
                 return carry
 
             lax.fori_loop(1, count, step, 0)
-            last = [diffuse_columns(field, keep, mix, m, ROWS, ROWS, EDGE) for m in range(members)]
+            last = [diffuse_columns(field, keep, mix, i, ROWS, ROWS, EDGE) for i in range(len(sources))]
             for c, values in enumerate(zip(*last)):
                 emit(j, c, values)
 
         @pl.when(rank < top)
         def _():
             for c in range(tiles):
-                if with_deep:
-                    spots = [deep_place(rank * members + m, deep.shape[0], per_device) for m in range(members)]
-                    emit(j, c, [deep[spot, :, span(c)] for spot in spots])
+                if deep_count > 0:
+                    spots = [deep_place(rank * members + m, deeps[0].shape[0], per_device) for m in range(members)]
+                    emit(j, c, [deep[spot, :, span(c)] for deep in deeps for spot in spots])
                 else:
-                    emit(j, c, [jnp.zeros((ROWS, LANES), F32)] * members)
+                    emit(j, c, [jnp.zeros((ROWS, LANES), F32)] * len(sources))
 
         return carry
 
     lax.fori_loop(0, block, one_level, 0)
 
 
-def smooth_owner(places, chips, d, other, low, count, top, per_device, plan, pert, grad, halos, keep, mix, deep, part, variance, block, dtype):
+def smooth_owner(places, chips, d, other, low, count, top, per_device, plan, pert, mate, grad, halos, keep, mix, deeps, variance, block, dtype):
     members, _, variables, rows, cells = pert.shape
     tiles = cells // LANES
     capacity = halos[0].shape[0]
     owned = grad.shape[0]
-    wholes = [halos[0], halos[1], keep, mix] + ([] if deep is None else [deep])
-    extra = [x for x in (part, variance) if x is not None]
+    mates = [] if mate is None else [mate]
+    extra = [] if variance is None else [variance]
     kernel = functools.partial(
-        smooth_kernel, places, chips, d, other, low, owned, top, per_device, deep is not None, part is not None, variance is not None
+        smooth_kernel, places, chips, d, other, low, owned, top, per_device, mate is not None, len(deeps), variance is not None
     )
 
     def whole(x):
@@ -465,26 +544,29 @@
     def levels_from(start):
         return pl.BlockSpec((block, variables, rows, cells), lambda i, *refs: (start // block + i, 0, 0, 0))
 
+    pert_block = (members, block, variables, rows, cells)
     return pl.pallas_call(
         kernel,
         out_shape=jax.ShapeDtypeStruct((count,) + grad.shape[1:], dtype),
         grid_spec=pltpu.PrefetchScalarGridSpec(
             num_scalar_prefetch=1,
             grid=(count // block,),
-            in_specs=[pl.BlockSpec((members, block, variables, rows, cells), pert_place), levels_from(low)]
-            + [whole(x) for x in wholes]
-            + [levels_from(0) for x in extra],
+            in_specs=[pl.BlockSpec(pert_block, pert_place), levels_from(low)]
+            + [whole(x) for x in (halos[0], halos[1], keep, mix)]
+            + [pl.BlockSpec(pert_block, lambda i, plan: (0, low // block + i, 0, 0, 0)) for x in mates]
+            + [whole(x) for x in deeps]
+            + [levels_from(low) for x in extra],
             out_specs=levels_from(0),
             scratch_shapes=[
                 pltpu.VMEM((tiles, capacity + ROWS, LANES), F32),
                 pltpu.VMEM((tiles, capacity + ROWS, LANES), F32),
-                pltpu.VMEM((members, tiles, 3 * ROWS, LANES), F32),
+                pltpu.VMEM(((1 + len(mates)) * members, tiles, 3 * ROWS, LANES), F32),
                 pltpu.SMEM((1,), I32),
             ],
         ),
         compiler_params=pltpu.CompilerParams(vmem_limit_bytes=VMEM_BYTES),
         cost_estimate=cost(100 * grad.size, grad.size * 2 * (members + 3)),
-    )(plan, pert, grad, *wholes, *extra)
+    )(plan, pert, grad, halos[0], halos[1], keep, mix, *mates, *deeps, *extra)
 
 
 def final_kernel(places, top, per_device, owned, parts, plan, pert, near, part, deep, *rest):
@@ -550,12 +632,11 @@
     )(plan, pert, near, part, deep, *arrived)
 
 
-def program(pert, gradient, variance, class_map, values, level_steps, top, capacity):
+def program(pert, gradient, variance, class_map, values, level_steps, top, capacities):
     members, levels, _, rows, cells = pert.shape
     mem_count = lax.axis_size("mem")
     tile_count = lax.axis_size("tile")
     owned = gradient.shape[0]
-    block, smooth_block, parts = 4, 2, PARTS
     chips = mem_count // 2
     per_device = top * members // tile_count
     places = Plan(levels, top, per_device)
@@ -569,75 +650,78 @@
     south = [(i + 1, i) for i in range(tile_count - 1)]
     north = [(i, i + 1) for i in range(tile_count - 1)]
 
-    far = []
+    grads = [gradient]
     for d in range(1, chips):
-        far.append(hop(gradient, d))
-    position = jnp.stack([lax.axis_index("mem"), lax.axis_index("tile"), jnp.int32(tile_count)])
-    plan, keep, mix = make_plan(places, top, per_device, owned, members, capacity, position, level_steps, values, class_map, rows)
-    grads, halos = [], []
+        grads.append(hop(gradient, d))
+    me = lax.axis_index("mem")
+    plan, fits = make_plan(places, top, per_device, owned, members, capacities, level_steps)
+    keep, mix = make_weights(places, plan, values, class_map, rows)
+    fits = fits[0] > 0
+    mates = [None]
+    for d in range(1, chips):
+        mates.append(swap(lax.dynamic_slice_in_dim(pert, owner_of(me, chips, d, 1) * owned, owned, axis=1)))
+    halos, both_grads = [], []
     for d in range(chips):
-        near = gradient if d == 0 else far[d - 1]
-        other = swap(near)
-        grads += [near, other]
+        other = swap(grads[d])
+        both_grads += [grads[d], other]
         if top < levels:
-            tops, bottoms = pack_halos(places, chips, d, plan, pert, near, other, block, capacity)
+            if d == 0:
+                tops, bottoms = pack_owners(places, chips, d, plan, pert, gradient, other, min(8, owned), capacities[0])
+            else:
+                tops, bottoms = pack_members(places, chips, d, plan, pert, mates[d], grads[d], min(4, owned), capacities[1])
             below = lax.ppermute(tops, "tile", south)
             above = lax.ppermute(bottoms, "tile", north)
             halos.append((below, above))
         else:
             halos.append((jnp.zeros((16, cells), BF16),) * 2)
 
-    deep = deep_products(places, chips, plan, pert, grads, top, per_device)
+    deep = deep_products(places, chips, plan, pert, both_grads, top, per_device)
     deep = deep.reshape(tile_count, per_device, rows, cells)
     field = lax.all_to_all(deep, "tile", split_axis=0, concat_axis=0, tiled=True)
     field = deep_smooth(places, plan, field, class_map, values)
     deep = lax.all_to_all(field, "tile", split_axis=0, concat_axis=0, tiled=True).reshape(-1, rows, cells)
-
-    def smooth(d, other, low, count, whole, part, var, dtype):
+    deeps = (deep, swap(deep))
+
+    def smooth(d, other, low, size, whole, var, dtype):
         return smooth_owner(
-            places, chips, d, other, low, count, top, per_device, plan, pert, grads[2 * d + other], halos[d], keep, mix,
-            whole, part, var, smooth_block, dtype
+            places, chips, d, other, low, size, top, per_device, plan, pert, mates[d], both_grads[2 * d + other], halos[d], keep, mix,
+            whole, var, min(4, size), dtype
         )
 
-    near_sum = smooth(0, 0, 0, owned, None, None, variance, F32)
+    near = smooth(0, 0, 0, owned, (), variance, F32)
     arrived = []
-    size = owned // parts
+    size = owned // PARTS
     for d in range(1, chips):
-        crossed = []
-        for p in range(parts):
-            other = smooth(d, 1, p * size, size, deep, None, None, BF16)
-            crossed.append(swap(other))
-        for p in range(parts):
-            both = smooth(d, 0, p * size, size, deep, crossed[p], None, BF16)
-            arrived.append(hop(both, chips - d))
-    part = smooth(0, 1, 0, owned, deep, None, None, BF16)
+        for p in range(PARTS):
+            part = smooth(d, 0, p * size, size, deeps, None, BF16)
+            arrived.append(hop(part, chips - d))
+    part = smooth(0, 1, 0, owned, deeps[:1], None, BF16)
     part = swap(part)
-
-    return plan, near_sum, part, deep, arrived
+    return fits, (plan, near, part, deep, arrived)
 
 
 def finish(places, top, per_device, pert, sums):
     plan, near, part, deep, arrived = sums
-    return final_sum(places, top, per_device, PARTS, plan, pert, near, part, deep, arrived, 2)
+    return final_sum(places, top, per_device, PARTS, plan, pert, near, part, deep, arrived, min(4, near.shape[0] // PARTS))
 
 
 def shards(perturbations, gradient, static_variance, level_steps, class_map, class_diffusivity):
     members, levels = perturbations.shape[:2]
     owned = gradient.shape[0]
     top = lax.axis_size("tile") // members
-    capacity = (5 * members * owned + 15) // 16 * 16
+    capacities = ((5 * members * owned + 7) // 8 * 8, (11 * members * owned // 2 + 7) // 8 * 8)
     operands = (perturbations, gradient, static_variance, class_map, class_diffusivity, level_steps)
     tiles = lax.axis_size("tile")
-    sums = program(*operands, top, capacity)
+    fits, sums = program(*operands, top, capacities)
 
     def halo(sums, *operands):
         return finish(Plan(levels, top, top * members // tiles), top, top * members // tiles, operands[0], sums)
 
     def general(sums, *operands):
         per_device = levels * members // tiles
-        return finish(Plan(levels, levels, per_device), levels, per_device, operands[0], program(*operands, levels, 16))
-
-    return lax.cond(sums[0][Plan.FITS] > 0, halo, general, sums, *operands)
+        return finish(Plan(levels, levels, per_device), levels, per_device, operands[0], program(*operands, levels, (0, 0))[1])
+
+    return lax.cond(fits, halo, general, sums, *operands)
 
 
 def solution(mesh):

time: 151 us -> 144 us (0.954)
  Pallas kernels: 65.4 us -> 58.2 us
    pallas_call x6 -> x4, Pallas kernels: 36.1 us -> 29.1 us  [smooth_owner(): pl.pallas_call(kernel, out_shape=jax.ShapeDtypeStruct((count,) + grad.sha...]
    dynamic_slice x0 -> x1, local copies, waits for them, and re-layouts: none -> 2.69 us  [program(): lax.dynamic_slice_in_dim(pert, owner_of(me, chips, d, 1) * owned, owned,...]
    pallas_call x2 -> x3, Pallas kernels: 10.9 us -> 11.8 us  [the longest x1 4.77 us: pack_owners(): pl.pallas_call(functools.partial(pack_owners_kernel, places, chips, d), o...]
  transfers between devices with their start and end apart: 13 -> 13, of which waited for: 3 -> 4; matrix products, arithmetic and copies ran while one was open for 1% -> 2% of each run, Pallas kernels for 33% -> 38%
where the time goes in v3:
time: 144 us; the launch traced here: 143 us
  Pallas kernels  58.2 us (40%)
  waiting for transfers between devices  41.2 us (29%)
  starting transfers between devices  21.4 us (15%)
  blocking collectives  18.5 us (13%)
  local copies, waits for them, and re-layouts  2.69 us (2%)
    pallas_call x4, Pallas kernels, smooth_owner(): pl.pallas_call(kernel, out_shape=jax.ShapeDtypeStruct((count,) + grad.sha...  29.1 us
    ppermute x3, waiting for transfers between devices, hop(): lax.ppermute(value, 'mem', [(i, (i // 2 + d) % chips * 2 + i % 2) for i i...  22.4 us
    ppermute x2, waiting for transfers between devices, program(): above = lax.ppermute(bottoms, 'tile', north)  18.8 us
    all_to_all x1, blocking collectives, program(): lax.all_to_all(deep, 'tile', split_axis=0, concat_axis=0, tiled=True)  18.5 us
    ppermute x2, starting transfers between devices, program(): above = lax.ppermute(bottoms, 'tile', north)  10.6 us
    pallas_call x1, Pallas kernels, deep_smooth(): pl.pallas_call(functools.partial(deep_kernel, places.mine), out_shape=jax...  7.33 us
    pallas_call x1, Pallas kernels, pack_owners(): pl.pallas_call(functools.partial(pack_owners_kernel, places, chips, d), o...  4.77 us
    pallas_call x1, Pallas kernels, pack_members(): pl.pallas_call(functools.partial(pack_members_kernel, places, chips, d),...  4.48 us
  transfers between devices with their start and end apart: 13, of which 4 were waited for; matrix products, arithmetic and copies ran while one was open for 2% of the time, Pallas kernels for 38%

profile of v3, /device:TPU:0, one launch (start us, length us, event | category | flops | bytes accessed | tf_op | source)
XLA Modules:
  0.0 142.8 jit_solution(17305844586970226967)
XLA Ops:
  0.0 3.0 %collective-permute-start.11 = (bf16[8,2,8,3072]{3,2,1,0:T(8,128)(2,1)}, bf16[8,2,8,3072]{3,2,1,0:T(8,128)(2,1)}, u32[]{:S(2)}, u32[]{:S(2)}) collective-permute-start(bf16[8,2,8,3072]{3,2,1,0:T(8,128)(2,1)} %refs_16_.1), channel_id=1, source_target_pairs={{0,16},{8,24},{16,0},{24,8},{1,17},{9,25},{17,1},{25,9},{2,18},{10... | collective-permute-start | bytes 2359304 | tf_op jit(solution)/shard_map/ppermute | solution.py:645
  3.0 17.9 %collective-permute-done.11.refs_6_.refs_10_.refs_14_.refs_18_.grad = bf16[8,2,8,3072]{3,2,1,0:T(8,128)(2,1)} collective-permute-done((bf16[8,2,8,3072]{3,2,1,0:T(8,128)(2,1)}, bf16[8,2,8,3072]{3,2,1,0:T(8,128)(2,1)}, u32[]{:S(2)}, u32[]{:S(2)}) %collective-permute-start.11) | collective-permute-done | bytes 786464 | tf_op jit(solution)/shard_map/ppermute | solution.py:645
  20.8 0.0 collective-permute-start.12
  20.8 2.7 %constant_dynamic-slice_fusion.1 = bf16[2,8,2,8,3072]{4,3,2,1,0:T(8,128)(2,1)} fusion(bf16[2,32,2,8,3072]{4,3,2,1,0:T(8,128)(2,1)} %pert.11, s32[]{:T(128)S(6)} %select_n.15), kind=kLoop, calls=%fused_computation.1 | loop fusion | bytes 3145732 | tf_op jit(solution)/shard_map/dynamic_slice | solution.py:662
  23.5 0.5 collective-permute-start.14
  24.0 2.1 %plan.3 = (s32[78]{0:T(128)}, s32[1]{0:T(128)}) custom-call(s32[32]{0:T(128)} %level_steps.1), custom_call_target="tpu_custom_call" | custom-call | bytes 312 | tf_op jit(solution)/shard_map/plan/pallas_call | solution.py:141
  26.2 0.0 collective-permute-done.12.refs_7_.refs_11_.refs_15_.refs_19_
  26.2 3.5 %deep_product.3 = bf16[8,8,3072]{2,1,0:T(8,128)(2,1)} custom-call(s32[78]{0:T(128)} %get-tuple-element.59.plan, bf16[2,32,2,8,3072]{4,3,2,1,0:T(8,128)(2,1)} %pert.11, bf16[2,32,2,8,3072]{4,3,2,1,0:T(8,128)(2,1)} %pert.11, bf16[2,32,2,8,3072]{4,3,2,1,0:T(8,128)(2,1)} %pert.11, bf16[2,32,2,8,3072]{4,3,2,1,0:T(8,128)(2,1)} %pert.11, ...), custom_call_target="tpu_custom_call" | custom-call | flops 786432 | bytes 1572864 | tf_op jit(solution)/shard_map/deep_product/pallas_call | solution.py:379
  29.7 18.5 %all_to_all.20.planes = bf16[8,1,8,3072]{3,2,1,0:T(8,128)(2,1)} all-to-all(bf16[8,1,8,3072]{3,2,1,0:T(8,128)(2,1)} %bitcast.6), channel_id=1, replica_groups=mesh['mem'=4,'tile'=8] {'tile'}, dimensions={0} | all-to-all | bytes 786432 | tf_op jit(solution)/shard_map/all_to_all | solution.py:680
  48.2 7.3 %deep_smooth.3 = bf16[8,1,8,3072]{3,2,1,0:T(8,128)(2,1)} custom-call(s32[78]{0:T(128)} %get-tuple-element.59.plan, f32[4]{0:T(128)} %values.3, bf16[8,1,8,3072]{3,2,1,0:T(8,128)(2,1)} %all_to_all.20.planes, s32[64,3072]{1,0:T(8,128)} %class_map.1), custom_call_target="tpu_custom_call" | custom-call | flops 29491200 | bytes 1572864 | tf_op jit(solution)/shard_map/deep_smooth/pallas_call | solution.py:425
  55.5 4.1 %all-to-all-start.3 = ((bf16[8,1,8,3072]{3,2,1,0:T(8,128)(2,1)}), bf16[8,1,8,3072]{3,2,1,0:T(8,128)(2,1)}, u32[]{:S(2)}, u32[]{:S(2)}) async-start(bf16[8,1,8,3072]{3,2,1,0:T(8,128)(2,1)} %deep_smooth.3), calls=%async_computation.3 | async-start | bytes 786432 | tf_op jit(solution)/shard_map/all_to_all | solution.py:682
  59.6 4.8 %shard_map.66 = (bf16[80,3072]{1,0:T(8,128)(2,1)}, bf16[80,3072]{1,0:T(8,128)(2,1)}) custom-call(s32[78]{0:T(128)} %get-tuple-element.59.plan, bf16[2,32,2,8,3072]{4,3,2,1,0:T(8,128)(2,1)} %pert.11, bf16[8,2,8,3072]{3,2,1,0:T(8,128)(2,1)} %refs_16_.1, bf16[8,2,8,3072]{3,2,1,0:T(8,128)(2,1)} %collective-permute-done.8.far.refs_5_.refs_9_.refs_13_.refs_17_.grad), custom_call_target="tpu_custom_call" | custom-call | flops 3145728 | bytes 4718592 | tf_op jit(solution)/shard_map/pallas_call | solution.py:251
  64.4 4.6 %collective-permute-start.10 = (bf16[80,3072]{1,0:T(8,128)(2,1)}, bf16[80,3072]{1,0:T(8,128)(2,1)}, u32[]{:S(2)}, u32[]{:S(2)}) collective-permute-start(bf16[80,3072]{1,0:T(8,128)(2,1)} %get-tuple-element.61), channel_id=1, source_target_pairs={{0,1},{1,2},{2,3},{3,4},{4,5},{5,6},{6,7},{8,9},{9,10},{10,11},{11... | collective-permute-start | bytes 1474568 | tf_op jit(solution)/shard_map/ppermute | solution.py:673
  69.0 1.3 collective-permute-start.9
  70.3 4.5 %shard_map.69 = (bf16[88,3072]{1,0:T(8,128)(2,1)}, bf16[88,3072]{1,0:T(8,128)(2,1)}) custom-call(s32[78]{0:T(128)} %get-tuple-element.59.plan, bf16[2,32,2,8,3072]{4,3,2,1,0:T(8,128)(2,1)} %pert.11, bf16[2,8,2,8,3072]{4,3,2,1,0:T(8,128)(2,1)} %collective-permute-done.14.mate.rest_0_, ...), custom_call_target="tpu_custom_call" | custom-call | flops 6291456 | bytes 3932160 | tf_op jit(solution)/shard_map/pallas_call | solution.py:313
  74.8 1.3 collective-permute-start.15
  76.1 6.0 %collective-permute-start.16 = (bf16[88,3072]{1,0:T(8,128)(2,1)}, bf16[88,3072]{1,0:T(8,128)(2,1)}, u32[]{:S(2)}, u32[]{:S(2)}) collective-permute-start(bf16[88,3072]{1,0:T(8,128)(2,1)} %get-tuple-element.65), channel_id=1, source_target_pairs={{0,1},{1,2},{2,3},{3,4},{4,5},{5,6},{6,7},{8,9},{9,10},{10,11},{11... | collective-permute-start | bytes 1622024 | tf_op jit(solution)/shard_map/ppermute | solution.py:673
  82.1 0.0 all-to-all-done.3
  82.1 0.0 collective-permute-start.17
  82.1 2.6 %weights.3 = (f32[24,16,128]{2,1,0:T(8,128)}, f32[24,16,128]{2,1,0:T(8,128)}) custom-call(s32[78]{0:T(128)} %get-tuple-element.59.plan, f32[4]{0:T(128)} %values.3, s32[64,3072]{1,0:T(8,128)} %class_map.1, s32[64,3072]{1,0:T(8,128)} %class_map.1, s32[64,3072]{1,0:T(8,128)} %class_map.1), custom_call_target="tpu_custom_call" | custom-call | bytes 393216 | tf_op jit(solution)/shard_map/weights/pallas_call | solution.py:175
  84.7 17.6 %collective-permute-done.10.above = bf16[80,3072]{1,0:T(8,128)(2,1)} collective-permute-done((bf16[80,3072]{1,0:T(8,128)(2,1)}, bf16[80,3072]{1,0:T(8,128)(2,1)}, u32[]{:S(2)}, u32[]{:S(2)}) %collective-permute-start.10) | collective-permute-done | bytes 491552 | tf_op jit(solution)/shard_map/ppermute | solution.py:673
  102.2 0.0 collective-permute-done.9.below
  102.2 8.2 %shard_map.68 = bf16[8,2,8,3072]{3,2,1,0:T(8,128)(2,1)} custom-call(s32[78]{0:T(128)} %get-tuple-element.59.plan, bf16[2,32,2,8,3072]{4,3,2,1,0:T(8,128)(2,1)} %pert.11, bf16[8,2,8,3072]{3,2,1,0:T(8,128)(2,1)} %collective-permute-done.8.far.refs_5_.refs_9_.refs_13_.refs_17_.grad, bf16[80,3072]{1,0:T(8,128)(2,1)} %collective-permute-done.9.below, ...), custom_call_target="tpu_custom_call" | custom-call | flops 39321600 | bytes 3932160 | tf_op jit(solution)/shard_map/pallas_call | solution.py:548
  110.5 1.2 collective-permute-done.16.above
  111.7 7.7 %shard_map.71 = bf16[4,2,8,3072]{3,2,1,0:T(8,128)(2,1)} custom-call(s32[78]{0:T(128)} %get-tuple-element.59.plan, bf16[2,32,2,8,3072]{4,3,2,1,0:T(8,128)(2,1)} %pert.11, bf16[8,2,8,3072]{3,2,1,0:T(8,128)(2,1)} %collective-permute-done.11.refs_6_.refs_10_.refs_14_.refs_18_.grad, bf16[88,3072]{1,0:T(8,128)(2,1)} %collective-permute-done.15.below, ...), custom_call_target="tpu_custom_call" | custom-call | flops 39321600 | bytes 3932160 | tf_op jit(solution)/shard_map/pallas_call | solution.py:548
  119.4 0.0 collective-permute-start.19
  119.4 7.2 %shard_map.70 = bf16[4,2,8,3072]{3,2,1,0:T(8,128)(2,1)} custom-call(s32[78]{0:T(128)} %get-tuple-element.59.plan, bf16[2,32,2,8,3072]{4,3,2,1,0:T(8,128)(2,1)} %pert.11, bf16[8,2,8,3072]{3,2,1,0:T(8,128)(2,1)} %collective-permute-done.11.refs_6_.refs_10_.refs_14_.refs_18_.grad, bf16[88,3072]{1,0:T(8,128)(2,1)} %collective-permute-done.15.below, ...), custom_call_target="tpu_custom_call" | custom-call | flops 39321600 | bytes 3932160 | tf_op jit(solution)/shard_map/pallas_call | solution.py:548
  126.6 0.7 collective-permute-start.18
  127.9 6.0 %shard_map.67 = f32[8,2,8,3072]{3,2,1,0:T(8,128)} custom-call(s32[78]{0:T(128)} %get-tuple-element.59.plan, bf16[2,32,2,8,3072]{4,3,2,1,0:T(8,128)(2,1)} %pert.11, bf16[8,2,8,3072]{3,2,1,0:T(8,128)(2,1)} %refs_16_.1, bf16[80,3072]{1,0:T(8,128)(2,1)} %collective-permute-done.9.below, bf16[80,3072]{1,0:T(8,128)(2,1)} %collective-permute-done.10.above, ...), custom_call_target="tpu_custom_call" | custom-call | flops 39321600 | bytes 3932160 | tf_op jit(solution)/shard_map/pallas_call | solution.py:548
  133.9 4.6 %collective-permute-done.18 = bf16[4,2,8,3072]{3,2,1,0:T(8,128)(2,1)} collective-permute-done((bf16[4,2,8,3072]{3,2,1,0:T(8,128)(2,1)}, bf16[4,2,8,3072]{3,2,1,0:T(8,128)(2,1)}, u32[]{:S(2)}, u32[]{:S(2)}) %collective-permute-start.18) | collective-permute-done | bytes 393248 | tf_op jit(solution)/shard_map/ppermute | solution.py:645
  138.5 4.3 %conditional.1 = (f32[8,2,8,3072]{3,2,1,0:T(8,128)}) conditional(s32[]{:T(128)} %bitcast.2, (s32[32]{0:T(128)}, f32[4]{0:T(128)}, s32[64,3072]{1,0:T(8,128)}, bf16[2,32,2,8,3072]{4,3,2,1,0:T(8,128)(2,1)}, bf16[8,2,8,3072]{3,2,1,0:T(8,128)(2,1)}, /*index=5*/f32[8,2,8,3072]{3,2,1,0:T(8,128)}) %tuple.11, (s32[78]{0:T(128)}, ...), branch_computations={%region_0.1_spmd, %region_1.2_spmd} | conditional | flops 401080320 | bytes 90932376 | solution.py:724
  138.5 4.3 %final_sum.3 = f32[8,2,8,3072]{3,2,1,0:T(8,128)} custom-call(s32[78]{0:T(128)} %get-tuple-element.43.plan, bf16[2,32,2,8,3072]{4,3,2,1,0:T(8,128)(2,1)} %get-tuple-element.44.pert, f32[8,2,8,3072]{3,2,1,0:T(8,128)} %get-tuple-element.45.near, bf16[8,2,8,3072]{3,2,1,0:T(8,128)(2,1)} %get-tuple-element.46.part, bf16[8,8,3072]{2,1,0:T(8,128)(2,1)} %get-tuple-element.47.deep, ...), custom_call_target="tpu_custom_call" | custom-call | flops 1572864 | bytes 4718592 | tf_op jit(solution)/shard_map/cond/branch_1_fun/final_sum/pallas_call | solution.py:617
  (8 shorter events, 0.0 us)
Async XLA Ops:
  0.0 20.8 %collective-permute-start.11 = (bf16[8,2,8,3072]{3,2,1,0:T(8,128)(2,1)}, bf16[8,2,8,3072]{3,2,1,0:T(8,128)(2,1)}, u32[]{:S(2)}, u32[]{:S(2)}) collective-permute-start(bf16[8,2,8,3072]{3,2,1,0:T(8,128)(2,1)} %refs_16_.1), channel_id=1, source_target_pairs={{0,16},{8,24},{16,0},{24,8},{1,17},{9,25},{17,1},{25,9},{2,18},{10... | collective-permute-start | bytes 2359304 | tf_op jit(solution)/shard_map/ppermute | solution.py:645
  3.0 23.2 %collective-permute-start.8 = (bf16[8,2,8,3072]{3,2,1,0:T(8,128)(2,1)}, bf16[8,2,8,3072]{3,2,1,0:T(8,128)(2,1)}, u32[]{:S(2)}, u32[]{:S(2)}) collective-permute-start(bf16[8,2,8,3072]{3,2,1,0:T(8,128)(2,1)} %refs_16_.1), channel_id=1, source_target_pairs={{0,8},{8,0},{16,24},{24,16},{1,9},{9,1},{17,25},{25,17},{2,10},{10... | collective-permute-start | bytes 2359304 | tf_op jit(solution)/shard_map/ppermute | solution.py:648
  20.8 5.4 %collective-permute-start.12 = (bf16[8,2,8,3072]{3,2,1,0:T(8,128)(2,1)}, bf16[8,2,8,3072]{3,2,1,0:T(8,128)(2,1)}, u32[]{:S(2)}, u32[]{:S(2)}) collective-permute-start(bf16[8,2,8,3072]{3,2,1,0:T(8,128)(2,1)} %collective-permute-done.11.refs_6_.refs_10_.refs_14_.refs_18_.grad), channel_id=1, source_target_pairs={{0,8},{8,0},{16,24},{24,16},{1,9},{9,1},{17,25},{25,17},{2,10},{10... | collective-permute-start | bytes 2359304 | tf_op jit(solution)/shard_map/ppermute | solution.py:648
  23.5 46.8 %collective-permute-start.14 = (bf16[2,8,2,8,3072]{4,3,2,1,0:T(8,128)(2,1)}, bf16[2,8,2,8,3072]{4,3,2,1,0:T(8,128)(2,1)}, u32[]{:S(2)}, u32[]{:S(2)}) collective-permute-start(bf16[2,8,2,8,3072]{4,3,2,1,0:T(8,128)(2,1)} %constant_dynamic-slice_fusion.1), channel_id=1, source_target_pairs={{0,8},{8,0},{16,24},{24,16},{1,9},{9,1},{17,25},{25,17},{2,10},{10... | collective-permute-start | bytes 4718600 | tf_op jit(solution)/shard_map/ppermute | solution.py:648
  55.5 26.5 %all-to-all-start.3 = ((bf16[8,1,8,3072]{3,2,1,0:T(8,128)(2,1)}), bf16[8,1,8,3072]{3,2,1,0:T(8,128)(2,1)}, u32[]{:S(2)}, u32[]{:S(2)}) async-start(bf16[8,1,8,3072]{3,2,1,0:T(8,128)(2,1)} %deep_smooth.3), calls=%async_computation.3 | async-start | bytes 786432 | tf_op jit(solution)/shard_map/all_to_all | solution.py:682
  64.4 37.8 %collective-permute-start.10 = (bf16[80,3072]{1,0:T(8,128)(2,1)}, bf16[80,3072]{1,0:T(8,128)(2,1)}, u32[]{:S(2)}, u32[]{:S(2)}) collective-permute-start(bf16[80,3072]{1,0:T(8,128)(2,1)} %get-tuple-element.61), channel_id=1, source_target_pairs={{0,1},{1,2},{2,3},{3,4},{4,5},{5,6},{6,7},{8,9},{9,10},{10,11},{11... | collective-permute-start | bytes 1474568 | tf_op jit(solution)/shard_map/ppermute | solution.py:673
  69.0 33.2 %collective-permute-start.9 = (bf16[80,3072]{1,0:T(8,128)(2,1)}, bf16[80,3072]{1,0:T(8,128)(2,1)}, u32[]{:S(2)}, u32[]{:S(2)}) collective-permute-start(bf16[80,3072]{1,0:T(8,128)(2,1)} %get-tuple-element.60), channel_id=1, source_target_pairs={{1,0},{2,1},{3,2},{4,3},{5,4},{6,5},{7,6},{9,8},{10,9},{11,10},{12... | collective-permute-start | bytes 1474568 | tf_op jit(solution)/shard_map/ppermute | solution.py:672
  74.8 35.7 %collective-permute-start.15 = (bf16[88,3072]{1,0:T(8,128)(2,1)}, bf16[88,3072]{1,0:T(8,128)(2,1)}, u32[]{:S(2)}, u32[]{:S(2)}) collective-permute-start(bf16[88,3072]{1,0:T(8,128)(2,1)} %get-tuple-element.64), channel_id=1, source_target_pairs={{1,0},{2,1},{3,2},{4,3},{5,4},{6,5},{7,6},{9,8},{10,9},{11,10},{12... | collective-permute-start | bytes 1622024 | tf_op jit(solution)/shard_map/ppermute | solution.py:672
  76.1 35.6 %collective-permute-start.16 = (bf16[88,3072]{1,0:T(8,128)(2,1)}, bf16[88,3072]{1,0:T(8,128)(2,1)}, u32[]{:S(2)}, u32[]{:S(2)}) collective-permute-start(bf16[88,3072]{1,0:T(8,128)(2,1)} %get-tuple-element.65), channel_id=1, source_target_pairs={{0,1},{1,2},{2,3},{3,4},{4,5},{5,6},{6,7},{8,9},{9,10},{10,11},{11... | collective-permute-start | bytes 1622024 | tf_op jit(solution)/shard_map/ppermute | solution.py:673
  82.1 29.6 %collective-permute-start.17 = (bf16[8,8,3072]{2,1,0:T(8,128)(2,1)}, bf16[8,8,3072]{2,1,0:T(8,128)(2,1)}, u32[]{:S(2)}, u32[]{:S(2)}) collective-permute-start(bf16[8,8,3072]{2,1,0:T(8,128)(2,1)} %bitcast.4.rest_0_.rest_1_), channel_id=1, source_target_pairs={{0,8},{8,0},{16,24},{24,16},{1,9},{9,1},{17,25},{25,17},{2,10},{10... | collective-permute-start | bytes 1179656 | tf_op jit(solution)/shard_map/ppermute | solution.py:648
  110.5 23.4 %collective-permute-start.13 = (bf16[8,2,8,3072]{3,2,1,0:T(8,128)(2,1)}, bf16[8,2,8,3072]{3,2,1,0:T(8,128)(2,1)}, u32[]{:S(2)}, u32[]{:S(2)}) collective-permute-start(bf16[8,2,8,3072]{3,2,1,0:T(8,128)(2,1)} %shard_map.68), channel_id=1, source_target_pairs={{0,8},{8,0},{16,24},{24,16},{1,9},{9,1},{17,25},{25,17},{2,10},{10... | collective-permute-start | bytes 2359304 | tf_op jit(solution)/shard_map/ppermute | solution.py:648
  119.4 14.5 %collective-permute-start.19 = (bf16[4,2,8,3072]{3,2,1,0:T(8,128)(2,1)}, bf16[4,2,8,3072]{3,2,1,0:T(8,128)(2,1)}, u32[]{:S(2)}, u32[]{:S(2)}) collective-permute-start(bf16[4,2,8,3072]{3,2,1,0:T(8,128)(2,1)} %shard_map.71), channel_id=1, source_target_pairs={{0,16},{8,24},{16,0},{24,8},{1,17},{9,25},{17,1},{25,9},{2,18},{10... | collective-permute-start | bytes 1179656 | tf_op jit(solution)/shard_map/ppermute | solution.py:645
  126.6 11.9 %collective-permute-start.18 = (bf16[4,2,8,3072]{3,2,1,0:T(8,128)(2,1)}, bf16[4,2,8,3072]{3,2,1,0:T(8,128)(2,1)}, u32[]{:S(2)}, u32[]{:S(2)}) collective-permute-start(bf16[4,2,8,3072]{3,2,1,0:T(8,128)(2,1)} %shard_map.70), channel_id=1, source_target_pairs={{0,16},{8,24},{16,0},{24,8},{1,17},{9,25},{17,1},{25,9},{2,18},{10... | collective-permute-start | bytes 1179656 | tf_op jit(solution)/shard_map/ppermute | solution.py:645

commit v4 on v3

--- a/solution.py
+++ b/solution.py
@@ -13,7 +13,7 @@
 ROWS = 8
 EDGE = 4
 PARTS = 2
-VMEM_BYTES = 67043328
+VMEM_BYTES = 32 * 1024 * 1024
 SMEM_SPEC = pl.BlockSpec(memory_space=pltpu.SMEM)
 VMEM_SPEC = pl.BlockSpec(memory_space=pltpu.VMEM)
 ANY_SPEC = pl.BlockSpec(memory_space=pl.ANY)
@@ -107,7 +107,7 @@
         bins[bin_of(level)] += 1
         return carry
 
-    lax.fori_loop(0, levels, count, 0)
+    lax.fori_loop(0, levels, count, 0, unroll=4)
     total = jnp.int32(0)
     for i in reversed(range(BINS)):
         here_count = bins[i]
@@ -131,7 +131,7 @@
         inside = (chip_rows <= capacities[0]) & (owner_rows <= capacities[1]) & (steps <= EDGE)
         return chip_rows, owner_rows, jnp.where(inside, fits, 0)
 
-    fits[0] = lax.fori_loop(0, levels, assign, (jnp.int32(0), jnp.int32(0), jnp.int32(1)))[2]
+    fits[0] = lax.fori_loop(0, levels, assign, (jnp.int32(0), jnp.int32(0), jnp.int32(1)), unroll=4)[2]
     plan[places.deep + top] = 0
     for j in range(per_device):
         plan[places.mine + j] = deep_steps[(j * tile_count + tile) // members]
@@ -685,7 +685,7 @@
     def smooth(d, other, low, size, whole, var, dtype):
         return smooth_owner(
             places, chips, d, other, low, size, top, per_device, plan, pert, mates[d], both_grads[2 * d + other], halos[d], keep, mix,
-            whole, var, min(4, size), dtype
+            whole, var, min(2 if d else 4, size), dtype
         )
 
     near = smooth(0, 0, 0, owned, (), variance, F32)

time: 144 us -> 139 us (0.965)
  Pallas kernels: 58.2 us -> 46.7 us
  waiting for transfers between devices: 41.2 us -> 45.3 us
  local copies, waits for them, and re-layouts: 2.69 us -> 5 us
    pallas_call x4, Pallas kernels: 29.1 us -> 23.9 us  [smooth_owner(): pl.pallas_call(kernel, out_shape=jax.ShapeDtypeStruct((count,) + grad.sha...]
    ppermute x2, waiting for transfers between devices: 18.8 us -> 22 us  [program(): above = lax.ppermute(bottoms, 'tile', north)]
    pallas_call x1, Pallas kernels: 4.29 us -> 2.69 us  [final_sum(): pl.pallas_call(functools.partial(final_kernel, places, top, per_device, o...]
    pallas_call x1, Pallas kernels: 4.48 us -> 3.01 us  [pack_members(): pl.pallas_call(functools.partial(pack_members_kernel, places, chips, d),...]
  transfers between devices with their start and end apart: 13 -> 13, of which waited for: 4 -> 4; matrix products, arithmetic and copies ran while one was open for 2% -> 2% of each run, Pallas kernels for 38% -> 32%
where the time goes in v4:
time: 139 us; the launch traced here: 137 us
  Pallas kernels  46.7 us (34%)
  waiting for transfers between devices  45.3 us (33%)
  starting transfers between devices  20.9 us (15%)
  blocking collectives  18.1 us (13%)
  local copies, waits for them, and re-layouts  5 us (4%)
    pallas_call x4, Pallas kernels, smooth_owner(): pl.pallas_call(kernel, out_shape=jax.ShapeDtypeStruct((count,) + grad.sha...  23.9 us
    ppermute x3, waiting for transfers between devices, hop(): lax.ppermute(value, 'mem', [(i, (i // 2 + d) % chips * 2 + i % 2) for i i...  23.3 us
    ppermute x2, waiting for transfers between devices, program(): above = lax.ppermute(bottoms, 'tile', north)  22 us
    all_to_all x1, blocking collectives, program(): lax.all_to_all(deep, 'tile', split_axis=0, concat_axis=0, tiled=True)  18.1 us
    ppermute x2, starting transfers between devices, program(): above = lax.ppermute(bottoms, 'tile', north)  10.6 us
    pallas_call x1, Pallas kernels, deep_smooth(): pl.pallas_call(functools.partial(deep_kernel, places.mine), out_shape=jax...  6.6 us
    pallas_call x1, Pallas kernels, pack_owners(): pl.pallas_call(functools.partial(pack_owners_kernel, places, chips, d), o...  4.56 us
    ppermute x3, starting transfers between devices, hop(): lax.ppermute(value, 'mem', [(i, (i // 2 + d) % chips * 2 + i % 2) for i i...  3.75 us
  transfers between devices with their start and end apart: 13, of which 4 were waited for; matrix products, arithmetic and copies ran while one was open for 2% of the time, Pallas kernels for 32%

profile of v4, /device:TPU:0, one launch (start us, length us, event | category | flops | bytes accessed | tf_op | source)
XLA Modules:
  0.0 136.9 jit_solution(1867325280285070939)
XLA Ops:
  0.0 3.0 %collective-permute-start.11 = (bf16[8,2,8,3072]{3,2,1,0:T(8,128)(2,1)}, bf16[8,2,8,3072]{3,2,1,0:T(8,128)(2,1)S(1)}, u32[]{:S(2)}, u32[]{:S(2)}) collective-permute-start(bf16[8,2,8,3072]{3,2,1,0:T(8,128)(2,1)} %refs_16_.1), channel_id=1, source_target_pairs={{0,16},{8,24},{16,0},{24,8},{1,17},{9,25},{17,1},{25,9},{2,18},{10... | collective-permute-start | bytes 2359304 | tf_op jit(solution)/shard_map/ppermute | solution.py:645
  3.0 17.7 %collective-permute-done.11.refs_6_.refs_10_.refs_14_.refs_18_.grad = bf16[8,2,8,3072]{3,2,1,0:T(8,128)(2,1)S(1)} collective-permute-done((bf16[8,2,8,3072]{3,2,1,0:T(8,128)(2,1)}, bf16[8,2,8,3072]{3,2,1,0:T(8,128)(2,1)S(1)}, u32[]{:S(2)}, u32[]{:S(2)}) %collective-permute-start.11) | collective-permute-done | bytes 786464 | tf_op jit(solution)/shard_map/ppermute | solution.py:645
  20.7 2.8 %constant_dynamic-slice_fusion.1 = bf16[2,8,2,8,3072]{4,3,2,1,0:T(8,128)(2,1)} fusion(bf16[2,32,2,8,3072]{4,3,2,1,0:T(8,128)(2,1)} %pert.11, s32[]{:T(128)S(6)} %select_n.15), kind=kLoop, calls=%fused_computation.1 | loop fusion | bytes 3145732 | tf_op jit(solution)/shard_map/dynamic_slice | solution.py:662
  23.5 0.5 collective-permute-start.14
  24.0 1.8 %plan.3 = (s32[78]{0:T(128)S(1)}, s32[1]{0:T(128)}) custom-call(s32[32]{0:T(128)S(1)} %copy-done.21), custom_call_target="tpu_custom_call" | custom-call | bytes 312 | tf_op jit(solution)/shard_map/plan/pallas_call | solution.py:141
  25.8 0.0 copy-start.6
  25.9 2.3 %deep_product.3 = bf16[8,8,3072]{2,1,0:T(8,128)(2,1)S(1)} custom-call(s32[78]{0:T(128)S(1)} %get-tuple-element.59.plan, bf16[2,32,2,8,3072]{4,3,2,1,0:T(8,128)(2,1)} %pert.11, bf16[2,32,2,8,3072]{4,3,2,1,0:T(8,128)(2,1)} %pert.11, bf16[2,32,2,8,3072]{4,3,2,1,0:T(8,128)(2,1)} %pert.11, bf16[2,32,2,8,3072]{4,3,2,1,0:T(8,128)(2,1)} %pert.11, ...), custom_call_target="tpu_custom_call" | custom-call | flops 786432 | bytes 1572864 | tf_op jit(solution)/shard_map/deep_product/pallas_call | solution.py:379
  28.1 18.1 %all_to_all.20.planes = bf16[8,1,8,3072]{3,2,1,0:T(8,128)(2,1)S(1)} all-to-all(bf16[8,1,8,3072]{3,2,1,0:T(8,128)(2,1)S(1)} %bitcast.11), channel_id=1, replica_groups=mesh['mem'=4,'tile'=8] {'tile'}, dimensions={0} | all-to-all | bytes 786432 | tf_op jit(solution)/shard_map/all_to_all | solution.py:680
  46.2 6.6 %deep_smooth.3 = bf16[8,1,8,3072]{3,2,1,0:T(8,128)(2,1)} custom-call(s32[78]{0:T(128)S(1)} %get-tuple-element.59.plan, f32[4]{0:T(128)S(1)} %copy-done.20, bf16[8,1,8,3072]{3,2,1,0:T(8,128)(2,1)S(1)} %all_to_all.20.planes, s32[64,3072]{1,0:T(8,128)S(1)} %copy-done.6), custom_call_target="tpu_custom_call" | custom-call | flops 29491200 | bytes 1572864 | tf_op jit(solution)/shard_map/deep_smooth/pallas_call | solution.py:425
  52.8 3.5 %all-to-all-start.3 = ((bf16[8,1,8,3072]{3,2,1,0:T(8,128)(2,1)}), bf16[8,1,8,3072]{3,2,1,0:T(8,128)(2,1)S(1)}, u32[]{:S(2)}, u32[]{:S(2)}) async-start(bf16[8,1,8,3072]{3,2,1,0:T(8,128)(2,1)} %deep_smooth.3), calls=%async_computation.3 | async-start | bytes 786432 | tf_op jit(solution)/shard_map/all_to_all | solution.py:682
  56.3 4.6 %shard_map.66 = (bf16[80,3072]{1,0:T(8,128)(2,1)}, bf16[80,3072]{1,0:T(8,128)(2,1)}) custom-call(s32[78]{0:T(128)S(1)} %get-tuple-element.59.plan, bf16[2,32,2,8,3072]{4,3,2,1,0:T(8,128)(2,1)} %pert.11, bf16[8,2,8,3072]{3,2,1,0:T(8,128)(2,1)} %refs_16_.1, bf16[8,2,8,3072]{3,2,1,0:T(8,128)(2,1)S(1)} %collective-permute-done.8.far.refs_5_.refs_9_.refs_13_.refs_17_.grad), custom_call_target="tpu_custom_call" | custom-call | flops 3145728 | bytes 4718592 | tf_op jit(solution)/shard_map/pallas_call | solution.py:251
  60.9 4.6 %collective-permute-start.10 = (bf16[80,3072]{1,0:T(8,128)(2,1)}, bf16[80,3072]{1,0:T(8,128)(2,1)}, u32[]{:S(2)}, u32[]{:S(2)}) collective-permute-start(bf16[80,3072]{1,0:T(8,128)(2,1)} %get-tuple-element.61), channel_id=1, source_target_pairs={{0,1},{1,2},{2,3},{3,4},{4,5},{5,6},{6,7},{8,9},{9,10},{10,11},{11... | collective-permute-start | bytes 1474568 | tf_op jit(solution)/shard_map/ppermute | solution.py:673
  65.4 1.3 collective-permute-start.9
  66.8 3.0 %shard_map.69 = (bf16[88,3072]{1,0:T(8,128)(2,1)}, bf16[88,3072]{1,0:T(8,128)(2,1)}) custom-call(s32[78]{0:T(128)S(1)} %get-tuple-element.59.plan, bf16[2,32,2,8,3072]{4,3,2,1,0:T(8,128)(2,1)S(1)} %copy-done.4, bf16[2,8,2,8,3072]{4,3,2,1,0:T(8,128)(2,1)S(1)} %collective-permute-done.14.mate.rest_0_, ...), custom_call_target="tpu_custom_call" | custom-call | flops 6291456 | bytes 3932160 | tf_op jit(solution)/shard_map/pallas_call | solution.py:313
  69.8 1.3 collective-permute-start.15
  71.1 6.0 %collective-permute-start.16 = (bf16[88,3072]{1,0:T(8,128)(2,1)}, bf16[88,3072]{1,0:T(8,128)(2,1)}, u32[]{:S(2)}, u32[]{:S(2)}) collective-permute-start(bf16[88,3072]{1,0:T(8,128)(2,1)} %get-tuple-element.65), channel_id=1, source_target_pairs={{0,1},{1,2},{2,3},{3,4},{4,5},{5,6},{6,7},{8,9},{9,10},{10,11},{11... | collective-permute-start | bytes 1622024 | tf_op jit(solution)/shard_map/ppermute | solution.py:673
  77.1 1.9 %weights.3 = (f32[24,16,128]{2,1,0:T(8,128)S(1)}, f32[24,16,128]{2,1,0:T(8,128)S(1)}) custom-call(s32[78]{0:T(128)S(1)} %get-tuple-element.59.plan, f32[4]{0:T(128)S(1)} %copy-done.20, s32[64,3072]{1,0:T(8,128)} %class_map.1, s32[64,3072]{1,0:T(8,128)} %class_map.1, s32[64,3072]{1,0:T(8,128)} %class_map.1), custom_call_target="tpu_custom_call" | custom-call | bytes 393216 | tf_op jit(solution)/shard_map/weights/pallas_call | solution.py:175
  79.0 19.7 %collective-permute-done.10.above = bf16[80,3072]{1,0:T(8,128)(2,1)} collective-permute-done((bf16[80,3072]{1,0:T(8,128)(2,1)}, bf16[80,3072]{1,0:T(8,128)(2,1)}, u32[]{:S(2)}, u32[]{:S(2)}) %collective-permute-start.10) | collective-permute-done | bytes 491552 | tf_op jit(solution)/shard_map/ppermute | solution.py:673
  98.7 7.0 %shard_map.68 = bf16[8,2,8,3072]{3,2,1,0:T(8,128)(2,1)S(1)} custom-call(s32[78]{0:T(128)S(1)} %get-tuple-element.59.plan, bf16[2,32,2,8,3072]{4,3,2,1,0:T(8,128)(2,1)} %pert.11, bf16[8,2,8,3072]{3,2,1,0:T(8,128)(2,1)S(1)} %collective-permute-done.8.far.refs_5_.refs_9_.refs_13_.refs_17_.grad, bf16[80,3072]{1,0:T(8,128)(2,1)} %collective-permute-done.9.below, ...), custom_call_target="tpu_custom_call" | custom-call | flops 39321600 | bytes 3932160 | tf_op jit(solution)/shard_map/pallas_call | solution.py:548
  105.7 0.1 collective-permute-start.13
  105.8 2.3 %collective-permute-done.16.above = bf16[88,3072]{1,0:T(8,128)(2,1)} collective-permute-done((bf16[88,3072]{1,0:T(8,128)(2,1)}, bf16[88,3072]{1,0:T(8,128)(2,1)}, u32[]{:S(2)}, u32[]{:S(2)}) %collective-permute-start.16) | collective-permute-done | bytes 540704 | tf_op jit(solution)/shard_map/ppermute | solution.py:673
  108.1 6.1 %shard_map.71 = bf16[4,2,8,3072]{3,2,1,0:T(8,128)(2,1)S(1)} custom-call(s32[78]{0:T(128)S(1)} %get-tuple-element.59.plan, bf16[2,32,2,8,3072]{4,3,2,1,0:T(8,128)(2,1)S(1)} %bitcast.13, bf16[8,2,8,3072]{3,2,1,0:T(8,128)(2,1)S(1)} %collective-permute-done.11.refs_6_.refs_10_.refs_14_.refs_18_.grad, bf16[88,3072]{1,0:T(8,128)(2,1)} %collective-permute-done.15.below, ...), custom_call_target="tpu_custom_call" | custom-call | flops 39321600 | bytes 3932160 | tf_op jit(solution)/shard_map/pallas_call | solution.py:548
  114.2 0.1 collective-permute-start.19
  114.3 5.6 %shard_map.70 = bf16[4,2,8,3072]{3,2,1,0:T(8,128)(2,1)S(1)} custom-call(s32[78]{0:T(128)S(1)} %get-tuple-element.59.plan, bf16[2,32,2,8,3072]{4,3,2,1,0:T(8,128)(2,1)S(1)} %bitcast.13, bf16[8,2,8,3072]{3,2,1,0:T(8,128)(2,1)S(1)} %collective-permute-done.11.refs_6_.refs_10_.refs_14_.refs_18_.grad, bf16[88,3072]{1,0:T(8,128)(2,1)} %collective-permute-done.15.below, ...), custom_call_target="tpu_custom_call" | custom-call | flops 39321600 | bytes 3932160 | tf_op jit(solution)/shard_map/pallas_call | solution.py:548
  119.9 0.7 collective-permute-start.18
  121.2 5.2 %shard_map.67 = f32[8,2,8,3072]{3,2,1,0:T(8,128)} custom-call(s32[78]{0:T(128)S(1)} %get-tuple-element.59.plan, bf16[2,32,2,8,3072]{4,3,2,1,0:T(8,128)(2,1)S(1)} %bitcast.13, bf16[8,2,8,3072]{3,2,1,0:T(8,128)(2,1)S(1)} %copy-done.11, bf16[80,3072]{1,0:T(8,128)(2,1)} %collective-permute-done.9.below, bf16[80,3072]{1,0:T(8,128)(2,1)} %collective-permute-done.10.above, ...), custom_call_target="tpu_custom_call" | custom-call | flops 39321600 | bytes 3932160 | tf_op jit(solution)/shard_map/pallas_call | solution.py:548
  126.4 5.5 %collective-permute-done.18 = bf16[4,2,8,3072]{3,2,1,0:T(8,128)(2,1)S(1)} collective-permute-done((bf16[4,2,8,3072]{3,2,1,0:T(8,128)(2,1)S(1)}, bf16[4,2,8,3072]{3,2,1,0:T(8,128)(2,1)S(1)}, u32[]{:S(2)}, u32[]{:S(2)}) %collective-permute-start.18) | collective-permute-done | bytes 393248 | tf_op jit(solution)/shard_map/ppermute | solution.py:645
  132.0 3.7 %conditional.1 = (f32[8,2,8,3072]{3,2,1,0:T(8,128)S(1)}) conditional(s32[]{:T(128)} %bitcast.2, (s32[32]{0:T(128)S(1)}, f32[4]{0:T(128)S(1)}, s32[64,3072]{1,0:T(8,128)S(1)}, bf16[2,32,2,8,3072]{4,3,2,1,0:T(8,128)(2,1)S(1)}, bf16[8,2,8,3072]{3,2,1,0:T(8,128)(2,1)S(1)}, /*index=5*/f32[8,2,8,3072]{3,2,1,0:T(8,128)S(1)}) %tuple.25, (s32[78]{0:T(128)S(1)}, ...), branch_computations={%region_0.1_spmd, %region_1.2_spmd} | conditional | flops 401080320 | bytes 172721696 | solution.py:724
  132.0 0.9 copy-done.18
  132.9 0.1 copy-done.19
  133.0 2.7 %final_sum.3 = f32[8,2,8,3072]{3,2,1,0:T(8,128)S(1)} custom-call(s32[78]{0:T(128)S(1)} %get-tuple-element.43.plan, bf16[2,32,2,8,3072]{4,3,2,1,0:T(8,128)(2,1)S(1)} %get-tuple-element.44.pert, f32[8,2,8,3072]{3,2,1,0:T(8,128)} %get-tuple-element.45.near, bf16[8,2,8,3072]{3,2,1,0:T(8,128)(2,1)} %copy-done.18, bf16[8,8,3072]{2,1,0:T(8,128)(2,1)S(1)} %get-tuple-element.47.deep, ...), custom_call_target="tpu_custom_call" | custom-call | flops 1572864 | bytes 4718592 | tf_op jit(solution)/shard_map/cond/branch_1_fun/final_sum/pallas_call | solution.py:617
  135.7 1.1 copy-done.17
  (35 shorter events, 0.1 us)
Async XLA Ops:
  0.0 20.7 %collective-permute-start.11 = (bf16[8,2,8,3072]{3,2,1,0:T(8,128)(2,1)}, bf16[8,2,8,3072]{3,2,1,0:T(8,128)(2,1)S(1)}, u32[]{:S(2)}, u32[]{:S(2)}) collective-permute-start(bf16[8,2,8,3072]{3,2,1,0:T(8,128)(2,1)} %refs_16_.1), channel_id=1, source_target_pairs={{0,16},{8,24},{16,0},{24,8},{1,17},{9,25},{17,1},{25,9},{2,18},{10... | collective-permute-start | bytes 2359304 | tf_op jit(solution)/shard_map/ppermute | solution.py:645
  3.0 22.8 %collective-permute-start.8 = (bf16[8,2,8,3072]{3,2,1,0:T(8,128)(2,1)}, bf16[8,2,8,3072]{3,2,1,0:T(8,128)(2,1)S(1)}, u32[]{:S(2)}, u32[]{:S(2)}) collective-permute-start(bf16[8,2,8,3072]{3,2,1,0:T(8,128)(2,1)} %refs_16_.1), channel_id=1, source_target_pairs={{0,8},{8,0},{16,24},{24,16},{1,9},{9,1},{17,25},{25,17},{2,10},{10... | collective-permute-start | bytes 2359304 | tf_op jit(solution)/shard_map/ppermute | solution.py:648
  20.7 5.1 %collective-permute-start.12 = (bf16[8,2,8,3072]{3,2,1,0:T(8,128)(2,1)S(1)}, bf16[8,2,8,3072]{3,2,1,0:T(8,128)(2,1)}, u32[]{:S(2)}, u32[]{:S(2)}) collective-permute-start(bf16[8,2,8,3072]{3,2,1,0:T(8,128)(2,1)S(1)} %collective-permute-done.11.refs_6_.refs_10_.refs_14_.refs_18_.grad), channel_id=1, source_target_pairs={{0,8},{8,0},{16,24},{24,16},{1,9},{9,1},{17,25},{25,17},{2,10},{10... | collective-permute-start | bytes 2359304 | tf_op jit(solution)/shard_map/ppermute | solution.py:648
  20.7 3.3 %copy-start.21 = (s32[32]{0:T(128)S(1)}, s32[32]{0:T(128)}, u32[]{:S(2)}) copy-start(s32[32]{0:T(128)} %level_steps.1) | copy-start | bytes 388
  20.7 5.1 %copy-start.10 = (bf16[8,2,8,3072]{3,2,1,0:T(8,128)(2,1)S(1)}, bf16[8,2,8,3072]{3,2,1,0:T(8,128)(2,1)}, u32[]{:S(2)}) copy-start(bf16[8,2,8,3072]{3,2,1,0:T(8,128)(2,1)} %refs_16_.1) | copy-start | bytes 2359300
  23.5 43.2 %collective-permute-start.14 = (bf16[2,8,2,8,3072]{4,3,2,1,0:T(8,128)(2,1)}, bf16[2,8,2,8,3072]{4,3,2,1,0:T(8,128)(2,1)S(1)}, u32[]{:S(2)}, u32[]{:S(2)}) collective-permute-start(bf16[2,8,2,8,3072]{4,3,2,1,0:T(8,128)(2,1)} %constant_dynamic-slice_fusion.1), channel_id=1, source_target_pairs={{0,8},{8,0},{16,24},{24,16},{1,9},{9,1},{17,25},{25,17},{2,10},{10... | collective-permute-start | bytes 4718600 | tf_op jit(solution)/shard_map/ppermute | solution.py:648
  25.8 20.4 %copy-start.6 = (s32[64,3072]{1,0:T(8,128)S(1)}, s32[64,3072]{1,0:T(8,128)}, u32[]{:S(2)}) copy-start(s32[64,3072]{1,0:T(8,128)} %class_map.1) | copy-start | bytes 2359300
  25.9 20.4 %copy-start.20 = (f32[4]{0:T(128)S(1)}, f32[4]{0:T(128)}, u32[]{:S(2)}) copy-start(f32[4]{0:T(128)} %values.3) | copy-start | bytes 52
  52.8 24.2 %all-to-all-start.3 = ((bf16[8,1,8,3072]{3,2,1,0:T(8,128)(2,1)}), bf16[8,1,8,3072]{3,2,1,0:T(8,128)(2,1)S(1)}, u32[]{:S(2)}, u32[]{:S(2)}) async-start(bf16[8,1,8,3072]{3,2,1,0:T(8,128)(2,1)} %deep_smooth.3), calls=%async_computation.3 | async-start | bytes 786432 | tf_op jit(solution)/shard_map/all_to_all | solution.py:682
  56.3 10.5 %copy-start.4 = (bf16[2,32,2,8,3072]{4,3,2,1,0:T(8,128)(2,1)S(1)}, bf16[2,32,2,8,3072]{4,3,2,1,0:T(8,128)(2,1)}, u32[]{:S(2)}) copy-start(bf16[2,32,2,8,3072]{4,3,2,1,0:T(8,128)(2,1)} %pert.11) | copy-start | bytes 18874372
  60.9 37.8 %collective-permute-start.10 = (bf16[80,3072]{1,0:T(8,128)(2,1)}, bf16[80,3072]{1,0:T(8,128)(2,1)}, u32[]{:S(2)}, u32[]{:S(2)}) collective-permute-start(bf16[80,3072]{1,0:T(8,128)(2,1)} %get-tuple-element.61), channel_id=1, source_target_pairs={{0,1},{1,2},{2,3},{3,4},{4,5},{5,6},{6,7},{8,9},{9,10},{10,11},{11... | collective-permute-start | bytes 1474568 | tf_op jit(solution)/shard_map/ppermute | solution.py:673
  65.4 33.3 %collective-permute-start.9 = (bf16[80,3072]{1,0:T(8,128)(2,1)}, bf16[80,3072]{1,0:T(8,128)(2,1)}, u32[]{:S(2)}, u32[]{:S(2)}) collective-permute-start(bf16[80,3072]{1,0:T(8,128)(2,1)} %get-tuple-element.60), channel_id=1, source_target_pairs={{1,0},{2,1},{3,2},{4,3},{5,4},{6,5},{7,6},{9,8},{10,9},{11,10},{12... | collective-permute-start | bytes 1474568 | tf_op jit(solution)/shard_map/ppermute | solution.py:672
  69.8 36.1 %collective-permute-start.15 = (bf16[88,3072]{1,0:T(8,128)(2,1)}, bf16[88,3072]{1,0:T(8,128)(2,1)}, u32[]{:S(2)}, u32[]{:S(2)}) collective-permute-start(bf16[88,3072]{1,0:T(8,128)(2,1)} %get-tuple-element.64), channel_id=1, source_target_pairs={{1,0},{2,1},{3,2},{4,3},{5,4},{6,5},{7,6},{9,8},{10,9},{11,10},{12... | collective-permute-start | bytes 1622024 | tf_op jit(solution)/shard_map/ppermute | solution.py:672
  71.1 37.0 %collective-permute-start.16 = (bf16[88,3072]{1,0:T(8,128)(2,1)}, bf16[88,3072]{1,0:T(8,128)(2,1)}, u32[]{:S(2)}, u32[]{:S(2)}) collective-permute-start(bf16[88,3072]{1,0:T(8,128)(2,1)} %get-tuple-element.65), channel_id=1, source_target_pairs={{0,1},{1,2},{2,3},{3,4},{4,5},{5,6},{6,7},{8,9},{9,10},{10,11},{11... | collective-permute-start | bytes 1622024 | tf_op jit(solution)/shard_map/ppermute | solution.py:673
  77.1 31.0 %collective-permute-start.17 = (bf16[8,8,3072]{2,1,0:T(8,128)(2,1)S(1)}, bf16[8,8,3072]{2,1,0:T(8,128)(2,1)S(1)}, u32[]{:S(2)}, u32[]{:S(2)}) collective-permute-start(bf16[8,8,3072]{2,1,0:T(8,128)(2,1)S(1)} %bitcast.16), channel_id=1, source_target_pairs={{0,8},{8,0},{16,24},{24,16},{1,9},{9,1},{17,25},{25,17},{2,10},{10... | collective-permute-start | bytes 1179656 | tf_op jit(solution)/shard_map/ppermute | solution.py:648
  77.1 31.0 %slice-start = ((s8[6291456]{0:T(1024)(128)(4,1)}), s8[4194304]{0:T(1024)(128)(4,1)S(1)}, s32[]{:S(2)}) async-start(s8[6291456]{0:T(1024)(128)(4,1)} %bitcast.12), calls=%async_computation.4 | async-start | bytes 8388608
  98.7 9.4 %slice-start.1 = ((s8[6291456]{0:T(1024)(128)(4,1)}), s8[2097152]{0:T(1024)(128)(4,1)S(1)}, s32[]{:S(2)}) async-start(s8[6291456]{0:T(1024)(128)(4,1)} %bitcast.12), calls=%async_computation.5 | async-start | bytes 4194304
  105.7 20.7 %collective-permute-start.13 = (bf16[8,2,8,3072]{3,2,1,0:T(8,128)(2,1)S(1)}, bf16[8,2,8,3072]{3,2,1,0:T(8,128)(2,1)S(1)}, u32[]{:S(2)}, u32[]{:S(2)}) collective-permute-start(bf16[8,2,8,3072]{3,2,1,0:T(8,128)(2,1)S(1)} %shard_map.68), channel_id=1, source_target_pairs={{0,8},{8,0},{16,24},{24,16},{1,9},{9,1},{17,25},{25,17},{2,10},{10... | collective-permute-start | bytes 2359304 | tf_op jit(solution)/shard_map/ppermute | solution.py:648
  114.2 7.0 %copy-start.11 = (bf16[8,2,8,3072]{3,2,1,0:T(8,128)(2,1)S(1)}, bf16[8,2,8,3072]{3,2,1,0:T(8,128)(2,1)}, u32[]{:S(2)}) copy-start(bf16[8,2,8,3072]{3,2,1,0:T(8,128)(2,1)} %refs_16_.1) | copy-start | bytes 2359300
  114.2 7.0 %copy-start.14 = (f32[8,2,8,3072]{3,2,1,0:T(8,128)S(1)}, f32[8,2,8,3072]{3,2,1,0:T(8,128)}, u32[]{:S(2)}) copy-start(f32[8,2,8,3072]{3,2,1,0:T(8,128)} %rest_0_.1) | copy-start | bytes 4718596
  114.2 12.2 %collective-permute-start.19 = (bf16[4,2,8,3072]{3,2,1,0:T(8,128)(2,1)S(1)}, bf16[4,2,8,3072]{3,2,1,0:T(8,128)(2,1)S(1)}, u32[]{:S(2)}, u32[]{:S(2)}) collective-permute-start(bf16[4,2,8,3072]{3,2,1,0:T(8,128)(2,1)S(1)} %shard_map.71), channel_id=1, source_target_pairs={{0,16},{8,24},{16,0},{24,8},{1,17},{9,25},{17,1},{25,9},{2,18},{10... | collective-permute-start | bytes 1179656 | tf_op jit(solution)/shard_map/ppermute | solution.py:645
  119.9 12.1 %collective-permute-start.18 = (bf16[4,2,8,3072]{3,2,1,0:T(8,128)(2,1)S(1)}, bf16[4,2,8,3072]{3,2,1,0:T(8,128)(2,1)S(1)}, u32[]{:S(2)}, u32[]{:S(2)}) collective-permute-start(bf16[4,2,8,3072]{3,2,1,0:T(8,128)(2,1)S(1)} %shard_map.70), channel_id=1, source_target_pairs={{0,16},{8,24},{16,0},{24,8},{1,17},{9,25},{17,1},{25,9},{2,18},{10... | collective-permute-start | bytes 1179656 | tf_op jit(solution)/shard_map/ppermute | solution.py:645
  121.2 10.7 %copy-start.7 = (s32[64,3072]{1,0:T(8,128)S(1)}, s32[64,3072]{1,0:T(8,128)}, u32[]{:S(2)}) copy-start(s32[64,3072]{1,0:T(8,128)} %class_map.1) | copy-start | bytes 2359300
  132.0 0.9 copy-start.18
  132.0 1.0 copy-start.19
  135.7 1.1 copy-start.17
